TPU v7x, 512 devices: a whole 4x4x16 slice. The times are simulated.
512 devices in a mesh: gz: 32 (over z, core), gy: 16 (over y, x).
Axes of the slice: x: 4, y: 4, z: 16, core: 2. Of those that a mesh axis runs over, the one named last changes fastest.
Arguments:
- excess_warmth: float32 [512, 128, 128], P('gz', 'gy'), may hold values from -0.2 to 0.3
- conversion_degree: float32 [512, 128, 128], P('gz', 'gy'), may hold values from 0 to 0.9
- substance_label: int32 [512, 128, 128], P('gz', 'gy'), may hold values from 0 to 2
Outputs:
- temperature_out: float32 [512, 128, 128], P('gz', 'gy')
- cure_out: float32 [512, 128, 128], P('gz', 'gy')
Inputs may be any that keep to these rules, and one draw needn't show every extreme that they name: `substance_label`: material holds 0 for propellant, 1 for mandrel, 2 for case.
All inputs are finite; a program needn't handle non-finite values.
Results may differ from a plain program's by a relative error of at most 0.0003.
Values sent between devices are 32-bit elements; how exact they have to be, the bound alone decides.
No kernel may reach another device: no remote copies, remote signals or barrier semaphores. Data moves between devices by JAX's collectives and lax.ppermute only.
A program may use at most 64 MiB of HBM per device.

v0:
```python
import functools

import jax
import jax.numpy as jnp
from jax import lax
from jax.experimental import pallas as pl
from jax.experimental.pallas import tpu as pltpu
from jax.sharding import PartitionSpec as P

ZC = 16
YC = 8
XC = 128
ROWS = ZC * YC

VM = pl.BlockSpec(memory_space=pltpu.VMEM)
SM = pl.BlockSpec(memory_space=pltpu.SMEM)


def f32(*shape):
    return jax.ShapeDtypeStruct(shape, jnp.float32)


def conduct_of(label, cure):
    return jnp.where(label == 1, 40.0, jnp.where(label == 2, 20.0, 0.6 + 0.8 * cure))


def store_of(label):
    return jnp.where(label == 1, 3.0 / 60.0, jnp.where(label == 2, 2.0 / 60.0, 1.0 / 60.0))


def cure_of(label, warmth, cure):
    speed = 0.3 * jnp.exp(8.0 * warmth)
    return jnp.where(label == 0, 1.0 - (1.0 - cure) * jnp.exp(-speed), cure)


def y_rows(y):
    return pl.ds(y, ZC, stride=YC)


def z_rows(z):
    return pl.ds(z * YC, YC)


def edges_kernel(t_ref, c_ref, m_ref, zlo_ref, zhi_ref, ylo_ref, yhi_ref):
    def put(out, rows):
        t, c, m = t_ref[rows, :], c_ref[rows, :], m_ref[rows, :]
        out[0] = t
        out[1] = conduct_of(m, c)
        out[2] = conduct_of(m, cure_of(m, t, c))

    put(zlo_ref, z_rows(0))
    put(zhi_ref, z_rows(ZC - 1))
    put(ylo_ref, y_rows(0))
    put(yhi_ref, y_rows(YC - 1))


def eliminate(count, store, faces, right, entry, keep):
    ground, edge, side = store(0), entry, right(0)
    back_ground = back_side = None
    for i in range(count - 1):
        face = faces(i)
        inv = 1.0 / (ground + edge + face)
        edge_inv, face_inv, side_inv = edge * inv, face * inv, side * inv
        keep(i, side_inv, edge_inv, face_inv)
        more_ground, more_side = edge_inv * ground, edge_inv * side
        back_ground = more_ground if i == 0 else back_ground + more_ground
        back_side = more_side if i == 0 else back_side + more_side
        ground = store(i + 1) + face_inv * ground
        side = right(i + 1) + face_inv * side
        edge = edge_inv * face
    return back_ground, edge, ground, side, back_side


def front_kernel(
    place_ref,
    t_ref,
    c_ref,
    m_ref,
    ztlo_ref,
    zthi_ref,
    ytlo_ref,
    ythi_ref,
    zklo_ref,
    zkhi_ref,
    yklo_ref,
    ykhi_ref,
    pay_ref,
    sub_ref,
    fluxz_ref,
    cure_ref,
    k_ref,
    g_ref,
    fy_ref,
    r_ref,
    *,
    groups,
):
    t, c, m = t_ref[...], c_ref[...], m_ref[...]
    k_ref[...] = conduct_of(m, c)
    g_ref[...] = store_of(m)
    cure_ref[...] = cure_of(m, t, c)

    ks = [yklo_ref[...]] + [k_ref[y_rows(y), :] for y in range(YC)] + [ykhi_ref[...]]
    ts = [ytlo_ref[...]] + [t_ref[y_rows(y), :] for y in range(YC)] + [ythi_ref[...]]
    face_y = [0.5 * (ks[i] + ks[i + 1]) for i in range(YC + 1)]
    flow_y = [face_y[i] * (ts[i + 1] - ts[i]) for i in range(YC + 1)]
    for y in range(YC):
        fy_ref[y_rows(y), :] = flow_y[y + 1] - flow_y[y]

    lane = lax.broadcasted_iota(jnp.int32, (YC, XC), 1)
    first_lane, last_lane = lane == 0, lane == XC - 1
    k_prev, t_prev = zklo_ref[...], ztlo_ref[...]
    flow_prev = 0.5 * (k_prev + k_ref[z_rows(0), :]) * (t_ref[z_rows(0), :] - t_prev)
    batch = 4
    for z0 in range(0, ZC, batch):
        gs, ls, rs, sides, stores = [], [], [], [], []
        for z in range(z0, z0 + batch):
            kz, tz, g = k_ref[z_rows(z), :], t_ref[z_rows(z), :], g_ref[z_rows(z), :]
            k_next = k_ref[z_rows(z + 1), :] if z + 1 < ZC else zkhi_ref[...]
            t_next = t_ref[z_rows(z + 1), :] if z + 1 < ZC else zthi_ref[...]
            flow_next = 0.5 * (kz + k_next) * (t_next - tz)
            flux_z = flow_next - flow_prev
            flow_prev = flow_next
            fluxz_ref[z_rows(z), :] = flux_z
            k_left = jnp.where(first_lane, 0.0, pltpu.roll(kz, 1, 1))
            t_left = jnp.where(first_lane, 0.0, pltpu.roll(tz, 1, 1))
            face_left = 0.5 * (kz + k_left)
            flow_left = face_left * (tz - t_left)
            face_right = jnp.where(last_lane, 0.5 * kz, pltpu.roll(face_left, XC - 1, 1))
            flow_right = jnp.where(last_lane, -face_right * tz, pltpu.roll(flow_left, XC - 1, 1))
            delta = cure_ref[z_rows(z), :] - c_ref[z_rows(z), :]
            sides.append(
                g * (tz + 0.4 * delta)
                + (flow_right - flow_left)
                + 2.0 * (fy_ref[z_rows(z), :] + flux_z)
            )
            gs.append(
                g
                + jnp.where(first_lane, face_left, 0.0)
                + jnp.where(last_lane, face_right, 0.0)
            )
            ls.append(jnp.where(first_lane, 0.0, face_left))
            rs.append(jnp.where(last_lane, 0.0, face_right))
            stores.append(g)
        stride = 1
        while stride < XC:
            for b in range(batch):
                ground, left, right, side = gs[b], ls[b], rs[b], sides[b]
                inv = 1.0 / (ground + left + right)
                ground_inv, side_inv = ground * inv, side * inv
                gs[b] = (
                    ground
                    + left * pltpu.roll(ground_inv, stride, 1)
                    + right * pltpu.roll(ground_inv, XC - stride, 1)
                )
                sides[b] = (
                    side
                    + left * pltpu.roll(side_inv, stride, 1)
                    + right * pltpu.roll(side_inv, XC - stride, 1)
                )
                ls[b] = left * pltpu.roll(left * inv, stride, 1)
                rs[b] = right * pltpu.roll(right * inv, XC - stride, 1)
            stride *= 2
        for b in range(batch):
            rows = z_rows(z0 + b)
            r_ref[rows, :] = stores[b] * (sides[b] / gs[b]) - fy_ref[rows, :]

    def keep(i, side_inv, edge_inv, face_inv):
        sub_ref[0, i] = side_inv
        sub_ref[1, i] = edge_inv
        sub_ref[2, i] = face_inv

    back_ground, edge, ground, side, back_side = eliminate(
        YC,
        lambda i: g_ref[y_rows(i), :],
        lambda i: face_y[i + 1],
        lambda i: r_ref[y_rows(i), :],
        face_y[0],
        keep,
    )
    ground = ground + jnp.where(place_ref[0] == groups - 1, face_y[YC], 0.0)
    for d in range(groups):
        pay_ref[d, 0:16] = back_ground
        pay_ref[d, 16:32] = edge
        pay_ref[d, 32:48] = ground
        pay_ref[d, 48:64] = side
        pay_ref[d, 64:80] = back_side


def chain(count, read, put):
    def ground_of(j):
        return read(j, 2) + read(j + 1, 0) if j + 1 < count else read(j, 2)

    def side_of(j):
        return read(j, 3) + read(j + 1, 4) if j + 1 < count else read(j, 3)

    half = count // 2
    gain, part = [None] * count, [None] * count
    ground_l, side_l = ground_of(0) + read(0, 1), side_of(0)
    ground_r, side_r = ground_of(count - 1), side_of(count - 1)
    for i in range(half - 1):
        edge = read(i + 1, 1)
        inv = 1.0 / (ground_l + edge)
        gain[i], part[i] = edge * inv, side_l * inv
        ground_l = ground_of(i + 1) + gain[i] * ground_l
        side_l = side_of(i + 1) + gain[i] * side_l
        j = count - 1 - i
        edge = read(j, 1)
        inv = 1.0 / (ground_r + edge)
        gain[j], part[j] = edge * inv, side_r * inv
        ground_r = ground_of(j - 1) + gain[j] * ground_r
        side_r = side_of(j - 1) + gain[j] * side_r
    edge = read(half, 1)
    inv = 1.0 / (ground_l * ground_r + edge * (ground_l + ground_r))
    low = (side_l * (ground_r + edge) + edge * side_r) * inv
    high = (side_r * (ground_l + edge) + edge * side_l) * inv
    put(half - 1, low)
    put(half, high)
    for i in range(half - 2, -1, -1):
        low = part[i] + gain[i] * low
        put(i, low)
        j = count - 1 - i
        high = part[j] + gain[j] * high
        put(j, high)


def middle_kernel(
    place_ref,
    all_ref,
    sub_ref,
    fluxz_ref,
    c_ref,
    m_ref,
    zklo_ref,
    zkhi_ref,
    pay_ref,
    subz_ref,
    entry_ref,
    s_ref,
    v_ref,
    *,
    groups_y,
    groups_z,
    copies,
):
    zero = jnp.zeros((ZC, XC), jnp.float32)
    s_ref[0] = zero

    def put(j, value):
        s_ref[j + 1] = value

    chain(groups_y, lambda j, q: all_ref[j, 16 * q : 16 * q + 16, :], put)
    me = place_ref[0]
    before, value = s_ref[me], s_ref[me + 1]
    v_ref[y_rows(YC - 1), :] = value
    for i in range(YC - 2, -1, -1):
        value = (sub_ref[0, i] + sub_ref[1, i] * before) + sub_ref[2, i] * value
        v_ref[y_rows(i), :] = value

    ks = [zklo_ref[...]]
    for z in range(ZC):
        ks.append(conduct_of(m_ref[z_rows(z), :], c_ref[z_rows(z), :]))
    ks.append(zkhi_ref[...])
    faces = [0.5 * (ks[i] + ks[i + 1]) for i in range(ZC + 1)]
    entry_ref[...] = faces[ZC]

    def keep(i, side_inv, edge_inv, face_inv):
        subz_ref[0, i] = side_inv
        subz_ref[1, i] = edge_inv
        subz_ref[2, i] = face_inv

    def right(i):
        return store_of(m_ref[z_rows(i), :]) * v_ref[z_rows(i), :] - fluxz_ref[z_rows(i), :]

    back_ground, edge, ground, side, back_side = eliminate(
        ZC,
        lambda i: store_of(m_ref[z_rows(i), :]),
        lambda i: faces[i + 1],
        right,
        faces[0],
        keep,
    )
    ground = ground + jnp.where(place_ref[1] == groups_z - 1, faces[ZC], 0.0)
    for d in range(copies):
        pay_ref[d, 0:8] = back_ground
        pay_ref[d, 8:16] = edge
        pay_ref[d, 16:24] = ground
        pay_ref[d, 24:32] = side
        pay_ref[d, 32:40] = back_side


def back_kernel(
    place_ref,
    all_ref,
    subz_ref,
    entry_ref,
    t_ref,
    ylo_ref,
    yhi_ref,
    zlo_ref,
    zhi_ref,
    s_ref,
    *,
    groups_z,
    more,
):
    s_ref[0] = jnp.zeros((YC, XC), jnp.float32)

    def put(j, value):
        s_ref[j + 1] = value

    chain(groups_z, lambda j, q: all_ref[j % 2, j // 2, 8 * q : 8 * q + 8, :], put)
    me = place_ref[1]
    before, own = s_ref[me], s_ref[me + 1]
    value = own
    t_ref[z_rows(ZC - 1), :] = value
    for i in range(ZC - 2, -1, -1):
        value = (subz_ref[0, i] + subz_ref[1, i] * before) + subz_ref[2, i] * value
        t_ref[z_rows(i), :] = value
    if more:
        ylo_ref[...] = t_ref[y_rows(0), :]
        yhi_ref[...] = t_ref[y_rows(YC - 1), :]
        zlo_ref[...] = before
        then = jnp.minimum(me + 1, groups_z - 1)
        core, chip = lax.rem(then, 2), lax.div(then, 2)
        after = s_ref[then + 1]
        back_ground = all_ref[core, chip, 0:8, :]
        edge = all_ref[core, chip, 8:16, :]
        back_side = all_ref[core, chip, 32:40, :]
        drop = (back_ground * own + edge * (own - after) - back_side) / entry_ref[...]
        zhi_ref[...] = jnp.where(me == groups_z - 1, 0.0, own - drop)


def body(warmth, cure, label):
    groups_z, groups_y = lax.axis_size("gz"), lax.axis_size("gy")
    chips = groups_z // 2
    place = jnp.stack([lax.axis_index("gy"), lax.axis_index("gz")]).astype(jnp.int32)
    up = {a: [(i, i + 1) for i in range(n - 1)] for a, n in (("gz", groups_z), ("gy", groups_y))}
    down = {a: [(j, i) for i, j in up[a]] for a in up}
    pairs = [[2 * i, 2 * i + 1] for i in range(chips)]
    same_core = [[2 * i + core for i in range(chips)] for core in range(2)]

    t = warmth.reshape(ROWS, XC)
    c = cure.reshape(ROWS, XC)
    m = label.reshape(ROWS, XC)

    zlo, zhi, ylo, yhi = pl.pallas_call(
        edges_kernel,
        out_shape=(f32(3, YC, XC), f32(3, YC, XC), f32(3, ZC, XC), f32(3, ZC, XC)),
        in_specs=[VM] * 3,
        out_specs=(VM,) * 4,
        name="edges",
    )(t, c, m)
    from_below = lax.ppermute(zhi, "gz", up["gz"])
    from_above = lax.ppermute(zlo, "gz", down["gz"])
    from_south = lax.ppermute(yhi, "gy", up["gy"])
    from_north = lax.ppermute(ylo, "gy", down["gy"])
    zt = (from_below[0], from_above[0])
    yt = (from_south[0], from_north[0])

    for step in range(2):
        zk = (from_below[1 + step], from_above[1 + step])
        yk = (from_south[1 + step], from_north[1 + step])
        pay, sub, fluxz, next_c = pl.pallas_call(
            functools.partial(front_kernel, groups=groups_y),
            out_shape=(
                f32(groups_y, 5 * ZC, XC),
                f32(3, YC - 1, ZC, XC),
                f32(ROWS, XC),
                f32(ROWS, XC),
            ),
            in_specs=[SM] + [VM] * 11,
            out_specs=(VM,) * 4,
            scratch_shapes=[pltpu.VMEM((ROWS, XC), jnp.float32)] * 4,
            name="front",
        )(place, t, c, m, *zt, *yt, *zk, *yk)
        everyone = lax.all_to_all(pay, "gy", 0, 0, tiled=True)
        payz, subz, entry = pl.pallas_call(
            functools.partial(
                middle_kernel, groups_y=groups_y, groups_z=groups_z, copies=chips
            ),
            out_shape=(f32(chips, 5 * YC, XC), f32(3, ZC - 1, YC, XC), f32(YC, XC)),
            in_specs=[SM] + [VM] * 7,
            out_specs=(VM,) * 3,
            scratch_shapes=[
                pltpu.VMEM((groups_y + 1, ZC, XC), jnp.float32),
                pltpu.VMEM((ROWS, XC), jnp.float32),
            ],
            name="middle",
        )(place, everyone, sub, fluxz, c, m, *zk)
        column = lax.all_to_all(payz, "gz", 0, 0, tiled=True, axis_index_groups=same_core)
        column = lax.all_gather(column, "gz", axis_index_groups=pairs)
        t, ylo, yhi, zlo, zhi = pl.pallas_call(
            functools.partial(back_kernel, groups_z=groups_z, more=step == 0),
            out_shape=(f32(ROWS, XC), f32(ZC, XC), f32(ZC, XC), f32(YC, XC), f32(YC, XC)),
            in_specs=[SM] + [VM] * 3,
            out_specs=(VM,) * 5,
            scratch_shapes=[pltpu.VMEM((groups_z + 1, YC, XC), jnp.float32)],
            name="back",
        )(place, column, subz, entry)
        c = next_c
        if step == 0:
            zt = (zlo, zhi)
            yt = (lax.ppermute(yhi, "gy", up["gy"]), lax.ppermute(ylo, "gy", down["gy"]))
    return t.reshape(warmth.shape), c.reshape(cure.shape)


def solution(mesh):
    return jax.shard_map(
        body,
        mesh=mesh,
        in_specs=(P("gz", "gy", None),) * 3,
        out_specs=(P("gz", "gy", None),) * 2,
        check_vma=False,
    )
```

profile of v0, /device:TPU:1, one launch (start us, length us, event | category | flops | bytes accessed | tf_op | source)
XLA Modules:
  0.0 145.7 jit_solution(15896960439127011593)
XLA Ops:
  0.6 1.6 %edges.1 = (f32[3,8,128]{2,1,0:T(8,128)}, f32[3,8,128]{2,1,0:T(8,128)}, f32[3,16,128]{2,1,0:T(8,128)}, f32[3,16,128]{2,1,0:T(8,128)}) custom-call(f32[128,128]{1,0:T(8,128)} %bitcast.43, f32[128,128]{1,0:T(8,128)} %bitcast.40, s32[128,128]{1,0:T(8,128)} %bitcast.35), custom_call_target="tpu_custom_call" | custom-call | tf_op jit(solution)/shard_map/edges/pallas_call | solution.py:347
  2.2 4.9 %collective-permute-start = (f32[3,8,128]{2,1,0:T(8,128)}, f32[3,8,128]{2,1,0:T(8,128)S(1)}, u32[]{:S(2)}, u32[]{:S(2)}) collective-permute-start(f32[3,8,128]{2,1,0:T(8,128)} %get-tuple-element.26), channel_id=1, source_target_pairs={{0,16},{16,32},{32,48},{48,64},{64,80},{80,96},{96,112},{112,128},... | collective-permute-start | bytes 36872 | tf_op jit(solution)/shard_map/ppermute | solution.py:354
  7.1 5.1 %collective-permute-start.1 = (f32[3,8,128]{2,1,0:T(8,128)}, f32[3,8,128]{2,1,0:T(8,128)S(1)}, u32[]{:S(2)}, u32[]{:S(2)}) collective-permute-start(f32[3,8,128]{2,1,0:T(8,128)} %get-tuple-element.27), channel_id=1, source_target_pairs={{16,0},{32,16},{48,32},{64,48},{80,64},{96,80},{112,96},{128,112},... | collective-permute-start | bytes 36872 | tf_op jit(solution)/shard_map/ppermute | solution.py:355
  12.3 1.3 collective-permute-start.2
  13.6 1.3 collective-permute-start.3
  14.9 0.7 pad_add_fusion.place_ref
  15.5 0.0 collective-permute-done
  15.5 0.6 slice_bitcast_fusion.7
  16.1 0.0 collective-permute-done.1
  16.1 0.6 slice_bitcast_fusion.6
  16.7 0.0 collective-permute-done.2
  16.7 0.6 slice_bitcast_fusion.1
  17.4 1.2 collective-permute-done.3
  18.6 0.6 slice_bitcast_fusion
  19.2 3.1 %front.2 = (f32[16,80,128]{2,1,0:T(8,128)}, f32[3,7,16,128]{3,2,1,0:T(8,128)}, f32[128,128]{1,0:T(8,128)}, f32[128,128]{1,0:T(8,128)}) custom-call(s32[2]{0:T(128)} %pad_add_fusion.place_ref, f32[128,128]{1,0:T(8,128)} %bitcast.44, f32[128,128]{1,0:T(8,128)} %bitcast.41, s32[128,128]{1,0:T(8,128)} %bitcast.36, f32[8,128]{1,0:T(8,128)} %get-tuple-element.61.ztlo_ref, ...), custom_call_target="tpu_custom_call" | custom-call | tf_op jit(solution)/shard_map/front/pallas_call | solution.py:364
  22.3 20.2 %all_to_all.20.all_ref = f32[16,80,128]{2,1,0:T(8,128)} all-to-all(f32[16,80,128]{2,1,0:T(8,128)} %get-tuple-element.30), channel_id=1, replica_groups=mesh['gz'=32,'gy'=16] {'gy'}, dimensions={0} | all-to-all | bytes 1310720 | tf_op jit(solution)/shard_map/all_to_all | solution.py:377
  42.5 2.3 %middle.2 = (f32[16,40,128]{2,1,0:T(8,128)}, f32[3,15,8,128]{3,2,1,0:T(8,128)}, f32[8,128]{1,0:T(8,128)}) custom-call(s32[2]{0:T(128)} %pad_add_fusion.place_ref, f32[16,80,128]{2,1,0:T(8,128)} %all_to_all.20.all_ref, f32[3,7,16,128]{3,2,1,0:T(8,128)} %get-tuple-element.31.sub_ref, f32[128,128]{1,0:T(8,128)} %get-tuple-element.32.fluxz_ref, ...), custom_call_target="tpu_custom_call" | custom-call | tf_op jit(solution)/shard_map/middle/pallas_call | solution.py:378
  44.8 25.7 %all_to_all.21 = f32[16,40,128]{2,1,0:T(8,128)S(1)} all-to-all(f32[16,40,128]{2,1,0:T(8,128)} %get-tuple-element.33), channel_id=1, replica_groups={{0,32,64,96,128,160,192,224,256,288,320,352,384,416,448,480},{16,48,80,..., dimensions={0} | all-to-all | bytes 655360 | tf_op jit(solution)/shard_map/all_to_all | solution.py:391
  70.5 10.3 %all-gather = f32[32,40,128]{2,1,0:T(8,128)} all-gather(f32[16,40,128]{2,1,0:T(8,128)S(1)} %all_to_all.21), channel_id=2, replica_groups={{0,16},{32,48},{64,80},{96,112},{128,144},{160,176},{192,208},{224,240}..., dimensions={0}, use_global_device_ids=true | all-gather | bytes 983040 | tf_op jit(solution)/shard_map/all_gather | solution.py:392
  80.8 2.1 %back.2 = (f32[128,128]{1,0:T(8,128)}, f32[16,128]{1,0:T(8,128)}, f32[16,128]{1,0:T(8,128)}, f32[8,128]{1,0:T(8,128)}, f32[8,128]{1,0:T(8,128)}) custom-call(s32[2]{0:T(128)} %pad_add_fusion.place_ref, f32[2,16,40,128]{3,2,1,0:T(8,128)} %bitcast.34, f32[3,15,8,128]{3,2,1,0:T(8,128)} %get-tuple-element.34.subz_ref, f32[8,128]{1,0:T(8,128)} %get-tuple-element.35.entry_ref), custom_call_target="tpu_custom_call" | custom-call | tf_op jit(solution)/shard_map/back/pallas_call | solution.py:393
  82.9 2.3 %collective-permute-start.4 = (f32[16,128]{1,0:T(8,128)}, f32[16,128]{1,0:T(8,128)S(1)}, u32[]{:S(2)}, u32[]{:S(2)}) collective-permute-start(f32[16,128]{1,0:T(8,128)} %get-tuple-element.40), channel_id=1, source_target_pairs={{0,1},{1,2},{2,3},{3,4},{4,5},{5,6},{6,7},{7,8},{8,9},{9,10},{10,1... | collective-permute-start | bytes 24584 | tf_op jit(solution)/shard_map/ppermute | solution.py:404
  85.2 1.3 collective-permute-start.5
  86.5 0.0 collective-permute-done.4.ytlo_ref
  86.5 0.0 copy-start
  86.5 3.3 %collective-permute-done.5.ythi_ref = f32[16,128]{1,0:T(8,128)S(1)} collective-permute-done((f32[16,128]{1,0:T(8,128)}, f32[16,128]{1,0:T(8,128)S(1)}, u32[]{:S(2)}, u32[]{:S(2)}) %collective-permute-start.5) | collective-permute-done | bytes 8224 | tf_op jit(solution)/shard_map/ppermute | solution.py:404
  89.8 0.0 copy-start.1
  89.8 0.0 copy-done
  89.8 0.6 copy-done.1
  90.4 3.1 %front.3 = (f32[16,80,128]{2,1,0:T(8,128)}, f32[3,7,16,128]{3,2,1,0:T(8,128)}, f32[128,128]{1,0:T(8,128)}, f32[128,128]{1,0:T(8,128)}) custom-call(s32[2]{0:T(128)} %pad_add_fusion.place_ref, f32[128,128]{1,0:T(8,128)} %get-tuple-element.36.t_ref, f32[128,128]{1,0:T(8,128)} %get-tuple-element.37.c_ref, s32[128,128]{1,0:T(8,128)} %bitcast.38, ...), custom_call_target="tpu_custom_call" | custom-call | tf_op jit(solution)/shard_map/front/pallas_call | solution.py:364
  93.5 18.3 %all_to_all.22.all_ref = f32[16,80,128]{2,1,0:T(8,128)} all-to-all(f32[16,80,128]{2,1,0:T(8,128)} %get-tuple-element.42), channel_id=1, replica_groups=mesh['gz'=32,'gy'=16] {'gy'}, dimensions={0} | all-to-all | bytes 1310720 | tf_op jit(solution)/shard_map/all_to_all | solution.py:377
  111.7 2.2 %middle.3 = (f32[16,40,128]{2,1,0:T(8,128)}, f32[3,15,8,128]{3,2,1,0:T(8,128)}, f32[8,128]{1,0:T(8,128)}) custom-call(s32[2]{0:T(128)} %pad_add_fusion.place_ref, f32[16,80,128]{2,1,0:T(8,128)} %all_to_all.22.all_ref, f32[3,7,16,128]{3,2,1,0:T(8,128)} %get-tuple-element.43.sub_ref, f32[128,128]{1,0:T(8,128)} %get-tuple-element.44.fluxz_ref, ...), custom_call_target="tpu_custom_call" | custom-call | tf_op jit(solution)/shard_map/middle/pallas_call | solution.py:378
  114.0 19.3 %all_to_all.23 = f32[16,40,128]{2,1,0:T(8,128)S(1)} all-to-all(f32[16,40,128]{2,1,0:T(8,128)} %get-tuple-element.45), channel_id=1, replica_groups={{0,32,64,96,128,160,192,224,256,288,320,352,384,416,448,480},{16,48,80,..., dimensions={0} | all-to-all | bytes 655360 | tf_op jit(solution)/shard_map/all_to_all | solution.py:391
  133.3 10.3 %all-gather.1 = f32[32,40,128]{2,1,0:T(8,128)} all-gather(f32[16,40,128]{2,1,0:T(8,128)S(1)} %all_to_all.23), channel_id=3, replica_groups={{0,16},{32,48},{64,80},{96,112},{128,144},{160,176},{192,208},{224,240}..., dimensions={0}, use_global_device_ids=true | all-gather | bytes 983040 | tf_op jit(solution)/shard_map/all_gather | solution.py:392
  143.6 2.1 %back.3 = (f32[128,128]{1,0:T(8,128)}, f32[16,128]{1,0:T(8,128)}, f32[16,128]{1,0:T(8,128)}, f32[8,128]{1,0:T(8,128)}, f32[8,128]{1,0:T(8,128)}) custom-call(s32[2]{0:T(128)} %pad_add_fusion.place_ref, f32[2,16,40,128]{3,2,1,0:T(8,128)} %bitcast.33, f32[3,15,8,128]{3,2,1,0:T(8,128)} %get-tuple-element.46.subz_ref, f32[8,128]{1,0:T(8,128)} %get-tuple-element.47.entry_ref), custom_call_target="tpu_custom_call" | custom-call | tf_op jit(solution)/shard_map/back/pallas_call | solution.py:393
Async XLA Ops:
  2.2 13.3 %collective-permute-start = (f32[3,8,128]{2,1,0:T(8,128)}, f32[3,8,128]{2,1,0:T(8,128)S(1)}, u32[]{:S(2)}, u32[]{:S(2)}) collective-permute-start(f32[3,8,128]{2,1,0:T(8,128)} %get-tuple-element.26), channel_id=1, source_target_pairs={{0,16},{16,32},{32,48},{48,64},{64,80},{80,96},{96,112},{112,128},... | collective-permute-start | bytes 36872 | tf_op jit(solution)/shard_map/ppermute | solution.py:354
  7.1 9.0 %collective-permute-start.1 = (f32[3,8,128]{2,1,0:T(8,128)}, f32[3,8,128]{2,1,0:T(8,128)S(1)}, u32[]{:S(2)}, u32[]{:S(2)}) collective-permute-start(f32[3,8,128]{2,1,0:T(8,128)} %get-tuple-element.27), channel_id=1, source_target_pairs={{16,0},{32,16},{48,32},{64,48},{80,64},{96,80},{112,96},{128,112},... | collective-permute-start | bytes 36872 | tf_op jit(solution)/shard_map/ppermute | solution.py:355
  12.3 4.5 %collective-permute-start.2 = (f32[3,16,128]{2,1,0:T(8,128)}, f32[3,16,128]{2,1,0:T(8,128)S(1)}, u32[]{:S(2)}, u32[]{:S(2)}) collective-permute-start(f32[3,16,128]{2,1,0:T(8,128)} %get-tuple-element.28), channel_id=1, source_target_pairs={{0,1},{1,2},{2,3},{3,4},{4,5},{5,6},{6,7},{7,8},{8,9},{9,10},{10,1... | collective-permute-start | bytes 73736 | tf_op jit(solution)/shard_map/ppermute | solution.py:356
  13.6 5.0 %collective-permute-start.3 = (f32[3,16,128]{2,1,0:T(8,128)}, f32[3,16,128]{2,1,0:T(8,128)S(1)}, u32[]{:S(2)}, u32[]{:S(2)}) collective-permute-start(f32[3,16,128]{2,1,0:T(8,128)} %get-tuple-element.29), channel_id=1, source_target_pairs={{1,0},{2,1},{3,2},{4,3},{5,4},{6,5},{7,6},{8,7},{9,8},{10,9},{11,1... | collective-permute-start | bytes 73736 | tf_op jit(solution)/shard_map/ppermute | solution.py:357
  82.9 3.6 %collective-permute-start.4 = (f32[16,128]{1,0:T(8,128)}, f32[16,128]{1,0:T(8,128)S(1)}, u32[]{:S(2)}, u32[]{:S(2)}) collective-permute-start(f32[16,128]{1,0:T(8,128)} %get-tuple-element.40), channel_id=1, source_target_pairs={{0,1},{1,2},{2,3},{3,4},{4,5},{5,6},{6,7},{7,8},{8,9},{9,10},{10,1... | collective-permute-start | bytes 24584 | tf_op jit(solution)/shard_map/ppermute | solution.py:404
  85.2 4.6 %collective-permute-start.5 = (f32[16,128]{1,0:T(8,128)}, f32[16,128]{1,0:T(8,128)S(1)}, u32[]{:S(2)}, u32[]{:S(2)}) collective-permute-start(f32[16,128]{1,0:T(8,128)} %get-tuple-element.41), channel_id=1, source_target_pairs={{1,0},{2,1},{3,2},{4,3},{5,4},{6,5},{7,6},{8,7},{9,8},{10,9},{11,1... | collective-permute-start | bytes 24584 | tf_op jit(solution)/shard_map/ppermute | solution.py:404
  86.5 3.3 %copy-start = (f32[16,128]{1,0:T(8,128)}, f32[16,128]{1,0:T(8,128)S(1)}, u32[]{:S(2)}) copy-start(f32[16,128]{1,0:T(8,128)S(1)} %collective-permute-done.4.ytlo_ref) | copy-start | bytes 24580
  89.8 0.6 copy-start.1
where the time goes:
time: 147 us; the launch traced here: 146 us
  blocking collectives  104 us (71%)
  Pallas kernels  16.4 us (11%)
  starting transfers between devices  16.2 us (11%)
  waiting for transfers between devices  4.52 us (3%)
  local copies, waits for them, and re-layouts  3.02 us (2%)
    all_to_all x2, blocking collectives, body(): lax.all_to_all(payz, 'gz', 0, 0, tiled=True, axis_index_groups=same_core)  45.1 us
    all_to_all x2, blocking collectives, body(): everyone = lax.all_to_all(pay, 'gy', 0, 0, tiled=True)  38.5 us
    all_gather x2, blocking collectives, body(): column = lax.all_gather(column, 'gz', axis_index_groups=pairs)  20.6 us
    pallas_call x2, Pallas kernels, body(): pl.pallas_call(functools.partial(front_kernel, groups=groups_y), out_shap...  6.22 us
    ppermute x1, starting transfers between devices, body(): from_above = lax.ppermute(zlo, 'gz', down['gz'])  5.14 us
    ppermute x1, starting transfers between devices, body(): from_below = lax.ppermute(zhi, 'gz', up['gz'])  4.92 us
    pallas_call x2, Pallas kernels, body(): pl.pallas_call(functools.partial(middle_kernel, groups_y=groups_y, groups...  4.5 us
    pallas_call x2, Pallas kernels, body(): pl.pallas_call(functools.partial(back_kernel, groups_z=groups_z, more=ste...  4.14 us
  transfers between devices with their start and end apart: 6, of which 2 were waited for; matrix products, arithmetic and copies ran while one was open for 2% of the time, Pallas kernels for 0%

commit v1 on v0

v1 whole, which is shorter than its diff:
```python
import functools

import jax
import jax.numpy as jnp
from jax import lax
from jax.experimental import pallas as pl
from jax.experimental.pallas import tpu as pltpu
from jax.sharding import PartitionSpec as P

ZC = 16
YC = 8
XC = 128
ROWS = ZC * YC


def f32(*shape):
    return jax.ShapeDtypeStruct(shape, jnp.float32)


def conduct_of(label, cure):
    return jnp.where(label == 1, 40.0, jnp.where(label == 2, 20.0, 0.6 + 0.8 * cure))


def store_of(label):
    return jnp.where(label == 1, 3.0 / 60.0, jnp.where(label == 2, 2.0 / 60.0, 1.0 / 60.0))


def cure_of(label, warmth, cure):
    speed = 0.3 * jnp.exp(8.0 * warmth)
    return jnp.where(label == 0, 1.0 - (1.0 - cure) * jnp.exp(-speed), cure)


def y_rows(y):
    return pl.ds(y, ZC, stride=YC)


def z_rows(z):
    return pl.ds(z * YC, YC)


def edges_kernel(t_ref, c_ref, m_ref, zlo_ref, zhi_ref, ylo_ref, yhi_ref):
    def put(out, rows):
        t, c, m = t_ref[rows, :], c_ref[rows, :], m_ref[rows, :]
        out[0] = t
        out[1] = conduct_of(m, c)
        out[2] = conduct_of(m, cure_of(m, t, c))

    put(zlo_ref, z_rows(0))
    put(zhi_ref, z_rows(ZC - 1))
    put(ylo_ref, y_rows(0))
    put(yhi_ref, y_rows(YC - 1))


def eliminate(count, store, faces, right, entry, keep):
    ground, edge, side = store(0), entry, right(0)
    back_ground = back_side = None
    for i in range(count - 1):
        face = faces(i)
        inv = 1.0 / (ground + edge + face)
        edge_inv, face_inv, side_inv = edge * inv, face * inv, side * inv
        keep(i, side_inv, edge_inv, face_inv)
        more_ground, more_side = edge_inv * ground, edge_inv * side
        back_ground = more_ground if i == 0 else back_ground + more_ground
        back_side = more_side if i == 0 else back_side + more_side
        ground = store(i + 1) + face_inv * ground
        side = right(i + 1) + face_inv * side
        edge = edge_inv * face
    return back_ground, edge, ground, side, back_side


def front(groups, t_ref, c_ref, m_ref, zt, yt, zk, yk, outs, scratch):
    pay_ref, sub_ref, fluxz_ref, cure_ref, entry_ref = outs
    k_ref, g_ref, fy_ref, r_ref = scratch
    t, c, m = t_ref[...], c_ref[...], m_ref[...]
    k_ref[...] = conduct_of(m, c)
    g_ref[...] = store_of(m)
    cure_ref[...] = cure_of(m, t, c)

    ks = [yk[0]] + [k_ref[y_rows(y), :] for y in range(YC)] + [yk[1]]
    ts = [yt[0]] + [t_ref[y_rows(y), :] for y in range(YC)] + [yt[1]]
    face_y = [0.5 * (ks[i] + ks[i + 1]) for i in range(YC + 1)]
    flow_y = [face_y[i] * (ts[i + 1] - ts[i]) for i in range(YC + 1)]
    for y in range(YC):
        fy_ref[y_rows(y), :] = flow_y[y + 1] - flow_y[y]
    if entry_ref is not None:
        entry_ref[...] = face_y[YC]

    lane = lax.broadcasted_iota(jnp.int32, (YC, XC), 1)
    first_lane, last_lane = lane == 0, lane == XC - 1
    k_prev, t_prev = zk[0], zt[0]
    flow_prev = 0.5 * (k_prev + k_ref[z_rows(0), :]) * (t_ref[z_rows(0), :] - t_prev)
    batch = 4
    for z0 in range(0, ZC, batch):
        gs, ls, rs, sides, stores = [], [], [], [], []
        for z in range(z0, z0 + batch):
            kz, tz, g = k_ref[z_rows(z), :], t_ref[z_rows(z), :], g_ref[z_rows(z), :]
            k_next = k_ref[z_rows(z + 1), :] if z + 1 < ZC else zk[1]
            t_next = t_ref[z_rows(z + 1), :] if z + 1 < ZC else zt[1]
            flow_next = 0.5 * (kz + k_next) * (t_next - tz)
            flux_z = flow_next - flow_prev
            flow_prev = flow_next
            fluxz_ref[z_rows(z), :] = flux_z
            k_left = jnp.where(first_lane, 0.0, pltpu.roll(kz, 1, 1))
            t_left = jnp.where(first_lane, 0.0, pltpu.roll(tz, 1, 1))
            face_left = 0.5 * (kz + k_left)
            flow_left = face_left * (tz - t_left)
            face_right = jnp.where(last_lane, 0.5 * kz, pltpu.roll(face_left, XC - 1, 1))
            flow_right = jnp.where(last_lane, -face_right * tz, pltpu.roll(flow_left, XC - 1, 1))
            delta = cure_ref[z_rows(z), :] - c_ref[z_rows(z), :]
            sides.append(
                g * (tz + 0.4 * delta)
                + (flow_right - flow_left)
                + 2.0 * (fy_ref[z_rows(z), :] + flux_z)
            )
            gs.append(
                g
                + jnp.where(first_lane, face_left, 0.0)
                + jnp.where(last_lane, face_right, 0.0)
            )
            ls.append(jnp.where(first_lane, 0.0, face_left))
            rs.append(jnp.where(last_lane, 0.0, face_right))
            stores.append(g)
        stride = 1
        while stride < XC:
            for b in range(batch):
                ground, left, right, side = gs[b], ls[b], rs[b], sides[b]
                inv = 1.0 / (ground + left + right)
                ground_inv, side_inv = ground * inv, side * inv
                gs[b] = (
                    ground
                    + left * pltpu.roll(ground_inv, stride, 1)
                    + right * pltpu.roll(ground_inv, XC - stride, 1)
                )
                sides[b] = (
                    side
                    + left * pltpu.roll(side_inv, stride, 1)
                    + right * pltpu.roll(side_inv, XC - stride, 1)
                )
                if 2 * stride < XC:
                    ls[b] = left * pltpu.roll(left * inv, stride, 1)
                    rs[b] = right * pltpu.roll(right * inv, XC - stride, 1)
            stride *= 2
        for b in range(batch):
            rows = z_rows(z0 + b)
            r_ref[rows, :] = stores[b] * (sides[b] / gs[b]) - fy_ref[rows, :]

    def keep(i, side_inv, edge_inv, face_inv):
        sub_ref[0, i] = side_inv
        sub_ref[1, i] = edge_inv
        sub_ref[2, i] = face_inv

    back_ground, edge, ground, side, back_side = eliminate(
        YC,
        lambda i: g_ref[y_rows(i), :],
        lambda i: face_y[i + 1],
        lambda i: r_ref[y_rows(i), :],
        face_y[0],
        keep,
    )
    ground = ground + jnp.where(lax.axis_index("gy") == groups - 1, face_y[YC], 0.0)
    for d in range(groups):
        pay_ref[d, 0:16] = back_ground
        pay_ref[d, 16:32] = edge
        pay_ref[d, 32:48] = ground
        pay_ref[d, 48:64] = side
        pay_ref[d, 64:80] = back_side


def front_kernel(
    t_ref,
    c_ref,
    m_ref,
    below_ref,
    above_ref,
    south_ref,
    north_ref,
    pay_ref,
    sub_ref,
    fluxz_ref,
    cure_ref,
    entry_ref,
    toward_south_ref,
    toward_north_ref,
    k_ref,
    g_ref,
    fy_ref,
    r_ref,
    *,
    groups,
):
    front(
        groups,
        t_ref,
        c_ref,
        m_ref,
        (below_ref[0], above_ref[0]),
        (south_ref[0], north_ref[0]),
        (below_ref[1], above_ref[1]),
        (south_ref[1], north_ref[1]),
        (pay_ref, sub_ref, fluxz_ref, cure_ref, entry_ref),
        (k_ref, g_ref, fy_ref, r_ref),
    )
    for out, y in ((toward_south_ref, 0), (toward_north_ref, YC - 1)):
        k = k_ref[y_rows(y), :]
        out[0:16] = fluxz_ref[y_rows(y), :]
        out[16:32] = g_ref[y_rows(y), :]
        fy_ref[8:24, :] = k
        fy_ref[7:8, :] = below_ref[1, y : y + 1, :]
        fy_ref[24:25, :] = above_ref[1, y : y + 1, :]
        out[32:48] = 0.5 * (fy_ref[7:23, :] + k)
        out[48:49] = 0.5 * (fy_ref[23:24, :] + fy_ref[24:25, :])


def chain(count, read, put):
    def ground_of(j):
        return read(j, 2) + read(j + 1, 0) if j + 1 < count else read(j, 2)

    def side_of(j):
        return read(j, 3) + read(j + 1, 4) if j + 1 < count else read(j, 3)

    half = count // 2
    gain, part = [None] * count, [None] * count
    ground_l, side_l = ground_of(0) + read(0, 1), side_of(0)
    ground_r, side_r = ground_of(count - 1), side_of(count - 1)
    for i in range(half - 1):
        edge = read(i + 1, 1)
        inv = 1.0 / (ground_l + edge)
        gain[i], part[i] = edge * inv, side_l * inv
        ground_l = ground_of(i + 1) + gain[i] * ground_l
        side_l = side_of(i + 1) + gain[i] * side_l
        j = count - 1 - i
        edge = read(j, 1)
        inv = 1.0 / (ground_r + edge)
        gain[j], part[j] = edge * inv, side_r * inv
        ground_r = ground_of(j - 1) + gain[j] * ground_r
        side_r = side_of(j - 1) + gain[j] * side_r
    edge = read(half, 1)
    inv = 1.0 / (ground_l * ground_r + edge * (ground_l + ground_r))
    low = (side_l * (ground_r + edge) + edge * side_r) * inv
    high = (side_r * (ground_l + edge) + edge * side_l) * inv
    put(half - 1, low)
    put(half, high)
    for i in range(half - 2, -1, -1):
        low = part[i] + gain[i] * low
        put(i, low)
        j = count - 1 - i
        high = part[j] + gain[j] * high
        put(j, high)


def first_of_next(own, after, back_ground, edge, back_side, entry):
    return own - (back_ground * own + edge * (own - after) - back_side) / entry


def middle_kernel(*refs, groups_y, groups_z, copies, now, wide):
    all_ref, sub_ref, fluxz_ref, c_ref, m_ref, below_ref, above_ref = refs[:7]
    refs = refs[7:]
    if wide:
        y_entry_ref, of_south_ref, of_north_ref = refs[:3]
        refs = refs[3:]
    pay_ref, subz_ref, entry_ref = refs[:3]
    refs = refs[3:]
    if wide:
        sub_wide_ref, refs = refs[0], refs[1:]
    s_ref, v_ref, p_ref = refs[:3]
    s_ref[0] = jnp.zeros((ZC, XC), jnp.float32)

    def put(j, value):
        s_ref[j + 1] = value

    chain(groups_y, lambda j, q: all_ref[j, 16 * q : 16 * q + 16, :], put)
    me = lax.axis_index("gy")
    before, own = s_ref[me], s_ref[me + 1]
    value = own
    v_ref[y_rows(YC - 1), :] = value
    for i in range(YC - 2, -1, -1):
        value = (sub_ref[0, i] + sub_ref[1, i] * before) + sub_ref[2, i] * value
        v_ref[y_rows(i), :] = value

    ks = [below_ref[now]]
    for z in range(ZC):
        ks.append(conduct_of(m_ref[z_rows(z), :], c_ref[z_rows(z), :]))
    ks.append(above_ref[now])
    faces = [0.5 * (ks[i] + ks[i + 1]) for i in range(ZC + 1)]
    entry_ref[...] = faces[ZC]

    def keep(i, side_inv, edge_inv, face_inv):
        subz_ref[0, i] = side_inv
        subz_ref[1, i] = edge_inv
        subz_ref[2, i] = face_inv

    def right(i):
        return store_of(m_ref[z_rows(i), :]) * v_ref[z_rows(i), :] - fluxz_ref[z_rows(i), :]

    at_end = lax.axis_index("gz") == groups_z - 1
    numbers = eliminate(
        ZC,
        lambda i: store_of(m_ref[z_rows(i), :]),
        lambda i: faces[i + 1],
        right,
        faces[0],
        keep,
    )
    for q, number in enumerate(numbers):
        if q == 2:
            number = number + jnp.where(at_end, faces[ZC], 0.0)
        p_ref[8 * q : 8 * q + 8] = number

    if wide:
        h_ref = refs[3]
        p_ref[48:56] = jnp.zeros((8, XC), jnp.float32)
        then = jnp.minimum(me + 1, groups_y - 1)
        after = s_ref[then + 1]
        north = first_of_next(
            own,
            after,
            all_ref[then, 0:16, :],
            all_ref[then, 16:32, :],
            all_ref[then, 64:80, :],
            y_entry_ref[...],
        )
        for side, value, of_ref in ((0, before, of_south_ref), (1, north, of_north_ref)):
            capacity = of_ref[16:32]
            rows = pl.ds(side, ZC, stride=2)
            h_ref[0, rows, :] = jnp.where(capacity > 0.0, capacity, 1.0)
            h_ref[1, rows, :] = capacity * value - of_ref[0:16]
            h_ref[2, rows, :] = of_ref[32:48]
            h_ref[2, 32 + side : 33 + side, :] = of_ref[48:49]

        def keep_wide(i, side_inv, edge_inv, face_inv):
            sub_wide_ref[0, i] = side_inv
            sub_wide_ref[1, i] = edge_inv
            sub_wide_ref[2, i] = face_inv

        numbers = eliminate(
            ZC,
            lambda i: h_ref[0, 2 * i : 2 * i + 2, :],
            lambda i: h_ref[2, 2 * i + 2 : 2 * i + 4, :],
            lambda i: h_ref[1, 2 * i : 2 * i + 2, :],
            h_ref[2, 0:2, :],
            keep_wide,
        )
        for q, number in enumerate(numbers):
            if q == 2:
                number = number + jnp.where(at_end, h_ref[2, 32:34, :], 0.0)
            p_ref[40 + 2 * q : 42 + 2 * q] = number
    for d in range(copies):
        pay_ref[d] = p_ref[...]


def back(groups_z, all_ref, subz_ref, t_ref, s_ref):
    s_ref[0] = jnp.zeros((YC, XC), jnp.float32)

    def put(j, value):
        s_ref[j + 1] = value

    chain(groups_z, lambda j, q: all_ref[j % 2, j // 2, 8 * q : 8 * q + 8, :], put)
    me = lax.axis_index("gz")
    before, own = s_ref[me], s_ref[me + 1]
    value = own
    t_ref[z_rows(ZC - 1), :] = value
    for i in range(ZC - 2, -1, -1):
        value = (subz_ref[0, i] + subz_ref[1, i] * before) + subz_ref[2, i] * value
        t_ref[z_rows(i), :] = value
    return before, own


def back_kernel(all_ref, subz_ref, t_ref, s_ref, *, groups_z):
    back(groups_z, all_ref, subz_ref, t_ref, s_ref)


def turn_kernel(
    all_ref,
    subz_ref,
    sub_wide_ref,
    z_entry_ref,
    c_ref,
    m_ref,
    below_ref,
    above_ref,
    south_ref,
    north_ref,
    pay_ref,
    sub_ref,
    fluxz_ref,
    cure_ref,
    s_ref,
    w_ref,
    t_ref,
    e_ref,
    k_ref,
    g_ref,
    fy_ref,
    r_ref,
    *,
    groups_y,
    groups_z,
):
    before, own = back(groups_z, all_ref, subz_ref, t_ref, s_ref)
    me = lax.axis_index("gz")
    then = jnp.minimum(me + 1, groups_z - 1)
    core, chip = lax.rem(then, 2), lax.div(then, 2)
    above = first_of_next(
        own,
        s_ref[then + 1],
        all_ref[core, chip, 0:8, :],
        all_ref[core, chip, 8:16, :],
        all_ref[core, chip, 32:40, :],
        z_entry_ref[...],
    )
    above = jnp.where(me == groups_z - 1, 0.0, above)

    w_ref[0] = jnp.zeros((2, XC), jnp.float32)

    def put(j, value):
        w_ref[j + 1] = value

    chain(groups_z, lambda j, q: all_ref[j % 2, j // 2, 40 + 2 * q : 42 + 2 * q, :], put)
    before_wide, value = w_ref[me], w_ref[me + 1]
    e_ref[2 * ZC - 2 : 2 * ZC] = value
    for i in range(ZC - 2, -1, -1):
        value = (sub_wide_ref[0, i] + sub_wide_ref[1, i] * before_wide) + sub_wide_ref[2, i] * value
        e_ref[2 * i : 2 * i + 2] = value
    row = lax.axis_index("gy")
    south = jnp.where(row == 0, 0.0, e_ref[pl.ds(0, ZC, stride=2), :])
    north = jnp.where(row == groups_y - 1, 0.0, e_ref[pl.ds(1, ZC, stride=2), :])
    front(
        groups_y,
        t_ref,
        c_ref,
        m_ref,
        (before, above),
        (south, north),
        (below_ref[2], above_ref[2]),
        (south_ref[2], north_ref[2]),
        (pay_ref, sub_ref, fluxz_ref, cure_ref, None),
        (k_ref, g_ref, fy_ref, r_ref),
    )


def call(kernel, outs, scratch=(), **static):
    return pl.pallas_call(
        functools.partial(kernel, **static),
        out_shape=outs,
        scratch_shapes=[pltpu.VMEM(shape, jnp.float32) for shape in scratch],
        compiler_params=pltpu.CompilerParams(vmem_limit_bytes=12 * 1024 * 1024),
        name=kernel.__name__,
    )


def body(warmth, cure, label):
    groups_z, groups_y = lax.axis_size("gz"), lax.axis_size("gy")
    chips = groups_z // 2
    up = {a: [(i, i + 1) for i in range(n - 1)] for a, n in (("gz", groups_z), ("gy", groups_y))}
    down = {a: [(j, i) for i, j in up[a]] for a in up}
    pairs = [[2 * i, 2 * i + 1] for i in range(chips)]
    same_core = [[2 * i + core for i in range(chips)] for core in range(2)]
    cells = (ROWS, XC)

    t = warmth.reshape(cells)
    c = cure.reshape(cells)
    m = label.reshape(cells)

    zlo, zhi, ylo, yhi = call(
        edges_kernel, (f32(3, YC, XC), f32(3, YC, XC), f32(3, ZC, XC), f32(3, ZC, XC))
    )(t, c, m)
    z_halo = (lax.ppermute(zhi, "gz", up["gz"]), lax.ppermute(zlo, "gz", down["gz"]))
    y_halo = (lax.ppermute(yhi, "gy", up["gy"]), lax.ppermute(ylo, "gy", down["gy"]))

    def gather_y(pay):
        return lax.all_to_all(pay, "gy", 0, 0, tiled=True)

    def gather_z(pay):
        column = lax.all_to_all(pay, "gz", 0, 0, tiled=True, axis_index_groups=same_core)
        return lax.all_gather(column, "gz", axis_index_groups=pairs)

    sizes = dict(groups_y=groups_y, groups_z=groups_z)
    pay_y, sub_y, block = f32(groups_y, 5 * ZC, XC), f32(3, YC - 1, ZC, XC), f32(*cells)
    sub_z, z_entry = f32(3, ZC - 1, YC, XC), f32(YC, XC)
    line = (groups_y + 1, ZC, XC)
    message = f32(3 * ZC + 1, XC)

    pay, sub, fluxz, c1, y_entry, toward_south, toward_north = call(
        front_kernel,
        (pay_y, sub_y, block, block, f32(ZC, XC), message, message),
        [cells] * 4,
        groups=groups_y,
    )(t, c, m, *z_halo, *y_halo)
    of_south = lax.ppermute(toward_north, "gy", up["gy"])
    of_north = lax.ppermute(toward_south, "gy", down["gy"])
    pay, subz, entry, sub_wide = call(
        middle_kernel,
        (f32(chips, 56, XC), sub_z, z_entry, f32(3, ZC - 1, 2, XC)),
        [line, cells, (56, XC), (3, 2 * ZC + 2, XC)],
        copies=chips,
        now=1,
        wide=True,
        **sizes,
    )(gather_y(pay), sub, fluxz, c, m, *z_halo, y_entry, of_south, of_north)
    pay, sub, fluxz, c2 = call(
        turn_kernel,
        (pay_y, sub_y, block, block),
        [(groups_z + 1, YC, XC), (groups_z + 1, 2, XC), cells, (2 * ZC, XC)] + [cells] * 4,
        **sizes,
    )(gather_z(pay), subz, sub_wide, entry, c1, m, *z_halo, *y_halo)
    pay, subz, entry = call(
        middle_kernel,
        (f32(chips, 40, XC), sub_z, z_entry),
        [line, cells, (40, XC)],
        copies=chips,
        now=2,
        wide=False,
        **sizes,
    )(gather_y(pay), sub, fluxz, c1, m, *z_halo)
    t2 = call(back_kernel, block, [(groups_z + 1, YC, XC)], groups_z=groups_z)(gather_z(pay), subz)
    return t2.reshape(warmth.shape), c2.reshape(cure.shape)


def solution(mesh):
    return jax.shard_map(
        body,
        mesh=mesh,
        in_specs=(P("gz", "gy", None),) * 3,
        out_specs=(P("gz", "gy", None),) * 2,
        check_vma=False,
    )
```

time: 147 us -> 133 us (0.905)
  blocking collectives: 104 us -> 89.5 us
  Pallas kernels: 16.4 us -> 5.08 us
  starting transfers between devices: 16.2 us -> 25.3 us
  waiting for transfers between devices: 4.52 us -> 9.72 us
    all_to_all x4 -> x3, blocking collectives: 83.5 us -> 70.7 us  [the longest x2 55.5 us: gather_z(): lax.all_to_all(pay, 'gz', 0, 0, tiled=True, axis_index_groups=same_core)]
    pallas_call x7 -> x6, Pallas kernels: 16.4 us -> 5.08 us  [the longest x1 2.07 us: body(): call(front_kernel, (pay_y, sub_y, block, block, f32(ZC, XC), message, mes...]
    all_to_all x0 -> x1, starting transfers between devices: none -> 8.04 us  [gather_y(): return lax.all_to_all(pay, 'gy', 0, 0, tiled=True)]
    ppermute x4, waiting for transfers between devices: 1.23 us -> 6.7 us  [the longest x1 2.52 us: body(): of_north = lax.ppermute(toward_south, 'gy', down['gy'])]
    ppermute x1, waiting for transfers between devices: 3.28 us -> 0.01 us  [body(): lax.ppermute(ylo, 'gy', down['gy'])]
    all_to_all x0 -> x1, waiting for transfers between devices: none -> 3.02 us  [gather_y(): return lax.all_to_all(pay, 'gy', 0, 0, tiled=True)]
    squeeze x4 -> x0, local copies, waits for them, and re-layouts: 2.43 us -> none  [the longest x2 1.22 us: body(): yk = (from_south[1 + step], from_north[1 + step])]
    unnamed x4 -> x10, local copies, waits for them, and re-layouts: 0.6 us -> 2.52 us
  transfers between devices with their start and end apart: 6 -> 7, of which waited for: 2 -> 4; matrix products, arithmetic and copies ran while one was open for 2% -> 0% of each run, Pallas kernels for 0% -> 0%
where the time goes in v1:
time: 133 us
  blocking collectives  89.5 us (67%)
  starting transfers between devices  25.3 us (19%)
  waiting for transfers between devices  9.72 us (7%)
  Pallas kernels  5.08 us (4%)
  local copies, waits for them, and re-layouts  2.52 us (2%)
    all_to_all x2, blocking collectives, gather_z(): lax.all_to_all(pay, 'gz', 0, 0, tiled=True, axis_index_groups=same_core)  55.5 us
    all_gather x2, blocking collectives, gather_z(): return lax.all_gather(column, 'gz', axis_index_groups=pairs)  18.8 us
    all_to_all x1, blocking collectives, gather_y(): return lax.all_to_all(pay, 'gy', 0, 0, tiled=True)  15.2 us
    all_to_all x1, starting transfers between devices, gather_y(): return lax.all_to_all(pay, 'gy', 0, 0, tiled=True)  8.04 us
    ppermute x1, starting transfers between devices, body(): lax.ppermute(zhi, 'gz', up['gz'])  4.39 us
    ppermute x1, starting transfers between devices, body(): lax.ppermute(yhi, 'gy', up['gy'])  3.95 us
    ppermute x1, starting transfers between devices, body(): of_south = lax.ppermute(toward_north, 'gy', up['gy'])  3.26 us
    ppermute x1, starting transfers between devices, body(): lax.ppermute(zlo, 'gz', down['gz'])  3.04 us
  transfers between devices with their start and end apart: 7, of which 4 were waited for; matrix products, arithmetic and copies ran while one was open for 0% of the time, Pallas kernels for 0%

profile of v1, /device:TPU:1, one launch (start us, length us, event | category | flops | bytes accessed | tf_op | source)
XLA Modules:
  0.0 132.8 jit_solution(5367942779399814302)
XLA Ops:
  0.6 0.0 copy-start
  0.6 0.8 copy-done
  1.5 0.0 copy-start.2
  1.5 0.8 copy-done.2
  2.3 0.0 copy-start.4
  2.3 0.8 copy-done.4
  3.2 3.9 %collective-permute-start.2 = (f32[3,16,128]{2,1,0:T(8,128)S(1)}, f32[3,16,128]{2,1,0:T(8,128)S(1)}, u32[]{:S(2)}, u32[]{:S(2)}) collective-permute-start(f32[3,16,128]{2,1,0:T(8,128)S(1)} %get-tuple-element.25), channel_id=1, source_target_pairs={{0,1},{1,2},{2,3},{3,4},{4,5},{5,6},{6,7},{7,8},{8,9},{9,10},{10,1... | collective-permute-start | bytes 73736 | tf_op jit(solution)/shard_map/ppermute | solution.py:468
  7.1 1.3 collective-permute-start.3
  8.4 4.4 %collective-permute-start = (f32[3,8,128]{2,1,0:T(8,128)S(1)}, f32[3,8,128]{2,1,0:T(8,128)S(1)}, u32[]{:S(2)}, u32[]{:S(2)}) collective-permute-start(f32[3,8,128]{2,1,0:T(8,128)S(1)} %get-tuple-element.23), channel_id=1, source_target_pairs={{0,16},{16,32},{32,48},{48,64},{64,80},{80,96},{96,112},{112,128},... | collective-permute-start | bytes 36872 | tf_op jit(solution)/shard_map/ppermute | solution.py:467
  12.8 3.0 %collective-permute-start.1 = (f32[3,8,128]{2,1,0:T(8,128)S(1)}, f32[3,8,128]{2,1,0:T(8,128)S(1)}, u32[]{:S(2)}, u32[]{:S(2)}) collective-permute-start(f32[3,8,128]{2,1,0:T(8,128)S(1)} %get-tuple-element.24), channel_id=1, source_target_pairs={{16,0},{32,16},{48,32},{64,48},{80,64},{96,80},{112,96},{128,112},... | collective-permute-start | bytes 36872 | tf_op jit(solution)/shard_map/ppermute | solution.py:467
  15.9 0.0 collective-permute-done.below_ref.refs_5_
  15.9 2.0 %collective-permute-done.1.above_ref.refs_6_ = f32[3,8,128]{2,1,0:T(8,128)S(1)} collective-permute-done((f32[3,8,128]{2,1,0:T(8,128)S(1)}, f32[3,8,128]{2,1,0:T(8,128)S(1)}, u32[]{:S(2)}, u32[]{:S(2)}) %collective-permute-start.1) | collective-permute-done | bytes 12320 | tf_op jit(solution)/shard_map/ppermute | solution.py:467
  17.9 0.0 collective-permute-done.2.south_ref
  17.9 0.0 collective-permute-done.3.north_ref
  17.9 2.1 %front_kernel.1 = (f32[16,80,128]{2,1,0:T(8,128)}, f32[3,7,16,128]{3,2,1,0:T(8,128)S(1)}, f32[128,128]{1,0:T(8,128)S(1)}, f32[128,128]{1,0:T(8,128)S(1)}, f32[16...) custom-call(f32[128,128]{1,0:T(8,128)S(1)} %bitcast.18, f32[128,128]{1,0:T(8,128)S(1)} %bitcast.15, ...), custom_call_target="tpu_custom_call" | custom-call | tf_op jit(solution)/shard_map/front_kernel/pallas_call | solution.py:483
  19.9 0.0 copy-start.1
  19.9 0.0 copy-start.3
  19.9 8.0 %all-to-all-start = ((f32[16,80,128]{2,1,0:T(8,128)}), f32[16,80,128]{2,1,0:T(8,128)S(1)}, u32[]{:S(2)}, u32[]{:S(2)}) async-start(f32[16,80,128]{2,1,0:T(8,128)} %get-tuple-element.27), calls=%async_computation | async-start | bytes 1310720 | tf_op jit(solution)/shard_map/all_to_all | solution.py:471
  28.0 3.3 %collective-permute-start.4 = (f32[49,128]{1,0:T(8,128)S(1)}, f32[49,128]{1,0:T(8,128)S(1)}, u32[]{:S(2)}, u32[]{:S(2)}) collective-permute-start(f32[49,128]{1,0:T(8,128)S(1)} %get-tuple-element.31), channel_id=1, source_target_pairs={{0,1},{1,2},{2,3},{3,4},{4,5},{5,6},{6,7},{7,8},{8,9},{9,10},{10,1... | collective-permute-start | bytes 75272 | tf_op jit(solution)/shard_map/ppermute | solution.py:489
  31.3 1.3 collective-permute-start.5
  32.6 2.2 %collective-permute-done.4.refs_8_ = f32[49,128]{1,0:T(8,128)S(1)} collective-permute-done((f32[49,128]{1,0:T(8,128)S(1)}, f32[49,128]{1,0:T(8,128)S(1)}, u32[]{:S(2)}, u32[]{:S(2)}) %collective-permute-start.4) | collective-permute-done | bytes 25120 | tf_op jit(solution)/shard_map/ppermute | solution.py:489
  34.8 2.5 %collective-permute-done.5.refs_9_ = f32[49,128]{1,0:T(8,128)S(1)} collective-permute-done((f32[49,128]{1,0:T(8,128)S(1)}, f32[49,128]{1,0:T(8,128)S(1)}, u32[]{:S(2)}, u32[]{:S(2)}) %collective-permute-start.5) | collective-permute-done | bytes 25120 | tf_op jit(solution)/shard_map/ppermute | solution.py:490
  37.3 3.0 %all-to-all-done.refs_0_ = f32[16,80,128]{2,1,0:T(8,128)S(1)} async-done(((f32[16,80,128]{2,1,0:T(8,128)}), f32[16,80,128]{2,1,0:T(8,128)S(1)}, u32[]{:S(2)}, u32[]{:S(2)}) %all-to-all-start) | async-done | bytes 655392 | tf_op jit(solution)/shard_map/all_to_all | solution.py:471
  40.3 0.0 copy-done.1
  40.3 0.0 copy-done.3
  40.3 0.3 middle_kernel.2
  40.6 35.9 %all_to_all.20 = f32[16,56,128]{2,1,0:T(8,128)S(1)} all-to-all(f32[16,56,128]{2,1,0:T(8,128)S(1)} %get-tuple-element.33), channel_id=1, replica_groups={{0,32,64,96,128,160,192,224,256,288,320,352,384,416,448,480},{16,48,80,..., dimensions={0} | all-to-all | bytes 917504 | tf_op jit(solution)/shard_map/all_to_all | solution.py:474
  76.5 8.9 %all-gather = f32[32,56,128]{2,1,0:T(8,128)S(1)} all-gather(f32[16,56,128]{2,1,0:T(8,128)S(1)} %all_to_all.20), channel_id=2, replica_groups={{0,16},{32,48},{64,80},{96,112},{128,144},{160,176},{192,208},{224,240}..., dimensions={0}, use_global_device_ids=true | all-gather | bytes 1376256 | tf_op jit(solution)/shard_map/all_gather | solution.py:475
  85.5 1.2 turn_kernel.1
  86.6 15.2 %all_to_all.21.refs_0_ = f32[16,80,128]{2,1,0:T(8,128)S(1)} all-to-all(f32[16,80,128]{2,1,0:T(8,128)S(1)} %get-tuple-element.38), channel_id=1, replica_groups=mesh['gz'=32,'gy'=16] {'gy'}, dimensions={0} | all-to-all | bytes 1310720 | tf_op jit(solution)/shard_map/all_to_all | solution.py:471
  101.8 0.7 middle_kernel.3
  102.5 19.5 %all_to_all.22 = f32[16,40,128]{2,1,0:T(8,128)S(1)} all-to-all(f32[16,40,128]{2,1,0:T(8,128)S(1)} %get-tuple-element.41), channel_id=1, replica_groups={{0,32,64,96,128,160,192,224,256,288,320,352,384,416,448,480},{16,48,80,..., dimensions={0} | all-to-all | bytes 655360 | tf_op jit(solution)/shard_map/all_to_all | solution.py:474
  122.0 9.9 %all-gather.1 = f32[32,40,128]{2,1,0:T(8,128)S(1)} all-gather(f32[16,40,128]{2,1,0:T(8,128)S(1)} %all_to_all.22), channel_id=3, replica_groups={{0,16},{32,48},{64,80},{96,112},{128,144},{160,176},{192,208},{224,240}..., dimensions={0}, use_global_device_ids=true | all-gather | bytes 983040 | tf_op jit(solution)/shard_map/all_gather | solution.py:475
  131.9 0.9 back_kernel.1
  (1 shorter events, 0.0 us)
Async XLA Ops:
  0.6 0.8 copy-start
  1.5 0.8 copy-start.2
  2.3 0.8 copy-start.4
  3.2 14.7 %collective-permute-start.2 = (f32[3,16,128]{2,1,0:T(8,128)S(1)}, f32[3,16,128]{2,1,0:T(8,128)S(1)}, u32[]{:S(2)}, u32[]{:S(2)}) collective-permute-start(f32[3,16,128]{2,1,0:T(8,128)S(1)} %get-tuple-element.25), channel_id=1, source_target_pairs={{0,1},{1,2},{2,3},{3,4},{4,5},{5,6},{6,7},{7,8},{8,9},{9,10},{10,1... | collective-permute-start | bytes 73736 | tf_op jit(solution)/shard_map/ppermute | solution.py:468
  7.1 10.7 %collective-permute-start.3 = (f32[3,16,128]{2,1,0:T(8,128)S(1)}, f32[3,16,128]{2,1,0:T(8,128)S(1)}, u32[]{:S(2)}, u32[]{:S(2)}) collective-permute-start(f32[3,16,128]{2,1,0:T(8,128)S(1)} %get-tuple-element.26), channel_id=1, source_target_pairs={{1,0},{2,1},{3,2},{4,3},{5,4},{6,5},{7,6},{8,7},{9,8},{10,9},{11,1... | collective-permute-start | bytes 73736 | tf_op jit(solution)/shard_map/ppermute | solution.py:468
  8.4 7.4 %collective-permute-start = (f32[3,8,128]{2,1,0:T(8,128)S(1)}, f32[3,8,128]{2,1,0:T(8,128)S(1)}, u32[]{:S(2)}, u32[]{:S(2)}) collective-permute-start(f32[3,8,128]{2,1,0:T(8,128)S(1)} %get-tuple-element.23), channel_id=1, source_target_pairs={{0,16},{16,32},{32,48},{48,64},{64,80},{80,96},{96,112},{112,128},... | collective-permute-start | bytes 36872 | tf_op jit(solution)/shard_map/ppermute | solution.py:467
  12.8 5.0 %collective-permute-start.1 = (f32[3,8,128]{2,1,0:T(8,128)S(1)}, f32[3,8,128]{2,1,0:T(8,128)S(1)}, u32[]{:S(2)}, u32[]{:S(2)}) collective-permute-start(f32[3,8,128]{2,1,0:T(8,128)S(1)} %get-tuple-element.24), channel_id=1, source_target_pairs={{16,0},{32,16},{48,32},{64,48},{80,64},{96,80},{112,96},{128,112},... | collective-permute-start | bytes 36872 | tf_op jit(solution)/shard_map/ppermute | solution.py:467
  19.9 20.4 %copy-start.1 = (s32[16,8,128]{2,1,0:T(8,128)S(1)}, s32[16,8,128]{2,1,0:T(8,128)}, u32[]{:S(2)}) copy-start(s32[16,8,128]{2,1,0:T(8,128)} %param.5) | copy-start | bytes 196612
  19.9 20.4 %copy-start.3 = (f32[16,8,128]{2,1,0:T(8,128)S(1)}, f32[16,8,128]{2,1,0:T(8,128)}, u32[]{:S(2)}) copy-start(f32[16,8,128]{2,1,0:T(8,128)} %param.4) | copy-start | bytes 196612
  19.9 20.4 %all-to-all-start = ((f32[16,80,128]{2,1,0:T(8,128)}), f32[16,80,128]{2,1,0:T(8,128)S(1)}, u32[]{:S(2)}, u32[]{:S(2)}) async-start(f32[16,80,128]{2,1,0:T(8,128)} %get-tuple-element.27), calls=%async_computation | async-start | bytes 1310720 | tf_op jit(solution)/shard_map/all_to_all | solution.py:471
  28.0 6.8 %collective-permute-start.4 = (f32[49,128]{1,0:T(8,128)S(1)}, f32[49,128]{1,0:T(8,128)S(1)}, u32[]{:S(2)}, u32[]{:S(2)}) collective-permute-start(f32[49,128]{1,0:T(8,128)S(1)} %get-tuple-element.31), channel_id=1, source_target_pairs={{0,1},{1,2},{2,3},{3,4},{4,5},{5,6},{6,7},{7,8},{8,9},{9,10},{10,1... | collective-permute-start | bytes 75272 | tf_op jit(solution)/shard_map/ppermute | solution.py:489
  31.3 6.0 %collective-permute-start.5 = (f32[49,128]{1,0:T(8,128)S(1)}, f32[49,128]{1,0:T(8,128)S(1)}, u32[]{:S(2)}, u32[]{:S(2)}) collective-permute-start(f32[49,128]{1,0:T(8,128)S(1)} %get-tuple-element.32), channel_id=1, source_target_pairs={{1,0},{2,1},{3,2},{4,3},{5,4},{6,5},{7,6},{8,7},{9,8},{10,9},{11,1... | collective-permute-start | bytes 75272 | tf_op jit(solution)/shard_map/ppermute | solution.py:490

commit v2 on v1

--- a/solution.py
+++ b/solution.py
@@ -38,7 +38,18 @@
     return pl.ds(z * YC, YC)
 
 
-def edges_kernel(t_ref, c_ref, m_ref, zlo_ref, zhi_ref, ylo_ref, yhi_ref):
+def edges_kernel(
+    t_in, c_in, m_in, zlo_ref, zhi_ref, ylo_ref, yhi_ref, t_ref, c_ref, m_ref, sem
+):
+    copies = [
+        pltpu.make_async_copy(src, dst, sem.at[i])
+        for i, (src, dst) in enumerate(((t_in, t_ref), (c_in, c_ref), (m_in, m_ref)))
+    ]
+    for copy in copies:
+        copy.start()
+    for copy in copies:
+        copy.wait()
+
     def put(out, rows):
         t, c, m = t_ref[rows, :], c_ref[rows, :], m_ref[rows, :]
         out[0] = t
@@ -49,6 +60,14 @@
     put(zhi_ref, z_rows(ZC - 1))
     put(ylo_ref, y_rows(0))
     put(yhi_ref, y_rows(YC - 1))
+
+
+def spread(one_ref, out_ref, sem, count):
+    copies = [pltpu.make_async_copy(one_ref, out_ref.at[d], sem.at[d]) for d in range(count)]
+    for copy in copies:
+        copy.start()
+    for copy in copies:
+        copy.wait()
 
 
 def eliminate(count, store, faces, right, entry, keep):
@@ -70,7 +89,7 @@
 
 def front(groups, t_ref, c_ref, m_ref, zt, yt, zk, yk, outs, scratch):
     pay_ref, sub_ref, fluxz_ref, cure_ref, entry_ref = outs
-    k_ref, g_ref, fy_ref, r_ref = scratch
+    k_ref, g_ref, fy_ref, r_ref, p_ref, sem = scratch
     t, c, m = t_ref[...], c_ref[...], m_ref[...]
     k_ref[...] = conduct_of(m, c)
     g_ref[...] = store_of(m)
@@ -158,12 +177,9 @@
         keep,
     )
     ground = ground + jnp.where(lax.axis_index("gy") == groups - 1, face_y[YC], 0.0)
-    for d in range(groups):
-        pay_ref[d, 0:16] = back_ground
-        pay_ref[d, 16:32] = edge
-        pay_ref[d, 32:48] = ground
-        pay_ref[d, 48:64] = side
-        pay_ref[d, 64:80] = back_side
+    for q, number in enumerate((back_ground, edge, ground, side, back_side)):
+        p_ref[ZC * q : ZC * q + ZC] = number
+    spread(p_ref, pay_ref, sem, groups)
 
 
 def front_kernel(
@@ -185,6 +201,8 @@
     g_ref,
     fy_ref,
     r_ref,
+    p_ref,
+    sem,
     *,
     groups,
 ):
@@ -198,7 +216,7 @@
         (below_ref[1], above_ref[1]),
         (south_ref[1], north_ref[1]),
         (pay_ref, sub_ref, fluxz_ref, cure_ref, entry_ref),
-        (k_ref, g_ref, fy_ref, r_ref),
+        (k_ref, g_ref, fy_ref, r_ref, p_ref, sem),
     )
     for out, y in ((toward_south_ref, 0), (toward_north_ref, YC - 1)):
         k = k_ref[y_rows(y), :]
@@ -252,17 +270,17 @@
     return own - (back_ground * own + edge * (own - after) - back_side) / entry
 
 
-def middle_kernel(*refs, groups_y, groups_z, copies, now, wide):
+def middle_kernel(*refs, groups_y, groups_z, now, wide):
     all_ref, sub_ref, fluxz_ref, c_ref, m_ref, below_ref, above_ref = refs[:7]
     refs = refs[7:]
     if wide:
         y_entry_ref, of_south_ref, of_north_ref = refs[:3]
         refs = refs[3:]
-    pay_ref, subz_ref, entry_ref = refs[:3]
+    p_ref, subz_ref, entry_ref = refs[:3]
     refs = refs[3:]
     if wide:
         sub_wide_ref, refs = refs[0], refs[1:]
-    s_ref, v_ref, p_ref = refs[:3]
+    s_ref, v_ref = refs[:2]
     s_ref[0] = jnp.zeros((ZC, XC), jnp.float32)
 
     def put(j, value):
@@ -307,7 +325,7 @@
         p_ref[8 * q : 8 * q + 8] = number
 
     if wide:
-        h_ref = refs[3]
+        h_ref = refs[2]
         p_ref[48:56] = jnp.zeros((8, XC), jnp.float32)
         then = jnp.minimum(me + 1, groups_y - 1)
         after = s_ref[then + 1]
@@ -344,33 +362,101 @@
             if q == 2:
                 number = number + jnp.where(at_end, h_ref[2, 32:34, :], 0.0)
             p_ref[40 + 2 * q : 42 + 2 * q] = number
-    for d in range(copies):
-        pay_ref[d] = p_ref[...]
-
-
-def back(groups_z, all_ref, subz_ref, t_ref, s_ref):
-    s_ref[0] = jnp.zeros((YC, XC), jnp.float32)
+
+
+def pair_numbers(pair_ref, rows):
+    return [[pair_ref[core, rows(q), :] for q in range(5)] for core in range(2)]
+
+
+def between(low, high):
+    ground, side = low[2] + high[0], low[3] + high[4]
+    return ground, side, 1.0 / (ground + low[1] + high[1])
+
+
+def main_rows(q):
+    return pl.ds(YC * q, YC)
+
+
+def wide_rows(q):
+    return pl.ds(5 * YC + 2 * q, 2)
+
+
+def merge_kernel(pair_ref, pay_ref, p_ref, sem, *, copies, wide):
+    def merged(rows):
+        low, high = pair_numbers(pair_ref, rows)
+        ground, side, inv = between(low, high)
+        low_inv, high_inv = low[1] * inv, high[1] * inv
+        return (
+            low[0] + low_inv * ground,
+            low_inv * high[1],
+            high[2] + high_inv * ground,
+            high[3] + high_inv * side,
+            low[4] + low_inv * side,
+        )
+
+    half = YC // 2
+    width = half + wide
+    core = lax.rem(lax.axis_index("gz"), 2)
+    if p_ref.shape[0] > 5 * width:
+        p_ref[p_ref.shape[0] - 8 :] = jnp.zeros((8, XC), jnp.float32)
+    for q, number in enumerate(merged(main_rows)):
+        p_ref[width * q : width * q + half] = jnp.where(core == 0, number[:half], number[half:])
+    if wide:
+        for q, number in enumerate(merged(wide_rows)):
+            row = width * q + half
+            p_ref[row : row + 1] = jnp.where(core == 0, number[:1], number[1:])
+    spread(p_ref, pay_ref, sem, copies)
+
+
+def chain_kernel(all_ref, out_ref, s_ref, *, chips, width):
+    s_ref[0] = jnp.zeros((width, XC), jnp.float32)
 
     def put(j, value):
         s_ref[j + 1] = value
 
-    chain(groups_z, lambda j, q: all_ref[j % 2, j // 2, 8 * q : 8 * q + 8, :], put)
-    me = lax.axis_index("gz")
-    before, own = s_ref[me], s_ref[me + 1]
+    chain(chips, lambda j, q: all_ref[j, width * q : width * q + width, :], put)
+    me = lax.div(lax.axis_index("gz"), 2)
+    then = jnp.minimum(me + 1, chips - 1)
+    own, after = s_ref[me + 1], s_ref[then + 1]
+    numbers = [all_ref[then, width * q : width * q + width, :] for q in range(5)]
+    out_ref[8:16] = jnp.zeros((8, XC), jnp.float32)
+    out_ref[0:width] = s_ref[me]
+    out_ref[width : 2 * width] = own
+    out_ref[2 * width : 3 * width] = numbers[0] * own + numbers[1] * (own - after) - numbers[4]
+
+
+def ends_of(pair_ref, rows, before, last):
+    low, high = pair_numbers(pair_ref, rows)
+    ground, side, inv = between(low, high)
+    node = (side + low[1] * before + high[1] * last) * inv
+    upper = lax.rem(lax.axis_index("gz"), 2) == 1
+    return jnp.where(upper, node, before), jnp.where(upper, last, node), node, high
+
+
+def back(pair_ref, res_ref, subz_ref, t_ref, u_ref, width):
+    half = YC // 2
+    for q in range(3):
+        for core in range(2):
+            u_ref[q, half * core : half * core + half] = res_ref[
+                core, width * q : width * q + half, :
+            ]
+    last = u_ref[1]
+    before, own, node, high = ends_of(pair_ref, main_rows, u_ref[0], last)
     value = own
     t_ref[z_rows(ZC - 1), :] = value
     for i in range(ZC - 2, -1, -1):
         value = (subz_ref[0, i] + subz_ref[1, i] * before) + subz_ref[2, i] * value
         t_ref[z_rows(i), :] = value
-    return before, own
-
-
-def back_kernel(all_ref, subz_ref, t_ref, s_ref, *, groups_z):
-    back(groups_z, all_ref, subz_ref, t_ref, s_ref)
+    return before, own, node, last, high
+
+
+def back_kernel(pair_ref, res_ref, subz_ref, t_ref, u_ref):
+    back(pair_ref, res_ref, subz_ref, t_ref, u_ref, YC // 2)
 
 
 def turn_kernel(
-    all_ref,
+    pair_ref,
+    res_ref,
     subz_ref,
     sub_wide_ref,
     z_entry_ref,
@@ -384,7 +470,7 @@
     sub_ref,
     fluxz_ref,
     cure_ref,
-    s_ref,
+    u_ref,
     w_ref,
     t_ref,
     e_ref,
@@ -392,31 +478,25 @@
     g_ref,
     fy_ref,
     r_ref,
+    p_ref,
+    sem,
     *,
     groups_y,
     groups_z,
 ):
-    before, own = back(groups_z, all_ref, subz_ref, t_ref, s_ref)
+    half = YC // 2
+    width = half + 1
+    before, own, node, last, high = back(pair_ref, res_ref, subz_ref, t_ref, u_ref, width)
     me = lax.axis_index("gz")
-    then = jnp.minimum(me + 1, groups_z - 1)
-    core, chip = lax.rem(then, 2), lax.div(then, 2)
-    above = first_of_next(
-        own,
-        s_ref[then + 1],
-        all_ref[core, chip, 0:8, :],
-        all_ref[core, chip, 8:16, :],
-        all_ref[core, chip, 32:40, :],
-        z_entry_ref[...],
-    )
-    above = jnp.where(me == groups_z - 1, 0.0, above)
-
-    w_ref[0] = jnp.zeros((2, XC), jnp.float32)
-
-    def put(j, value):
-        w_ref[j + 1] = value
-
-    chain(groups_z, lambda j, q: all_ref[j % 2, j // 2, 40 + 2 * q : 42 + 2 * q, :], put)
-    before_wide, value = w_ref[me], w_ref[me + 1]
+    inside = high[0] * node + high[1] * (node - last) - high[4]
+    current = jnp.where(lax.rem(me, 2) == 1, u_ref[2], inside)
+    above = jnp.where(me == groups_z - 1, 0.0, own - current / z_entry_ref[...])
+
+    for q in range(2):
+        for core in range(2):
+            row = width * q + half
+            w_ref[q, core : core + 1] = res_ref[core, row : row + 1, :]
+    before_wide, value, _, _ = ends_of(pair_ref, wide_rows, w_ref[0], w_ref[1])
     e_ref[2 * ZC - 2 : 2 * ZC] = value
     for i in range(ZC - 2, -1, -1):
         value = (sub_wide_ref[0, i] + sub_wide_ref[1, i] * before_wide) + sub_wide_ref[2, i] * value
@@ -434,15 +514,21 @@
         (below_ref[2], above_ref[2]),
         (south_ref[2], north_ref[2]),
         (pay_ref, sub_ref, fluxz_ref, cure_ref, None),
-        (k_ref, g_ref, fy_ref, r_ref),
+        (k_ref, g_ref, fy_ref, r_ref, p_ref, sem),
     )
 
 
-def call(kernel, outs, scratch=(), **static):
+def call(kernel, outs, scratch=(), spread_to=0, **static):
+    out_specs = [pl.BlockSpec(memory_space=pltpu.VMEM)] * len(outs)
+    shapes = [pltpu.VMEM(shape, jnp.float32) for shape in scratch]
+    if spread_to:
+        out_specs[0] = pl.BlockSpec(memory_space=pl.ANY)
+        shapes.append(pltpu.SemaphoreType.DMA((spread_to,)))
     return pl.pallas_call(
         functools.partial(kernel, **static),
-        out_shape=outs,
-        scratch_shapes=[pltpu.VMEM(shape, jnp.float32) for shape in scratch],
+        out_shape=tuple(outs),
+        out_specs=tuple(out_specs),
+        scratch_shapes=shapes,
         compiler_params=pltpu.CompilerParams(vmem_limit_bytes=12 * 1024 * 1024),
         name=kernel.__name__,
     )
@@ -456,13 +542,24 @@
     pairs = [[2 * i, 2 * i + 1] for i in range(chips)]
     same_core = [[2 * i + core for i in range(chips)] for core in range(2)]
     cells = (ROWS, XC)
+    block = f32(*cells)
 
     t = warmth.reshape(cells)
     c = cure.reshape(cells)
     m = label.reshape(cells)
 
-    zlo, zhi, ylo, yhi = call(
-        edges_kernel, (f32(3, YC, XC), f32(3, YC, XC), f32(3, ZC, XC), f32(3, ZC, XC))
+    zlo, zhi, ylo, yhi = pl.pallas_call(
+        edges_kernel,
+        out_shape=(f32(3, YC, XC), f32(3, YC, XC), f32(3, ZC, XC), f32(3, ZC, XC)),
+        in_specs=[pl.BlockSpec(memory_space=pltpu.HBM)] * 3,
+        scratch_shapes=[
+            pltpu.VMEM(cells, jnp.float32),
+            pltpu.VMEM(cells, jnp.float32),
+            pltpu.VMEM(cells, jnp.int32),
+            pltpu.SemaphoreType.DMA((3,)),
+        ],
+        compiler_params=pltpu.CompilerParams(vmem_limit_bytes=12 * 1024 * 1024),
+        name="edges_kernel",
     )(t, c, m)
     z_halo = (lax.ppermute(zhi, "gz", up["gz"]), lax.ppermute(zlo, "gz", down["gz"]))
     y_halo = (lax.ppermute(yhi, "gy", up["gy"]), lax.ppermute(ylo, "gy", down["gy"]))
@@ -470,49 +567,68 @@
     def gather_y(pay):
         return lax.all_to_all(pay, "gy", 0, 0, tiled=True)
 
-    def gather_z(pay):
+    def share(numbers):
+        return lax.all_gather(numbers, "gz", axis_index_groups=pairs)
+
+    def chain_z(pair, wide):
+        width = YC // 2 + wide
+        rows = -(-5 * width // 8) * 8
+        (pay,) = call(
+            merge_kernel,
+            [f32(chips, rows, XC)],
+            [(rows, XC)],
+            spread_to=chips,
+            copies=chips,
+            wide=wide,
+        )(pair)
         column = lax.all_to_all(pay, "gz", 0, 0, tiled=True, axis_index_groups=same_core)
-        return lax.all_gather(column, "gz", axis_index_groups=pairs)
+        (found,) = call(
+            chain_kernel, [f32(16, XC)], [(chips + 1, width, XC)], chips=chips, width=width
+        )(column)
+        return share(found)
 
     sizes = dict(groups_y=groups_y, groups_z=groups_z)
-    pay_y, sub_y, block = f32(groups_y, 5 * ZC, XC), f32(3, YC - 1, ZC, XC), f32(*cells)
+    pay_y, sub_y = f32(groups_y, 5 * ZC, XC), f32(3, YC - 1, ZC, XC)
     sub_z, z_entry = f32(3, ZC - 1, YC, XC), f32(YC, XC)
     line = (groups_y + 1, ZC, XC)
     message = f32(3 * ZC + 1, XC)
+    front_scratch = [cells] * 4 + [(5 * ZC, XC)]
 
     pay, sub, fluxz, c1, y_entry, toward_south, toward_north = call(
         front_kernel,
-        (pay_y, sub_y, block, block, f32(ZC, XC), message, message),
-        [cells] * 4,
+        [pay_y, sub_y, block, block, f32(ZC, XC), message, message],
+        front_scratch,
+        spread_to=groups_y,
         groups=groups_y,
     )(t, c, m, *z_halo, *y_halo)
     of_south = lax.ppermute(toward_north, "gy", up["gy"])
     of_north = lax.ppermute(toward_south, "gy", down["gy"])
-    pay, subz, entry, sub_wide = call(
+    numbers, subz, entry, sub_wide = call(
         middle_kernel,
-        (f32(chips, 56, XC), sub_z, z_entry, f32(3, ZC - 1, 2, XC)),
-        [line, cells, (56, XC), (3, 2 * ZC + 2, XC)],
-        copies=chips,
+        [f32(56, XC), sub_z, z_entry, f32(3, ZC - 1, 2, XC)],
+        [line, cells, (3, 2 * ZC + 2, XC)],
         now=1,
         wide=True,
         **sizes,
     )(gather_y(pay), sub, fluxz, c, m, *z_halo, y_entry, of_south, of_north)
+    pair = share(numbers)
     pay, sub, fluxz, c2 = call(
         turn_kernel,
-        (pay_y, sub_y, block, block),
-        [(groups_z + 1, YC, XC), (groups_z + 1, 2, XC), cells, (2 * ZC, XC)] + [cells] * 4,
+        [pay_y, sub_y, block, block],
+        [(3, YC, XC), (2, 2, XC), cells, (2 * ZC, XC)] + front_scratch,
+        spread_to=groups_y,
         **sizes,
-    )(gather_z(pay), subz, sub_wide, entry, c1, m, *z_halo, *y_halo)
-    pay, subz, entry = call(
+    )(pair, chain_z(pair, True), subz, sub_wide, entry, c1, m, *z_halo, *y_halo)
+    numbers, subz, entry = call(
         middle_kernel,
-        (f32(chips, 40, XC), sub_z, z_entry),
-        [line, cells, (40, XC)],
-        copies=chips,
+        [f32(40, XC), sub_z, z_entry],
+        [line, cells],
         now=2,
         wide=False,
         **sizes,
     )(gather_y(pay), sub, fluxz, c1, m, *z_halo)
-    t2 = call(back_kernel, block, [(groups_z + 1, YC, XC)], groups_z=groups_z)(gather_z(pay), subz)
+    pair = share(numbers)
+    (t2,) = call(back_kernel, [block], [(3, YC, XC)])(pair, chain_z(pair, False), subz)
     return t2.reshape(warmth.shape), c2.reshape(cure.shape)
 
 

time: 133 us -> 127 us (0.955)
  blocking collectives: 89.5 us -> 80.5 us
  Pallas kernels: 5.08 us -> 7.97 us
    all_to_all x2, blocking collectives: 55.5 us -> 47.9 us  [chain_z(): lax.all_to_all(pay, 'gz', 0, 0, tiled=True, axis_index_groups=same_core)]
    pallas_call x6 -> x10, Pallas kernels: 5.08 us -> 7.97 us  [the longest x1 2.78 us: body(): call(turn_kernel, [pay_y, sub_y, block, block], [(3, YC, XC), (2, 2, XC),...]
    all_gather x2 -> x4, blocking collectives: 18.8 us -> 16.1 us  [share(): return lax.all_gather(numbers, 'gz', axis_index_groups=pairs)]
where the time goes in v2:
time: 127 us
  blocking collectives  80.5 us (63%)
  starting transfers between devices  25.3 us (20%)
  waiting for transfers between devices  9.72 us (8%)
  Pallas kernels  7.97 us (6%)
  local copies, waits for them, and re-layouts  2.53 us (2%)
    all_to_all x2, blocking collectives, chain_z(): lax.all_to_all(pay, 'gz', 0, 0, tiled=True, axis_index_groups=same_core)  47.9 us
    all_to_all x1, blocking collectives, gather_y(): return lax.all_to_all(pay, 'gy', 0, 0, tiled=True)  16.5 us
    all_gather x4, blocking collectives, share(): return lax.all_gather(numbers, 'gz', axis_index_groups=pairs)  16.1 us
    all_to_all x1, starting transfers between devices, gather_y(): return lax.all_to_all(pay, 'gy', 0, 0, tiled=True)  8.05 us
    ppermute x1, starting transfers between devices, body(): lax.ppermute(zhi, 'gz', up['gz'])  4.39 us
    ppermute x1, starting transfers between devices, body(): lax.ppermute(yhi, 'gy', up['gy'])  3.95 us
    ppermute x1, starting transfers between devices, body(): of_south = lax.ppermute(toward_north, 'gy', up['gy'])  3.26 us
    ppermute x1, starting transfers between devices, body(): lax.ppermute(zlo, 'gz', down['gz'])  3.04 us
  transfers between devices with their start and end apart: 7, of which 4 were waited for; matrix products, arithmetic and copies ran while one was open for 0% of the time, Pallas kernels for 0%

profile of v2, /device:TPU:1, one launch (start us, length us, event | category | flops | bytes accessed | tf_op | source)
XLA Modules:
  0.0 126.7 jit_solution(6279851457114572470)
XLA Ops:
  0.6 0.0 copy-start
  0.6 0.8 copy-done
  1.5 0.0 copy-start.2
  1.5 0.8 copy-done.2
  2.3 0.0 copy-start.4
  2.3 0.8 copy-done.4
  3.2 0.3 edges_kernel.1
  3.4 3.9 %collective-permute-start.2 = (f32[3,16,128]{2,1,0:T(8,128)S(1)}, f32[3,16,128]{2,1,0:T(8,128)S(1)}, u32[]{:S(2)}, u32[]{:S(2)}) collective-permute-start(f32[3,16,128]{2,1,0:T(8,128)S(1)} %get-tuple-element.25), channel_id=1, source_target_pairs={{0,1},{1,2},{2,3},{3,4},{4,5},{5,6},{6,7},{7,8},{8,9},{9,10},{10,1... | collective-permute-start | bytes 73736 | tf_op jit(solution)/shard_map/ppermute | solution.py:565
  7.4 1.3 %collective-permute-start.3 = (f32[3,16,128]{2,1,0:T(8,128)S(1)}, f32[3,16,128]{2,1,0:T(8,128)S(1)}, u32[]{:S(2)}, u32[]{:S(2)}) collective-permute-start(f32[3,16,128]{2,1,0:T(8,128)S(1)} %get-tuple-element.26), channel_id=1, source_target_pairs={{1,0},{2,1},{3,2},{4,3},{5,4},{6,5},{7,6},{8,7},{9,8},{10,9},{11,1... | collective-permute-start | bytes 73736 | tf_op jit(solution)/shard_map/ppermute | solution.py:565
  8.7 4.4 %collective-permute-start = (f32[3,8,128]{2,1,0:T(8,128)S(1)}, f32[3,8,128]{2,1,0:T(8,128)S(1)}, u32[]{:S(2)}, u32[]{:S(2)}) collective-permute-start(f32[3,8,128]{2,1,0:T(8,128)S(1)} %get-tuple-element.23), channel_id=1, source_target_pairs={{0,16},{16,32},{32,48},{48,64},{64,80},{80,96},{96,112},{112,128},... | collective-permute-start | bytes 36872 | tf_op jit(solution)/shard_map/ppermute | solution.py:564
  13.1 3.0 %collective-permute-start.1 = (f32[3,8,128]{2,1,0:T(8,128)S(1)}, f32[3,8,128]{2,1,0:T(8,128)S(1)}, u32[]{:S(2)}, u32[]{:S(2)}) collective-permute-start(f32[3,8,128]{2,1,0:T(8,128)S(1)} %get-tuple-element.24), channel_id=1, source_target_pairs={{16,0},{32,16},{48,32},{64,48},{80,64},{96,80},{112,96},{128,112},... | collective-permute-start | bytes 36872 | tf_op jit(solution)/shard_map/ppermute | solution.py:564
  16.1 0.0 collective-permute-done.below_ref.refs_5_
  16.1 2.0 %collective-permute-done.1.above_ref.refs_6_ = f32[3,8,128]{2,1,0:T(8,128)S(1)} collective-permute-done((f32[3,8,128]{2,1,0:T(8,128)S(1)}, f32[3,8,128]{2,1,0:T(8,128)S(1)}, u32[]{:S(2)}, u32[]{:S(2)}) %collective-permute-start.1) | collective-permute-done | bytes 12320 | tf_op jit(solution)/shard_map/ppermute | solution.py:564
  18.1 0.0 collective-permute-done.2.south_ref
  18.1 0.0 collective-permute-done.3.north_ref
  18.1 2.2 %front_kernel.1 = (f32[16,80,128]{2,1,0:T(8,128)}, f32[3,7,16,128]{3,2,1,0:T(8,128)S(1)}, f32[128,128]{1,0:T(8,128)S(1)}, f32[128,128]{1,0:T(8,128)S(1)}, f32[16...) custom-call(f32[128,128]{1,0:T(8,128)S(1)} %bitcast.22, f32[128,128]{1,0:T(8,128)S(1)} %bitcast.15, ...), custom_call_target="tpu_custom_call" | custom-call | tf_op jit(solution)/shard_map/front_kernel/pallas_call | solution.py:597
  20.3 0.0 copy-start.1
  20.3 0.0 copy-start.3
  20.3 8.1 %all-to-all-start = ((f32[16,80,128]{2,1,0:T(8,128)}), f32[16,80,128]{2,1,0:T(8,128)S(1)}, u32[]{:S(2)}, u32[]{:S(2)}) async-start(f32[16,80,128]{2,1,0:T(8,128)} %get-tuple-element.27), calls=%async_computation | async-start | bytes 1310720 | tf_op jit(solution)/shard_map/all_to_all | solution.py:568
  28.4 3.3 %collective-permute-start.4 = (f32[49,128]{1,0:T(8,128)S(1)}, f32[49,128]{1,0:T(8,128)S(1)}, u32[]{:S(2)}, u32[]{:S(2)}) collective-permute-start(f32[49,128]{1,0:T(8,128)S(1)} %get-tuple-element.31), channel_id=1, source_target_pairs={{0,1},{1,2},{2,3},{3,4},{4,5},{5,6},{6,7},{7,8},{8,9},{9,10},{10,1... | collective-permute-start | bytes 75272 | tf_op jit(solution)/shard_map/ppermute | solution.py:604
  31.6 1.3 %collective-permute-start.5 = (f32[49,128]{1,0:T(8,128)S(1)}, f32[49,128]{1,0:T(8,128)S(1)}, u32[]{:S(2)}, u32[]{:S(2)}) collective-permute-start(f32[49,128]{1,0:T(8,128)S(1)} %get-tuple-element.32), channel_id=1, source_target_pairs={{1,0},{2,1},{3,2},{4,3},{5,4},{6,5},{7,6},{8,7},{9,8},{10,9},{11,1... | collective-permute-start | bytes 75272 | tf_op jit(solution)/shard_map/ppermute | solution.py:605
  32.9 2.2 %collective-permute-done.4.refs_8_ = f32[49,128]{1,0:T(8,128)S(1)} collective-permute-done((f32[49,128]{1,0:T(8,128)S(1)}, f32[49,128]{1,0:T(8,128)S(1)}, u32[]{:S(2)}, u32[]{:S(2)}) %collective-permute-start.4) | collective-permute-done | bytes 25120 | tf_op jit(solution)/shard_map/ppermute | solution.py:604
  35.2 2.5 %collective-permute-done.5.refs_9_ = f32[49,128]{1,0:T(8,128)S(1)} collective-permute-done((f32[49,128]{1,0:T(8,128)S(1)}, f32[49,128]{1,0:T(8,128)S(1)}, u32[]{:S(2)}, u32[]{:S(2)}) %collective-permute-start.5) | collective-permute-done | bytes 25120 | tf_op jit(solution)/shard_map/ppermute | solution.py:605
  37.7 3.0 %all-to-all-done.refs_0_ = f32[16,80,128]{2,1,0:T(8,128)S(1)} async-done(((f32[16,80,128]{2,1,0:T(8,128)}), f32[16,80,128]{2,1,0:T(8,128)S(1)}, u32[]{:S(2)}, u32[]{:S(2)}) %all-to-all-start) | async-done | bytes 655392 | tf_op jit(solution)/shard_map/all_to_all | solution.py:568
  40.7 0.0 copy-done.1
  40.7 0.0 copy-done.3
  40.7 0.2 middle_kernel.2
  41.0 1.8 %all-gather = f32[112,128]{1,0:T(8,128)S(1)} all-gather(f32[56,128]{1,0:T(8,128)S(1)} %get-tuple-element.33), channel_id=2, replica_groups={{0,16},{32,48},{64,80},{96,112},{128,144},{160,176},{192,208},{224,240}..., dimensions={0}, use_global_device_ids=true | all-gather | bytes 86016 | tf_op jit(solution)/shard_map/all_gather | solution.py:571
  42.8 0.5 merge_kernel.2
  43.3 29.4 %all_to_all.20.all_ref = f32[16,32,128]{2,1,0:T(8,128)S(1)} all-to-all(f32[16,32,128]{2,1,0:T(8,128)S(1)} %merge_kernel.2), channel_id=1, replica_groups={{0,32,64,96,128,160,192,224,256,288,320,352,384,416,448,480},{16,48,80,..., dimensions={0} | all-to-all | bytes 524288 | tf_op jit(solution)/shard_map/all_to_all | solution.py:584
  72.8 0.1 chain_kernel.2
  72.9 6.6 %all-gather.1 = f32[32,128]{1,0:T(8,128)S(1)} all-gather(f32[16,128]{1,0:T(8,128)S(1)} %chain_kernel.2), channel_id=3, replica_groups={{0,16},{32,48},{64,80},{96,112},{128,144},{160,176},{192,208},{224,240}..., dimensions={0}, use_global_device_ids=true | all-gather | bytes 24576 | tf_op jit(solution)/shard_map/all_gather | solution.py:571
  79.5 2.8 %turn_kernel.1 = (f32[16,80,128]{2,1,0:T(8,128)S(1)}, f32[3,7,16,128]{3,2,1,0:T(8,128)S(1)}, f32[128,128]{1,0:T(8,128)S(1)}, f32[128,128]{1,0:T(8,128)}) custom-call(f32[2,56,128]{2,1,0:T(8,128)S(1)} %bitcast.18, f32[2,16,128]{2,1,0:T(8,128)S(1)} %bitcast.23, f32[3,15,8,128]{3,2,1,0:T(8,128)S(1)} %get-tuple-element.34.subz_ref, ...), custom_call_target="tpu_custom_call" | custom-call | tf_op jit(solution)/shard_map/turn_kernel/pallas_call | solution.py:615
  82.3 16.5 %all_to_all.21.refs_0_ = f32[16,80,128]{2,1,0:T(8,128)S(1)} all-to-all(f32[16,80,128]{2,1,0:T(8,128)S(1)} %get-tuple-element.38), channel_id=1, replica_groups=mesh['gz'=32,'gy'=16] {'gy'}, dimensions={0} | all-to-all | bytes 1310720 | tf_op jit(solution)/shard_map/all_to_all | solution.py:568
  98.8 0.7 middle_kernel.3
  99.5 2.9 %all-gather.2 = f32[80,128]{1,0:T(8,128)S(1)} all-gather(f32[40,128]{1,0:T(8,128)S(1)} %get-tuple-element.41), channel_id=4, replica_groups={{0,16},{32,48},{64,80},{96,112},{128,144},{160,176},{192,208},{224,240}..., dimensions={0}, use_global_device_ids=true | all-gather | bytes 61440 | tf_op jit(solution)/shard_map/all_gather | solution.py:571
  102.4 0.4 merge_kernel.3
  102.8 18.4 %all_to_all.22.all_ref = f32[16,24,128]{2,1,0:T(8,128)S(1)} all-to-all(f32[16,24,128]{2,1,0:T(8,128)S(1)} %merge_kernel.3), channel_id=1, replica_groups={{0,32,64,96,128,160,192,224,256,288,320,352,384,416,448,480},{16,48,80,..., dimensions={0} | all-to-all | bytes 393216 | tf_op jit(solution)/shard_map/all_to_all | solution.py:584
  121.2 0.1 chain_kernel.3
  121.3 4.7 %all-gather.3 = f32[32,128]{1,0:T(8,128)S(1)} all-gather(f32[16,128]{1,0:T(8,128)S(1)} %chain_kernel.3), channel_id=5, replica_groups={{0,16},{32,48},{64,80},{96,112},{128,144},{160,176},{192,208},{224,240}..., dimensions={0}, use_global_device_ids=true | all-gather | bytes 24576 | tf_op jit(solution)/shard_map/all_gather | solution.py:571
  126.1 0.7 back_kernel.1
Async XLA Ops:
  0.6 0.8 copy-start
  1.5 0.8 copy-start.2
  2.3 0.8 copy-start.4
  3.4 14.7 %collective-permute-start.2 = (f32[3,16,128]{2,1,0:T(8,128)S(1)}, f32[3,16,128]{2,1,0:T(8,128)S(1)}, u32[]{:S(2)}, u32[]{:S(2)}) collective-permute-start(f32[3,16,128]{2,1,0:T(8,128)S(1)} %get-tuple-element.25), channel_id=1, source_target_pairs={{0,1},{1,2},{2,3},{3,4},{4,5},{5,6},{6,7},{7,8},{8,9},{9,10},{10,1... | collective-permute-start | bytes 73736 | tf_op jit(solution)/shard_map/ppermute | solution.py:565
  7.4 10.7 %collective-permute-start.3 = (f32[3,16,128]{2,1,0:T(8,128)S(1)}, f32[3,16,128]{2,1,0:T(8,128)S(1)}, u32[]{:S(2)}, u32[]{:S(2)}) collective-permute-start(f32[3,16,128]{2,1,0:T(8,128)S(1)} %get-tuple-element.26), channel_id=1, source_target_pairs={{1,0},{2,1},{3,2},{4,3},{5,4},{6,5},{7,6},{8,7},{9,8},{10,9},{11,1... | collective-permute-start | bytes 73736 | tf_op jit(solution)/shard_map/ppermute | solution.py:565
  8.7 7.4 %collective-permute-start = (f32[3,8,128]{2,1,0:T(8,128)S(1)}, f32[3,8,128]{2,1,0:T(8,128)S(1)}, u32[]{:S(2)}, u32[]{:S(2)}) collective-permute-start(f32[3,8,128]{2,1,0:T(8,128)S(1)} %get-tuple-element.23), channel_id=1, source_target_pairs={{0,16},{16,32},{32,48},{48,64},{64,80},{80,96},{96,112},{112,128},... | collective-permute-start | bytes 36872 | tf_op jit(solution)/shard_map/ppermute | solution.py:564
  13.1 5.0 %collective-permute-start.1 = (f32[3,8,128]{2,1,0:T(8,128)S(1)}, f32[3,8,128]{2,1,0:T(8,128)S(1)}, u32[]{:S(2)}, u32[]{:S(2)}) collective-permute-start(f32[3,8,128]{2,1,0:T(8,128)S(1)} %get-tuple-element.24), channel_id=1, source_target_pairs={{16,0},{32,16},{48,32},{64,48},{80,64},{96,80},{112,96},{128,112},... | collective-permute-start | bytes 36872 | tf_op jit(solution)/shard_map/ppermute | solution.py:564
  20.3 20.4 %copy-start.1 = (s32[16,8,128]{2,1,0:T(8,128)S(1)}, s32[16,8,128]{2,1,0:T(8,128)}, u32[]{:S(2)}) copy-start(s32[16,8,128]{2,1,0:T(8,128)} %param.5) | copy-start | bytes 196612
  20.3 20.4 %copy-start.3 = (f32[16,8,128]{2,1,0:T(8,128)S(1)}, f32[16,8,128]{2,1,0:T(8,128)}, u32[]{:S(2)}) copy-start(f32[16,8,128]{2,1,0:T(8,128)} %param.4) | copy-start | bytes 196612
  20.3 20.4 %all-to-all-start = ((f32[16,80,128]{2,1,0:T(8,128)}), f32[16,80,128]{2,1,0:T(8,128)S(1)}, u32[]{:S(2)}, u32[]{:S(2)}) async-start(f32[16,80,128]{2,1,0:T(8,128)} %get-tuple-element.27), calls=%async_computation | async-start | bytes 1310720 | tf_op jit(solution)/shard_map/all_to_all | solution.py:568
  28.4 6.8 %collective-permute-start.4 = (f32[49,128]{1,0:T(8,128)S(1)}, f32[49,128]{1,0:T(8,128)S(1)}, u32[]{:S(2)}, u32[]{:S(2)}) collective-permute-start(f32[49,128]{1,0:T(8,128)S(1)} %get-tuple-element.31), channel_id=1, source_target_pairs={{0,1},{1,2},{2,3},{3,4},{4,5},{5,6},{6,7},{7,8},{8,9},{9,10},{10,1... | collective-permute-start | bytes 75272 | tf_op jit(solution)/shard_map/ppermute | solution.py:604
  31.6 6.0 %collective-permute-start.5 = (f32[49,128]{1,0:T(8,128)S(1)}, f32[49,128]{1,0:T(8,128)S(1)}, u32[]{:S(2)}, u32[]{:S(2)}) collective-permute-start(f32[49,128]{1,0:T(8,128)S(1)} %get-tuple-element.32), channel_id=1, source_target_pairs={{1,0},{2,1},{3,2},{4,3},{5,4},{6,5},{7,6},{8,7},{9,8},{10,9},{11,1... | collective-permute-start | bytes 75272 | tf_op jit(solution)/shard_map/ppermute | solution.py:605

commit v3 on v2

v3 whole, which is shorter than its diff:
```python
import functools

import jax
import jax.numpy as jnp
from jax import lax
from jax.experimental import pallas as pl
from jax.experimental.pallas import tpu as pltpu
from jax.sharding import PartitionSpec as P

ZC = 16
YC = 8
XC = 128
ROWS = ZC * YC


def f32(*shape):
    return jax.ShapeDtypeStruct(shape, jnp.float32)


def conduct_of(label, cure):
    return jnp.where(label == 1, 40.0, jnp.where(label == 2, 20.0, 0.6 + 0.8 * cure))


def store_of(label):
    return jnp.where(label == 1, 3.0 / 60.0, jnp.where(label == 2, 2.0 / 60.0, 1.0 / 60.0))


def cure_of(label, warmth, cure):
    speed = 0.3 * jnp.exp(8.0 * warmth)
    return jnp.where(label == 0, 1.0 - (1.0 - cure) * jnp.exp(-speed), cure)


def y_rows(y):
    return pl.ds(y, ZC, stride=YC)


def z_rows(z):
    return pl.ds(z * YC, YC)


def edges_kernel(
    t_in, c_in, m_in, zlo_ref, zhi_ref, ylo_ref, yhi_ref, t_ref, c_ref, m_ref, sem
):
    copies = [
        pltpu.make_async_copy(src, dst, sem.at[i])
        for i, (src, dst) in enumerate(((t_in, t_ref), (c_in, c_ref), (m_in, m_ref)))
    ]
    for copy in copies:
        copy.start()
    for copy in copies:
        copy.wait()

    def put(out, rows):
        t, c, m = t_ref[rows, :], c_ref[rows, :], m_ref[rows, :]
        out[0] = t
        out[1] = conduct_of(m, c)
        out[2] = conduct_of(m, cure_of(m, t, c))

    put(zlo_ref, z_rows(0))
    put(zhi_ref, z_rows(ZC - 1))
    put(ylo_ref, y_rows(0))
    put(yhi_ref, y_rows(YC - 1))


def spread(one_ref, out_ref, sem, count):
    copies = [pltpu.make_async_copy(one_ref, out_ref.at[d], sem.at[d]) for d in range(count)]
    for copy in copies:
        copy.start()
    for copy in copies:
        copy.wait()


def reduce_coefficients(count, store, faces, entry, co_ref):
    ground, edge = store(0), entry
    back_ground = None
    for i in range(count - 1):
        face = faces(i)
        inv = 1.0 / (ground + edge + face)
        edge_inv, face_inv = edge * inv, face * inv
        co_ref[0, i] = inv
        co_ref[1, i] = edge_inv
        co_ref[2, i] = face_inv
        more = edge_inv * ground
        back_ground = more if i == 0 else back_ground + more
        ground = store(i + 1) + face_inv * ground
        edge = edge_inv * face
    return back_ground, edge, ground


def reduce_sides(count, right, co_ref, side_ref):
    side = right(0)
    back_side = None
    for i in range(count - 1):
        side_ref[i] = side * co_ref[0, i]
        more = co_ref[1, i] * side
        back_side = more if i == 0 else back_side + more
        side = right(i + 1) + co_ref[2, i] * side
    return side, back_side


def substitute(count, before, own, co_ref, side_ref, put):
    value = own
    put(count - 1, value)
    for i in range(count - 2, -1, -1):
        value = (side_ref[i] + co_ref[1, i] * before) + co_ref[2, i] * value
        put(i, value)


def edge_lanes():
    lane = lax.broadcasted_iota(jnp.int32, (YC, XC), 1)
    return lane == 0, lane == XC - 1


ROUNDS = 7


def x_coefficients(c_ref, m_ref, x_ref):
    first_lane, last_lane = edge_lanes()
    batch = 4
    for z0 in range(0, ZC, batch):
        gs, ls, rs, stores = [], [], [], []
        for z in range(z0, z0 + batch):
            rows = z_rows(z)
            m = m_ref[rows, :]
            k, g = conduct_of(m, c_ref[rows, :]), store_of(m)
            face_left = 0.5 * (k + jnp.where(first_lane, 0.0, pltpu.roll(k, 1, 1)))
            face_right = jnp.where(last_lane, 0.5 * k, pltpu.roll(face_left, XC - 1, 1))
            x_ref[2 * ROUNDS + 1, rows, :] = face_left
            gs.append(
                g
                + jnp.where(first_lane, face_left, 0.0)
                + jnp.where(last_lane, face_right, 0.0)
            )
            ls.append(jnp.where(first_lane, 0.0, face_left))
            rs.append(jnp.where(last_lane, 0.0, face_right))
            stores.append(g)
        for level in range(ROUNDS):
            low, high = 1 << level, XC - (1 << level)
            for b in range(batch):
                rows = z_rows(z0 + b)
                ground, left, right = gs[b], ls[b], rs[b]
                inv = 1.0 / (ground + left + right)
                to_left = left * pltpu.roll(inv, low, 1)
                to_right = right * pltpu.roll(inv, high, 1)
                x_ref[2 * level, rows, :] = to_left
                x_ref[2 * level + 1, rows, :] = to_right
                gs[b] = (
                    ground
                    + to_left * pltpu.roll(ground, low, 1)
                    + to_right * pltpu.roll(ground, high, 1)
                )
                if level + 1 < ROUNDS:
                    ls[b] = to_left * pltpu.roll(left, low, 1)
                    rs[b] = to_right * pltpu.roll(right, high, 1)
        for b in range(batch):
            x_ref[2 * ROUNDS, z_rows(z0 + b), :] = stores[b] / gs[b]


def x_kernel(c_ref, m_ref, x_ref):
    x_coefficients(c_ref, m_ref, x_ref)


def z_coefficients(groups_z, c_ref, m_ref, below, above, co_ref, num_ref):
    ks = [below]
    for z in range(ZC):
        ks.append(conduct_of(m_ref[z_rows(z), :], c_ref[z_rows(z), :]))
    ks.append(above)
    faces = [0.5 * (ks[i] + ks[i + 1]) for i in range(ZC + 1)]
    numbers = reduce_coefficients(
        ZC,
        lambda i: store_of(m_ref[z_rows(i), :]),
        lambda i: faces[i + 1],
        faces[0],
        co_ref,
    )
    num_ref[0] = numbers[0]
    num_ref[1] = numbers[1]
    at_end = lax.axis_index("gz") == groups_z - 1
    num_ref[2] = numbers[2] + jnp.where(at_end, faces[ZC], 0.0)
    return faces[ZC]


def ahead_kernel(
    c_ref,
    next_c_ref,
    m_ref,
    below_ref,
    above_ref,
    x_ref,
    co1_ref,
    num1_ref,
    co2_ref,
    num2_ref,
    entry_ref,
    *,
    groups_z,
):
    x_coefficients(next_c_ref, m_ref, x_ref)
    entry_ref[...] = z_coefficients(
        groups_z, c_ref, m_ref, below_ref[1], above_ref[1], co1_ref, num1_ref
    )
    z_coefficients(groups_z, next_c_ref, m_ref, below_ref[2], above_ref[2], co2_ref, num2_ref)


def flow_rhs(t_ref, c_ref, m_ref, x_ref, zt, yt, zk, yk, outs, scratch):
    fluxz_ref, cure_ref = outs
    k_ref, g_ref, fy_ref, r_ref = scratch
    t, c, m = t_ref[...], c_ref[...], m_ref[...]
    k_ref[...] = conduct_of(m, c)
    g_ref[...] = store_of(m)
    cure_ref[...] = cure_of(m, t, c)

    ks = [yk[0]] + [k_ref[y_rows(y), :] for y in range(YC)] + [yk[1]]
    ts = [yt[0]] + [t_ref[y_rows(y), :] for y in range(YC)] + [yt[1]]
    face_y = [0.5 * (ks[i] + ks[i + 1]) for i in range(YC + 1)]
    flow_y = [face_y[i] * (ts[i + 1] - ts[i]) for i in range(YC + 1)]
    for y in range(YC):
        fy_ref[y_rows(y), :] = flow_y[y + 1] - flow_y[y]

    first_lane, last_lane = edge_lanes()
    k_prev, t_prev = zk[0], zt[0]
    flow_prev = 0.5 * (k_prev + k_ref[z_rows(0), :]) * (t_ref[z_rows(0), :] - t_prev)
    batch = 4
    for z0 in range(0, ZC, batch):
        sides = []
        for z in range(z0, z0 + batch):
            rows = z_rows(z)
            kz, tz = k_ref[rows, :], t_ref[rows, :]
            k_next = k_ref[z_rows(z + 1), :] if z + 1 < ZC else zk[1]
            t_next = t_ref[z_rows(z + 1), :] if z + 1 < ZC else zt[1]
            flow_next = 0.5 * (kz + k_next) * (t_next - tz)
            flux_z = flow_next - flow_prev
            flow_prev = flow_next
            fluxz_ref[rows, :] = flux_z
            t_left = jnp.where(first_lane, 0.0, pltpu.roll(tz, 1, 1))
            flow_left = x_ref[2 * ROUNDS + 1, rows, :] * (tz - t_left)
            flow_right = jnp.where(last_lane, -0.5 * kz * tz, pltpu.roll(flow_left, XC - 1, 1))
            delta = cure_ref[rows, :] - c_ref[rows, :]
            sides.append(
                g_ref[rows, :] * (tz + 0.4 * delta)
                + (flow_right - flow_left)
                + 2.0 * (fy_ref[rows, :] + flux_z)
            )
        for level in range(ROUNDS):
            low, high = 1 << level, XC - (1 << level)
            for b in range(batch):
                rows = z_rows(z0 + b)
                side = sides[b]
                sides[b] = (
                    side
                    + x_ref[2 * level, rows, :] * pltpu.roll(side, low, 1)
                    + x_ref[2 * level + 1, rows, :] * pltpu.roll(side, high, 1)
                )
        for b in range(batch):
            rows = z_rows(z0 + b)
            r_ref[rows, :] = x_ref[2 * ROUNDS, rows, :] * sides[b] - fy_ref[rows, :]
    return face_y


def front_kernel(
    t_ref,
    c_ref,
    m_ref,
    x_ref,
    below_ref,
    above_ref,
    south_ref,
    north_ref,
    pay_ref,
    co1_ref,
    side_ref,
    co2_ref,
    fluxz_ref,
    cure_ref,
    entry_ref,
    toward_south_ref,
    toward_north_ref,
    k_ref,
    g_ref,
    fy_ref,
    r_ref,
    p_ref,
    sem,
    *,
    groups,
):
    face_y = flow_rhs(
        t_ref,
        c_ref,
        m_ref,
        x_ref,
        (below_ref[0], above_ref[0]),
        (south_ref[0], north_ref[0]),
        (below_ref[1], above_ref[1]),
        (south_ref[1], north_ref[1]),
        (fluxz_ref, cure_ref),
        (k_ref, g_ref, fy_ref, r_ref),
    )
    entry_ref[...] = face_y[YC]
    at_end = lax.axis_index("gy") == groups - 1
    back_ground, edge, ground = reduce_coefficients(
        YC, lambda i: g_ref[y_rows(i), :], lambda i: face_y[i + 1], face_y[0], co1_ref
    )
    ground = ground + jnp.where(at_end, face_y[YC], 0.0)
    side, back_side = reduce_sides(YC, lambda i: r_ref[y_rows(i), :], co1_ref, side_ref)
    for out, y in ((toward_south_ref, 0), (toward_north_ref, YC - 1)):
        k = k_ref[y_rows(y), :]
        out[0:16] = fluxz_ref[y_rows(y), :]
        out[16:32] = g_ref[y_rows(y), :]
        fy_ref[8:24, :] = k
        fy_ref[7:8, :] = below_ref[1, y : y + 1, :]
        fy_ref[24:25, :] = above_ref[1, y : y + 1, :]
        out[32:48] = 0.5 * (fy_ref[7:23, :] + k)
        out[48:49] = 0.5 * (fy_ref[23:24, :] + fy_ref[24:25, :])
    k_ref[...] = conduct_of(m_ref[...], cure_ref[...])
    ks = [south_ref[2]] + [k_ref[y_rows(y), :] for y in range(YC)] + [north_ref[2]]
    faces = [0.5 * (ks[i] + ks[i + 1]) for i in range(YC + 1)]
    back_ground2, edge2, ground2 = reduce_coefficients(
        YC, lambda i: g_ref[y_rows(i), :], lambda i: faces[i + 1], faces[0], co2_ref
    )
    ground2 = ground2 + jnp.where(at_end, faces[YC], 0.0)
    numbers = (back_ground, edge, ground, side, back_side, back_ground2, edge2, ground2)
    for q, number in enumerate(numbers):
        p_ref[ZC * q : ZC * q + ZC] = number
    spread(p_ref, pay_ref, sem, groups)


def chain(count, read, put):
    def ground_of(j):
        return read(j, 2) + read(j + 1, 0) if j + 1 < count else read(j, 2)

    def side_of(j):
        return read(j, 3) + read(j + 1, 4) if j + 1 < count else read(j, 3)

    half = count // 2
    gain, part = [None] * count, [None] * count
    ground_l, side_l = ground_of(0) + read(0, 1), side_of(0)
    ground_r, side_r = ground_of(count - 1), side_of(count - 1)
    for i in range(half - 1):
        edge = read(i + 1, 1)
        inv = 1.0 / (ground_l + edge)
        gain[i], part[i] = edge * inv, side_l * inv
        ground_l = ground_of(i + 1) + gain[i] * ground_l
        side_l = side_of(i + 1) + gain[i] * side_l
        j = count - 1 - i
        edge = read(j, 1)
        inv = 1.0 / (ground_r + edge)
        gain[j], part[j] = edge * inv, side_r * inv
        ground_r = ground_of(j - 1) + gain[j] * ground_r
        side_r = side_of(j - 1) + gain[j] * side_r
    edge = read(half, 1)
    inv = 1.0 / (ground_l * ground_r + edge * (ground_l + ground_r))
    low = (side_l * (ground_r + edge) + edge * side_r) * inv
    high = (side_r * (ground_l + edge) + edge * side_l) * inv
    put(half - 1, low)
    put(half, high)
    for i in range(half - 2, -1, -1):
        low = part[i] + gain[i] * low
        put(i, low)
        j = count - 1 - i
        high = part[j] + gain[j] * high
        put(j, high)


def first_of_next(own, after, back_ground, edge, back_side, entry):
    return own - (back_ground * own + edge * (own - after) - back_side) / entry


def y_solution(groups_y, read, co_ref, side_ref, s_ref, v_ref):
    s_ref[0] = jnp.zeros((ZC, XC), jnp.float32)

    def put(j, value):
        s_ref[j + 1] = value

    chain(groups_y, read, put)
    me = lax.axis_index("gy")

    def place(i, value):
        v_ref[y_rows(i), :] = value

    before, own = s_ref[me], s_ref[me + 1]
    substitute(YC, before, own, co_ref, side_ref, place)
    return before, own


def main_rows(q):
    return pl.ds(YC * q, YC)


def later_rows(q):
    return pl.ds(YC * (5 + q), YC)


def wide_rows(q):
    return pl.ds(8 * YC + 2 * q, 2)


SHARED = 8 * YC + 16


def middle_kernel(
    all_ref,
    co_y_ref,
    side_y_ref,
    fluxz_ref,
    m_ref,
    co_z_ref,
    num1_ref,
    num2_ref,
    y_entry_ref,
    of_south_ref,
    of_north_ref,
    p_ref,
    side_z_ref,
    co_wide_ref,
    side_wide_ref,
    s_ref,
    v_ref,
    h_ref,
    *,
    groups_y,
    groups_z,
):
    def read(j, q):
        return all_ref[j, ZC * q : ZC * q + ZC, :]

    before, own = y_solution(groups_y, read, co_y_ref, side_y_ref, s_ref, v_ref)

    def right(i):
        return store_of(m_ref[z_rows(i), :]) * v_ref[z_rows(i), :] - fluxz_ref[z_rows(i), :]

    for q in range(3):
        p_ref[main_rows(q), :] = num1_ref[q]
        p_ref[later_rows(q), :] = num2_ref[q]
    sides = reduce_sides(ZC, right, co_z_ref, side_z_ref)
    p_ref[main_rows(3), :] = sides[0]
    p_ref[main_rows(4), :] = sides[1]

    me = lax.axis_index("gy")
    then = jnp.minimum(me + 1, groups_y - 1)
    north = first_of_next(
        own,
        s_ref[then + 1],
        all_ref[then, 0:16, :],
        all_ref[then, 16:32, :],
        all_ref[then, 64:80, :],
        y_entry_ref[...],
    )
    for side, value, of_ref in ((0, before, of_south_ref), (1, north, of_north_ref)):
        capacity = of_ref[16:32]
        rows = pl.ds(side, ZC, stride=2)
        h_ref[0, rows, :] = jnp.where(capacity > 0.0, capacity, 1.0)
        h_ref[1, rows, :] = capacity * value - of_ref[0:16]
        h_ref[2, rows, :] = of_ref[32:48]
        h_ref[2, 32 + side : 33 + side, :] = of_ref[48:49]
    numbers = reduce_coefficients(
        ZC,
        lambda i: h_ref[0, 2 * i : 2 * i + 2, :],
        lambda i: h_ref[2, 2 * i + 2 : 2 * i + 4, :],
        h_ref[2, 0:2, :],
        co_wide_ref,
    )
    sides = reduce_sides(
        ZC, lambda i: h_ref[1, 2 * i : 2 * i + 2, :], co_wide_ref, side_wide_ref
    )
    at_end = lax.axis_index("gz") == groups_z - 1
    p_ref[8 * YC + 8 :, :] = jnp.zeros((8, XC), jnp.float32)
    p_ref[wide_rows(0), :] = numbers[0]
    p_ref[wide_rows(1), :] = numbers[1]
    p_ref[wide_rows(2), :] = numbers[2] + jnp.where(at_end, h_ref[2, 32:34, :], 0.0)
    p_ref[wide_rows(3), :] = sides[0]
    p_ref[wide_rows(4), :] = sides[1]


def later_middle_kernel(
    all_ref,
    more_ref,
    co_y_ref,
    side_y_ref,
    fluxz_ref,
    m_ref,
    co_z_ref,
    p_ref,
    side_z_ref,
    s_ref,
    v_ref,
    *,
    groups_y,
):
    def read(j, q):
        if q < 3:
            return all_ref[j, ZC * (5 + q) : ZC * (6 + q), :]
        return more_ref[j, ZC * (q - 3) : ZC * (q - 2), :]

    y_solution(groups_y, read, co_y_ref, side_y_ref, s_ref, v_ref)

    def right(i):
        return store_of(m_ref[z_rows(i), :]) * v_ref[z_rows(i), :] - fluxz_ref[z_rows(i), :]

    sides = reduce_sides(ZC, right, co_z_ref, side_z_ref)
    p_ref[0:YC] = sides[0]
    p_ref[YC : 2 * YC] = sides[1]


HALF = YC // 2
WIDTH = HALF + 1


def node_between(low, high):
    ground = low[2] + high[0]
    return ground, 1.0 / (ground + low[1] + high[1])


def merged_coefficients(low, high):
    ground, inv = node_between(low, high)
    low_inv, high_inv = low[1] * inv, high[1] * inv
    return low[0] + low_inv * ground, low_inv * high[1], high[2] + high_inv * ground


def merged_sides(low, high):
    _, inv = node_between(low, high)
    side = low[3] + high[4]
    return high[3] + high[1] * inv * side, low[4] + low[1] * inv * side


def first_numbers(pair_ref, rows):
    return [[pair_ref[core, rows(q), :] for q in range(5)] for core in range(2)]


def later_numbers(pair_ref, more_ref):
    return [
        [pair_ref[core, later_rows(q), :] for q in range(3)]
        + [more_ref[core, main_rows(q), :] for q in range(2)]
        for core in range(2)
    ]


def my_half(number):
    half = number.shape[0] // 2
    core = lax.rem(lax.axis_index("gz"), 2)
    return jnp.where(core == 0, number[:half], number[half:])


def merge_kernel(pair_ref, pay_ref, p_ref, sem, *, copies):
    p_ref[32:40] = jnp.zeros((8, XC), jnp.float32)
    low, high = first_numbers(pair_ref, main_rows)
    for q, number in enumerate(merged_coefficients(low, high) + merged_sides(low, high)):
        p_ref[WIDTH * q : WIDTH * q + HALF] = my_half(number)
    low, high = first_numbers(pair_ref, wide_rows)
    for q, number in enumerate(merged_coefficients(low, high) + merged_sides(low, high)):
        p_ref[WIDTH * q + HALF : WIDTH * q + WIDTH] = my_half(number)
    low, high = ([pair_ref[core, later_rows(q), :] for q in range(3)] for core in range(2))
    for q, number in enumerate(merged_coefficients(low, high)):
        row = 5 * WIDTH + HALF * q
        p_ref[row : row + HALF] = my_half(number)
    spread(p_ref, pay_ref, sem, copies)


def later_merge_kernel(pair_ref, more_ref, pay_ref, p_ref, sem, *, copies):
    low, high = later_numbers(pair_ref, more_ref)
    for q, number in enumerate(merged_sides(low, high)):
        p_ref[HALF * q : HALF * q + HALF] = my_half(number)
    spread(p_ref, pay_ref, sem, copies)


def chain_kernel(all_ref, out_ref, s_ref, *, chips):
    s_ref[0] = jnp.zeros((WIDTH, XC), jnp.float32)

    def put(j, value):
        s_ref[j + 1] = value

    chain(chips, lambda j, q: all_ref[j, WIDTH * q : WIDTH * q + WIDTH, :], put)
    me = lax.div(lax.axis_index("gz"), 2)
    then = jnp.minimum(me + 1, chips - 1)
    own, after = s_ref[me + 1], s_ref[then + 1]
    numbers = [all_ref[then, WIDTH * q : WIDTH * q + WIDTH, :] for q in (0, 1, 4)]
    out_ref[8:16] = jnp.zeros((8, XC), jnp.float32)
    out_ref[0:WIDTH] = s_ref[me]
    out_ref[WIDTH : 2 * WIDTH] = own
    out_ref[2 * WIDTH : 3 * WIDTH] = numbers[0] * own + numbers[1] * (own - after) - numbers[2]


def later_chain_kernel(all_ref, more_ref, out_ref, s_ref, *, chips):
    s_ref[0] = jnp.zeros((HALF, XC), jnp.float32)

    def put(j, value):
        s_ref[j + 1] = value

    def read(j, q):
        if q < 3:
            return all_ref[j, 5 * WIDTH + HALF * q : 5 * WIDTH + HALF * (q + 1), :]
        return more_ref[j, HALF * (q - 3) : HALF * (q - 2), :]

    chain(chips, read, put)
    me = lax.div(lax.axis_index("gz"), 2)
    out_ref[0:HALF] = s_ref[me]
    out_ref[HALF : 2 * HALF] = s_ref[me + 1]


def ends_of(low, high, before, last):
    _, inv = node_between(low, high)
    node = (low[3] + high[4] + low[1] * before + high[1] * last) * inv
    upper = lax.rem(lax.axis_index("gz"), 2) == 1
    return jnp.where(upper, node, before), jnp.where(upper, last, node), node


def joined(res_ref, u_ref, width, count):
    for q in range(count):
        for core in range(2):
            rows = pl.ds(HALF * core, HALF)
            u_ref[q, rows, :] = res_ref[core, width * q : width * q + HALF, :]


def back_kernel(pair_ref, more_ref, res_ref, co_z_ref, side_z_ref, t_ref, u_ref):
    joined(res_ref, u_ref, HALF, 2)
    low, high = later_numbers(pair_ref, more_ref)
    before, own, _ = ends_of(low, high, u_ref[0], u_ref[1])

    def place(i, value):
        t_ref[z_rows(i), :] = value

    substitute(ZC, before, own, co_z_ref, side_z_ref, place)


def turn_kernel(
    pair_ref,
    res_ref,
    co_z_ref,
    side_z_ref,
    co_wide_ref,
    side_wide_ref,
    z_entry_ref,
    c_ref,
    m_ref,
    x_ref,
    co_y_ref,
    below_ref,
    above_ref,
    south_ref,
    north_ref,
    pay_ref,
    side_y_ref,
    fluxz_ref,
    cure_ref,
    u_ref,
    w_ref,
    t_ref,
    e_ref,
    k_ref,
    g_ref,
    fy_ref,
    r_ref,
    p_ref,
    sem,
    *,
    groups_y,
    groups_z,
):
    joined(res_ref, u_ref, WIDTH, 3)
    low, high = first_numbers(pair_ref, main_rows)
    last = u_ref[1]
    before, own, node = ends_of(low, high, u_ref[0], last)

    def place(i, value):
        t_ref[z_rows(i), :] = value

    substitute(ZC, before, own, co_z_ref, side_z_ref, place)
    me = lax.axis_index("gz")
    inside = high[0] * node + high[1] * (node - last) - high[4]
    current = jnp.where(lax.rem(me, 2) == 1, u_ref[2], inside)
    above = jnp.where(me == groups_z - 1, 0.0, own - current / z_entry_ref[...])

    for q in range(2):
        for core in range(2):
            row = WIDTH * q + HALF
            w_ref[q, core : core + 1] = res_ref[core, row : row + 1, :]
    low, high = first_numbers(pair_ref, wide_rows)
    before_wide, own_wide, _ = ends_of(low, high, w_ref[0], w_ref[1])

    def place_wide(i, value):
        e_ref[2 * i : 2 * i + 2] = value

    substitute(ZC, before_wide, own_wide, co_wide_ref, side_wide_ref, place_wide)
    row = lax.axis_index("gy")
    south = jnp.where(row == 0, 0.0, e_ref[pl.ds(0, ZC, stride=2), :])
    north = jnp.where(row == groups_y - 1, 0.0, e_ref[pl.ds(1, ZC, stride=2), :])
    flow_rhs(
        t_ref,
        c_ref,
        m_ref,
        x_ref,
        (before, above),
        (south, north),
        (below_ref[2], above_ref[2]),
        (south_ref[2], north_ref[2]),
        (fluxz_ref, cure_ref),
        (k_ref, g_ref, fy_ref, r_ref),
    )
    side, back_side = reduce_sides(YC, lambda i: r_ref[y_rows(i), :], co_y_ref, side_y_ref)
    p_ref[0:ZC] = side
    p_ref[ZC : 2 * ZC] = back_side
    spread(p_ref, pay_ref, sem, groups_y)


def call(kernel, outs, scratch=(), spread_to=0, **static):
    out_specs = [pl.BlockSpec(memory_space=pltpu.VMEM)] * len(outs)
    shapes = [pltpu.VMEM(shape, jnp.float32) for shape in scratch]
    if spread_to:
        out_specs[0] = pl.BlockSpec(memory_space=pl.ANY)
        shapes.append(pltpu.SemaphoreType.DMA((spread_to,)))
    return pl.pallas_call(
        functools.partial(kernel, **static),
        out_shape=tuple(outs),
        out_specs=tuple(out_specs),
        scratch_shapes=shapes,
        compiler_params=pltpu.CompilerParams(vmem_limit_bytes=12 * 1024 * 1024),
        name=kernel.__name__,
    )


def body(warmth, cure, label):
    groups_z, groups_y = lax.axis_size("gz"), lax.axis_size("gy")
    chips = groups_z // 2
    up = {a: [(i, i + 1) for i in range(n - 1)] for a, n in (("gz", groups_z), ("gy", groups_y))}
    down = {a: [(j, i) for i, j in up[a]] for a in up}
    pairs = [[2 * i, 2 * i + 1] for i in range(chips)]
    same_core = [[2 * i + core for i in range(chips)] for core in range(2)]
    cells = (ROWS, XC)
    block = f32(*cells)

    zlo, zhi, ylo, yhi, t, c, m = pl.pallas_call(
        edges_kernel,
        out_shape=(
            f32(3, YC, XC),
            f32(3, YC, XC),
            f32(3, ZC, XC),
            f32(3, ZC, XC),
            block,
            block,
            jax.ShapeDtypeStruct(cells, jnp.int32),
        ),
        in_specs=[pl.BlockSpec(memory_space=pltpu.HBM)] * 3,
        scratch_shapes=[pltpu.SemaphoreType.DMA((3,))],
        compiler_params=pltpu.CompilerParams(vmem_limit_bytes=12 * 1024 * 1024),
        name="edges_kernel",
    )(*(pltpu.with_memory_space_constraint(a.reshape(cells), pltpu.HBM) for a in (warmth, cure, label)))
    z_halo = (lax.ppermute(zhi, "gz", up["gz"]), lax.ppermute(zlo, "gz", down["gz"]))
    y_halo = (lax.ppermute(yhi, "gy", up["gy"]), lax.ppermute(ylo, "gy", down["gy"]))

    def gather_y(pay):
        return lax.all_to_all(pay, "gy", 0, 0, tiled=True)

    def gather_z(pay):
        return lax.all_to_all(pay, "gz", 0, 0, tiled=True, axis_index_groups=same_core)

    def share(numbers):
        return lax.all_gather(numbers, "gz", axis_index_groups=pairs)

    sizes = dict(groups_y=groups_y, groups_z=groups_z)
    co_y, side_y = f32(3, YC - 1, ZC, XC), f32(YC - 1, ZC, XC)
    co_z, side_z, num_z = f32(3, ZC - 1, YC, XC), f32(ZC - 1, YC, XC), f32(3, YC, XC)
    x_shape = f32(2 * ROUNDS + 2, ROWS, XC)
    line = (groups_y + 1, ZC, XC)
    message = f32(3 * ZC + 1, XC)

    (x1,) = call(x_kernel, [x_shape])(c, m)
    pay, co_y1, side, co_y2, fluxz, c1, y_entry, toward_south, toward_north = call(
        front_kernel,
        [f32(groups_y, 8 * ZC, XC), co_y, side_y, co_y, block, block, f32(ZC, XC), message, message],
        [cells] * 4 + [(8 * ZC, XC)],
        spread_to=groups_y,
        groups=groups_y,
    )(t, c, m, x1, *z_halo, *y_halo)
    of_south = lax.ppermute(toward_north, "gy", up["gy"])
    of_north = lax.ppermute(toward_south, "gy", down["gy"])
    x2, co_z1, num_z1, co_z2, num_z2, z_entry = call(
        ahead_kernel,
        [x_shape, co_z, num_z, co_z, num_z, f32(YC, XC)],
        groups_z=groups_z,
    )(c, c1, m, *z_halo)
    everyone = gather_y(pay)
    numbers, side, co_wide, side_wide = call(
        middle_kernel,
        [f32(SHARED, XC), side_z, f32(3, ZC - 1, 2, XC), f32(ZC - 1, 2, XC)],
        [line, cells, (3, 2 * ZC + 2, XC)],
        **sizes,
    )(everyone, co_y1, side, fluxz, m, co_z1, num_z1, num_z2, y_entry, of_south, of_north)
    pair = share(numbers)
    (pay,) = call(
        merge_kernel, [f32(chips, 40, XC)], [(40, XC)], spread_to=chips, copies=chips
    )(pair)
    column = gather_z(pay)
    (found,) = call(chain_kernel, [f32(16, XC)], [(chips + 1, WIDTH, XC)], chips=chips)(column)
    pay, side, fluxz, c2 = call(
        turn_kernel,
        [f32(groups_y, 2 * ZC, XC), side_y, block, block],
        [(3, YC, XC), (2, 2, XC), cells, (2 * ZC, XC)] + [cells] * 4 + [(2 * ZC, XC)],
        spread_to=groups_y,
        **sizes,
    )(
        pair,
        share(found),
        co_z1,
        side,
        co_wide,
        side_wide,
        z_entry,
        c1,
        m,
        x2,
        co_y2,
        *z_halo,
        *y_halo,
    )
    numbers, side = call(
        later_middle_kernel, [f32(2 * YC, XC), side_z], [line, cells], groups_y=groups_y
    )(everyone, gather_y(pay), co_y2, side, fluxz, m, co_z2)
    more = share(numbers)
    (pay,) = call(
        later_merge_kernel, [f32(chips, YC, XC)], [(YC, XC)], spread_to=chips, copies=chips
    )(pair, more)
    (found,) = call(
        later_chain_kernel, [f32(YC, XC)], [(chips + 1, HALF, XC)], chips=chips
    )(column, gather_z(pay))
    (t2,) = call(back_kernel, [block], [(2, YC, XC)])(pair, more, share(found), co_z2, side)
    return t2.reshape(warmth.shape), c2.reshape(cure.shape)


def solution(mesh):
    return jax.shard_map(
        body,
        mesh=mesh,
        in_specs=(P("gz", "gy", None),) * 3,
        out_specs=(P("gz", "gy", None),) * 2,
        check_vma=False,
    )
```

time: 127 us -> 125 us (0.984)
  blocking collectives: 80.5 us -> 77.6 us
  local copies, waits for them, and re-layouts: 2.53 us -> 0 us
  waiting for transfers between devices: 9.72 us -> 11.7 us
  Pallas kernels: 7.97 us -> 9.41 us
    all_to_all x1, blocking collectives: 16.5 us -> 11.2 us  [gather_y(): return lax.all_to_all(pay, 'gy', 0, 0, tiled=True)]
    ppermute x1, waiting for transfers between devices: 2.22 us -> 5.32 us  [body(): of_south = lax.ppermute(toward_north, 'gy', up['gy'])]
    unnamed x10 -> x0, local copies, waits for them, and re-layouts: 2.53 us -> none
    all_to_all x2, blocking collectives: 47.9 us -> 49.9 us  [gather_z(): lax.all_to_all(pay, 'gz', 0, 0, tiled=True, axis_index_groups=same_core)]
    pallas_call x9 -> x11, Pallas kernels: 7.69 us -> 8.45 us  [the longest x1 2.06 us: body(): call(turn_kernel, [f32(groups_y, 2 * ZC, XC), side_y, block, block], [(3,...]
  transfers between devices with their start and end apart: 7 -> 7, of which waited for: 4 -> 4; matrix products, arithmetic and copies ran while one was open for 0% -> 0% of each run, Pallas kernels for 0% -> 2%
where the time goes in v3:
time: 125 us
  blocking collectives  77.6 us (62%)
  starting transfers between devices  25.1 us (20%)
  waiting for transfers between devices  11.7 us (9%)
  Pallas kernels  9.41 us (8%)
    all_to_all x2, blocking collectives, gather_z(): lax.all_to_all(pay, 'gz', 0, 0, tiled=True, axis_index_groups=same_core)  49.9 us
    all_gather x4, blocking collectives, share(): return lax.all_gather(numbers, 'gz', axis_index_groups=pairs)  16.5 us
    all_to_all x1, blocking collectives, gather_y(): return lax.all_to_all(pay, 'gy', 0, 0, tiled=True)  11.2 us
    all_to_all x1, starting transfers between devices, gather_y(): return lax.all_to_all(pay, 'gy', 0, 0, tiled=True)  7.92 us
    ppermute x1, waiting for transfers between devices, body(): of_south = lax.ppermute(toward_north, 'gy', up['gy'])  5.32 us
    ppermute x1, starting transfers between devices, body(): lax.ppermute(zhi, 'gz', up['gz'])  4.39 us
    ppermute x1, starting transfers between devices, body(): lax.ppermute(yhi, 'gy', up['gy'])  3.95 us
    ppermute x1, starting transfers between devices, body(): of_south = lax.ppermute(toward_north, 'gy', up['gy'])  3.26 us
  transfers between devices with their start and end apart: 7, of which 4 were waited for; matrix products, arithmetic and copies ran while one was open for 0% of the time, Pallas kernels for 2%

profile of v3, /device:TPU:1, one launch (start us, length us, event | category | flops | bytes accessed | tf_op | source)
XLA Modules:
  0.0 124.7 jit_solution(8667063036953867325)
XLA Ops:
  0.6 1.0 edges_kernel.1
  1.6 3.9 %collective-permute-start.2 = (f32[3,16,128]{2,1,0:T(8,128)S(1)}, f32[3,16,128]{2,1,0:T(8,128)S(1)}, u32[]{:S(2)}, u32[]{:S(2)}) collective-permute-start(f32[3,16,128]{2,1,0:T(8,128)S(1)} %get-tuple-element.39), channel_id=1, source_target_pairs={{0,1},{1,2},{2,3},{3,4},{4,5},{5,6},{6,7},{7,8},{8,9},{9,10},{10,1... | collective-permute-start | bytes 73736 | tf_op jit(solution)/shard_map/ppermute | solution.py:748
  5.6 1.3 %collective-permute-start.3 = (f32[3,16,128]{2,1,0:T(8,128)S(1)}, f32[3,16,128]{2,1,0:T(8,128)S(1)}, u32[]{:S(2)}, u32[]{:S(2)}) collective-permute-start(f32[3,16,128]{2,1,0:T(8,128)S(1)} %get-tuple-element.40), channel_id=1, source_target_pairs={{1,0},{2,1},{3,2},{4,3},{5,4},{6,5},{7,6},{8,7},{9,8},{10,9},{11,1... | collective-permute-start | bytes 73736 | tf_op jit(solution)/shard_map/ppermute | solution.py:748
  6.9 4.4 %collective-permute-start = (f32[3,8,128]{2,1,0:T(8,128)S(1)}, f32[3,8,128]{2,1,0:T(8,128)S(1)}, u32[]{:S(2)}, u32[]{:S(2)}) collective-permute-start(f32[3,8,128]{2,1,0:T(8,128)S(1)} %get-tuple-element.37), channel_id=1, source_target_pairs={{0,16},{16,32},{32,48},{48,64},{64,80},{80,96},{96,112},{112,128},... | collective-permute-start | bytes 36872 | tf_op jit(solution)/shard_map/ppermute | solution.py:747
  11.3 3.0 %collective-permute-start.1 = (f32[3,8,128]{2,1,0:T(8,128)S(1)}, f32[3,8,128]{2,1,0:T(8,128)S(1)}, u32[]{:S(2)}, u32[]{:S(2)}) collective-permute-start(f32[3,8,128]{2,1,0:T(8,128)S(1)} %get-tuple-element.38), channel_id=1, source_target_pairs={{16,0},{32,16},{48,32},{64,48},{80,64},{96,80},{112,96},{128,112},... | collective-permute-start | bytes 36872 | tf_op jit(solution)/shard_map/ppermute | solution.py:747
  14.3 1.1 x_kernel.1.x_ref
  15.4 0.0 collective-permute-done.below_ref
  15.4 0.8 collective-permute-done.1.above_ref
  16.3 0.0 collective-permute-done.2.south_ref
  16.3 0.0 collective-permute-done.3.north_ref
  16.3 2.0 %front_kernel.1 = (f32[16,128,128]{2,1,0:T(8,128)}, f32[3,7,16,128]{3,2,1,0:T(8,128)S(1)}, f32[7,16,128]{2,1,0:T(8,128)S(1)}, f32[3,7,16,128]{3,2,1,0:T(8,128)S(...) custom-call(f32[128,128]{1,0:T(8,128)S(1)} %get-tuple-element.34.t_r, ...), custom_call_target="tpu_custom_call" | custom-call | tf_op jit(solution)/shard_map/front_kernel/pallas_call | solution.py:767
  18.2 7.9 %all-to-all-start = ((f32[16,128,128]{2,1,0:T(8,128)}), f32[16,128,128]{2,1,0:T(8,128)S(1)}, u32[]{:S(2)}, u32[]{:S(2)}) async-start(f32[16,128,128]{2,1,0:T(8,128)} %get-tuple-element.41), calls=%async_computation | async-start | bytes 2097152 | tf_op jit(solution)/shard_map/all_to_all | solution.py:751
  26.2 3.3 %collective-permute-start.4 = (f32[49,128]{1,0:T(8,128)S(1)}, f32[49,128]{1,0:T(8,128)S(1)}, u32[]{:S(2)}, u32[]{:S(2)}) collective-permute-start(f32[49,128]{1,0:T(8,128)S(1)} %get-tuple-element.50), channel_id=1, source_target_pairs={{0,1},{1,2},{2,3},{3,4},{4,5},{5,6},{6,7},{7,8},{8,9},{9,10},{10,1... | collective-permute-start | bytes 75272 | tf_op jit(solution)/shard_map/ppermute | solution.py:774
  29.4 1.3 %collective-permute-start.5 = (f32[49,128]{1,0:T(8,128)S(1)}, f32[49,128]{1,0:T(8,128)S(1)}, u32[]{:S(2)}, u32[]{:S(2)}) collective-permute-start(f32[49,128]{1,0:T(8,128)S(1)} %get-tuple-element.51), channel_id=1, source_target_pairs={{1,0},{2,1},{3,2},{4,3},{5,4},{6,5},{7,6},{8,7},{9,8},{10,9},{11,1... | collective-permute-start | bytes 75272 | tf_op jit(solution)/shard_map/ppermute | solution.py:775
  30.7 1.2 ahead_kernel.1
  31.9 5.3 %collective-permute-done.4.of_south_ref = f32[49,128]{1,0:T(8,128)S(1)} collective-permute-done((f32[49,128]{1,0:T(8,128)S(1)}, f32[49,128]{1,0:T(8,128)S(1)}, u32[]{:S(2)}, u32[]{:S(2)}) %collective-permute-start.4) | collective-permute-done | bytes 25120 | tf_op jit(solution)/shard_map/ppermute | solution.py:774
  37.2 2.5 %collective-permute-done.5.of_north_ref = f32[49,128]{1,0:T(8,128)S(1)} collective-permute-done((f32[49,128]{1,0:T(8,128)S(1)}, f32[49,128]{1,0:T(8,128)S(1)}, u32[]{:S(2)}, u32[]{:S(2)}) %collective-permute-start.5) | collective-permute-done | bytes 25120 | tf_op jit(solution)/shard_map/ppermute | solution.py:775
  39.7 3.1 %all-to-all-done.all_ref = f32[16,128,128]{2,1,0:T(8,128)S(1)} async-done(((f32[16,128,128]{2,1,0:T(8,128)}), f32[16,128,128]{2,1,0:T(8,128)S(1)}, u32[]{:S(2)}, u32[]{:S(2)}) %all-to-all-start) | async-done | bytes 1048608 | tf_op jit(solution)/shard_map/all_to_all | solution.py:751
  42.8 0.2 middle_kernel.1
  43.0 1.9 %all-gather = f32[160,128]{1,0:T(8,128)S(1)} all-gather(f32[80,128]{1,0:T(8,128)S(1)} %get-tuple-element.52), channel_id=2, replica_groups={{0,16},{32,48},{64,80},{96,112},{128,144},{160,176},{192,208},{224,240}..., dimensions={0}, use_global_device_ids=true | all-gather | bytes 122880 | tf_op jit(solution)/shard_map/all_gather | solution.py:757
  44.9 0.6 merge_kernel.1
  45.5 32.9 %all_to_all.20.all_ref = f32[16,40,128]{2,1,0:T(8,128)S(1)} all-to-all(f32[16,40,128]{2,1,0:T(8,128)S(1)} %merge_kernel.1), channel_id=1, replica_groups={{0,32,64,96,128,160,192,224,256,288,320,352,384,416,448,480},{16,48,80,..., dimensions={0} | all-to-all | bytes 655360 | tf_op jit(solution)/shard_map/all_to_all | solution.py:754
  78.4 0.1 chain_kernel.1
  78.5 8.1 %all-gather.1 = f32[32,128]{1,0:T(8,128)S(1)} all-gather(f32[16,128]{1,0:T(8,128)S(1)} %chain_kernel.1), channel_id=3, replica_groups={{0,16},{32,48},{64,80},{96,112},{128,144},{160,176},{192,208},{224,240}..., dimensions={0}, use_global_device_ids=true | all-gather | bytes 24576 | tf_op jit(solution)/shard_map/all_gather | solution.py:757
  86.6 2.1 %turn_kernel.1 = (f32[16,32,128]{2,1,0:T(8,128)S(1)}, f32[7,16,128]{2,1,0:T(8,128)S(1)}, f32[128,128]{1,0:T(8,128)S(1)}, f32[128,128]{1,0:T(8,128)}) custom-call(f32[2,80,128]{2,1,0:T(8,128)S(1)} %bitcast.10, f32[2,16,128]{2,1,0:T(8,128)S(1)} %bitcast.15, f32[3,15,8,128]{3,2,1,0:T(8,128)S(1)} %get-tuple-element.46.co_z_ref, ...), custom_call_target="tpu_custom_call" | custom-call | tf_op jit(solution)/shard_map/turn_kernel/pallas_call | solution.py:794
  88.7 11.2 %all_to_all.21.more_ref = f32[16,32,128]{2,1,0:T(8,128)S(1)} all-to-all(f32[16,32,128]{2,1,0:T(8,128)S(1)} %get-tuple-element.59), channel_id=1, replica_groups=mesh['gz'=32,'gy'=16] {'gy'}, dimensions={0} | all-to-all | bytes 524288 | tf_op jit(solution)/shard_map/all_to_all | solution.py:751
  99.9 0.2 later_middle_kernel.1
  100.1 3.0 %all-gather.2 = f32[32,128]{1,0:T(8,128)S(1)} all-gather(f32[16,128]{1,0:T(8,128)S(1)} %get-tuple-element.63), channel_id=4, replica_groups={{0,16},{32,48},{64,80},{96,112},{128,144},{160,176},{192,208},{224,240}..., dimensions={0}, use_global_device_ids=true | all-gather | bytes 24576 | tf_op jit(solution)/shard_map/all_gather | solution.py:757
  103.0 0.3 later_merge_kernel.1
  103.3 17.0 %all_to_all.22.more_ref = f32[16,8,128]{2,1,0:T(8,128)S(1)} all-to-all(f32[16,8,128]{2,1,0:T(8,128)S(1)} %later_merge_kernel.1), channel_id=1, replica_groups={{0,32,64,96,128,160,192,224,256,288,320,352,384,416,448,480},{16,48,80,..., dimensions={0} | all-to-all | bytes 131072 | tf_op jit(solution)/shard_map/all_to_all | solution.py:754
  120.3 0.1 later_chain_kernel.1
  120.4 3.6 %all-gather.3 = f32[16,128]{1,0:T(8,128)S(1)} all-gather(f32[8,128]{1,0:T(8,128)S(1)} %later_chain_kernel.1), channel_id=5, replica_groups={{0,16},{32,48},{64,80},{96,112},{128,144},{160,176},{192,208},{224,240}..., dimensions={0}, use_global_device_ids=true | all-gather | bytes 12288 | tf_op jit(solution)/shard_map/all_gather | solution.py:757
  124.0 0.7 back_kernel.1
Async XLA Ops:
  1.6 14.7 %collective-permute-start.2 = (f32[3,16,128]{2,1,0:T(8,128)S(1)}, f32[3,16,128]{2,1,0:T(8,128)S(1)}, u32[]{:S(2)}, u32[]{:S(2)}) collective-permute-start(f32[3,16,128]{2,1,0:T(8,128)S(1)} %get-tuple-element.39), channel_id=1, source_target_pairs={{0,1},{1,2},{2,3},{3,4},{4,5},{5,6},{6,7},{7,8},{8,9},{9,10},{10,1... | collective-permute-start | bytes 73736 | tf_op jit(solution)/shard_map/ppermute | solution.py:748
  5.6 10.7 %collective-permute-start.3 = (f32[3,16,128]{2,1,0:T(8,128)S(1)}, f32[3,16,128]{2,1,0:T(8,128)S(1)}, u32[]{:S(2)}, u32[]{:S(2)}) collective-permute-start(f32[3,16,128]{2,1,0:T(8,128)S(1)} %get-tuple-element.40), channel_id=1, source_target_pairs={{1,0},{2,1},{3,2},{4,3},{5,4},{6,5},{7,6},{8,7},{9,8},{10,9},{11,1... | collective-permute-start | bytes 73736 | tf_op jit(solution)/shard_map/ppermute | solution.py:748
  6.9 8.6 %collective-permute-start = (f32[3,8,128]{2,1,0:T(8,128)S(1)}, f32[3,8,128]{2,1,0:T(8,128)S(1)}, u32[]{:S(2)}, u32[]{:S(2)}) collective-permute-start(f32[3,8,128]{2,1,0:T(8,128)S(1)} %get-tuple-element.37), channel_id=1, source_target_pairs={{0,16},{16,32},{32,48},{48,64},{64,80},{80,96},{96,112},{112,128},... | collective-permute-start | bytes 36872 | tf_op jit(solution)/shard_map/ppermute | solution.py:747
  11.3 5.0 %collective-permute-start.1 = (f32[3,8,128]{2,1,0:T(8,128)S(1)}, f32[3,8,128]{2,1,0:T(8,128)S(1)}, u32[]{:S(2)}, u32[]{:S(2)}) collective-permute-start(f32[3,8,128]{2,1,0:T(8,128)S(1)} %get-tuple-element.38), channel_id=1, source_target_pairs={{16,0},{32,16},{48,32},{64,48},{80,64},{96,80},{112,96},{128,112},... | collective-permute-start | bytes 36872 | tf_op jit(solution)/shard_map/ppermute | solution.py:747
  18.2 24.6 %all-to-all-start = ((f32[16,128,128]{2,1,0:T(8,128)}), f32[16,128,128]{2,1,0:T(8,128)S(1)}, u32[]{:S(2)}, u32[]{:S(2)}) async-start(f32[16,128,128]{2,1,0:T(8,128)} %get-tuple-element.41), calls=%async_computation | async-start | bytes 2097152 | tf_op jit(solution)/shard_map/all_to_all | solution.py:751
  26.2 11.0 %collective-permute-start.4 = (f32[49,128]{1,0:T(8,128)S(1)}, f32[49,128]{1,0:T(8,128)S(1)}, u32[]{:S(2)}, u32[]{:S(2)}) collective-permute-start(f32[49,128]{1,0:T(8,128)S(1)} %get-tuple-element.50), channel_id=1, source_target_pairs={{0,1},{1,2},{2,3},{3,4},{4,5},{5,6},{6,7},{7,8},{8,9},{9,10},{10,1... | collective-permute-start | bytes 75272 | tf_op jit(solution)/shard_map/ppermute | solution.py:774
  29.4 10.3 %collective-permute-start.5 = (f32[49,128]{1,0:T(8,128)S(1)}, f32[49,128]{1,0:T(8,128)S(1)}, u32[]{:S(2)}, u32[]{:S(2)}) collective-permute-start(f32[49,128]{1,0:T(8,128)S(1)} %get-tuple-element.51), channel_id=1, source_target_pairs={{1,0},{2,1},{3,2},{4,3},{5,4},{6,5},{7,6},{8,7},{9,8},{10,9},{11,1... | collective-permute-start | bytes 75272 | tf_op jit(solution)/shard_map/ppermute | solution.py:775

commit v4 on v3

--- a/solution.py
+++ b/solution.py
@@ -23,6 +23,10 @@
 
 def store_of(label):
     return jnp.where(label == 1, 3.0 / 60.0, jnp.where(label == 2, 2.0 / 60.0, 1.0 / 60.0))
+
+
+def store_by(k):
+    return jnp.where(k > 30.0, 3.0 / 60.0, jnp.where(k > 10.0, 2.0 / 60.0, 1.0 / 60.0))
 
 
 def cure_of(label, warmth, cure):
@@ -273,8 +277,6 @@
     fluxz_ref,
     cure_ref,
     entry_ref,
-    toward_south_ref,
-    toward_north_ref,
     k_ref,
     g_ref,
     fy_ref,
@@ -303,15 +305,9 @@
     )
     ground = ground + jnp.where(at_end, face_y[YC], 0.0)
     side, back_side = reduce_sides(YC, lambda i: r_ref[y_rows(i), :], co1_ref, side_ref)
-    for out, y in ((toward_south_ref, 0), (toward_north_ref, YC - 1)):
-        k = k_ref[y_rows(y), :]
-        out[0:16] = fluxz_ref[y_rows(y), :]
-        out[16:32] = g_ref[y_rows(y), :]
-        fy_ref[8:24, :] = k
-        fy_ref[7:8, :] = below_ref[1, y : y + 1, :]
-        fy_ref[24:25, :] = above_ref[1, y : y + 1, :]
-        out[32:48] = 0.5 * (fy_ref[7:23, :] + k)
-        out[48:49] = 0.5 * (fy_ref[23:24, :] + fy_ref[24:25, :])
+    for y, row in ((0, 8 * ZC), (YC - 1, 8 * ZC + 4)):
+        for i, corner in enumerate((below_ref[0], above_ref[0], below_ref[1], above_ref[1])):
+            p_ref[row + i : row + i + 1] = corner[y : y + 1]
     k_ref[...] = conduct_of(m_ref[...], cure_ref[...])
     ks = [south_ref[2]] + [k_ref[y_rows(y), :] for y in range(YC)] + [north_ref[2]]
     faces = [0.5 * (ks[i] + ks[i + 1]) for i in range(YC + 1)]
@@ -408,8 +404,8 @@
     num1_ref,
     num2_ref,
     y_entry_ref,
-    of_south_ref,
-    of_north_ref,
+    south_ref,
+    north_ref,
     p_ref,
     side_z_ref,
     co_wide_ref,
@@ -446,28 +442,39 @@
         all_ref[then, 64:80, :],
         y_entry_ref[...],
     )
-    for side, value, of_ref in ((0, before, of_south_ref), (1, north, of_north_ref)):
-        capacity = of_ref[16:32]
-        rows = pl.ds(side, ZC, stride=2)
-        h_ref[0, rows, :] = jnp.where(capacity > 0.0, capacity, 1.0)
-        h_ref[1, rows, :] = capacity * value - of_ref[0:16]
-        h_ref[2, rows, :] = of_ref[32:48]
-        h_ref[2, 32 + side : 33 + side, :] = of_ref[48:49]
+    last = jnp.maximum(me - 1, 0)
+    beside = (
+        (0, before, south_ref, all_ref[last, 8 * ZC + 4 : 8 * ZC + 8, :]),
+        (1, north, north_ref, all_ref[then, 8 * ZC : 8 * ZC + 4, :]),
+    )
+    for side, value, halo_ref, corners in beside:
+        rows = pl.ds(2 + side, ZC, stride=2)
+        for q in range(2):
+            h_ref[q, rows, :] = halo_ref[q]
+            h_ref[q, side : side + 1, :] = corners[2 * q : 2 * q + 1]
+            h_ref[q, 34 + side : 35 + side, :] = corners[2 * q + 1 : 2 * q + 2]
+        h_ref[2, rows, :] = value
+    faces = 0.5 * (h_ref[1, 0:34, :] + h_ref[1, 2:36, :])
+    h_ref[3, 0:34, :] = faces
+    h_ref[4, 0:34, :] = faces * (h_ref[0, 2:36, :] - h_ref[0, 0:34, :])
+    capacity = store_by(h_ref[1, 2:34, :])
+    h_ref[5, 0:32, :] = capacity
+    h_ref[6, 0:32, :] = capacity * h_ref[2, 2:34, :] - (h_ref[4, 2:34, :] - h_ref[4, 0:32, :])
     numbers = reduce_coefficients(
         ZC,
-        lambda i: h_ref[0, 2 * i : 2 * i + 2, :],
-        lambda i: h_ref[2, 2 * i + 2 : 2 * i + 4, :],
-        h_ref[2, 0:2, :],
+        lambda i: h_ref[5, 2 * i : 2 * i + 2, :],
+        lambda i: h_ref[3, 2 * i + 2 : 2 * i + 4, :],
+        h_ref[3, 0:2, :],
         co_wide_ref,
     )
     sides = reduce_sides(
-        ZC, lambda i: h_ref[1, 2 * i : 2 * i + 2, :], co_wide_ref, side_wide_ref
+        ZC, lambda i: h_ref[6, 2 * i : 2 * i + 2, :], co_wide_ref, side_wide_ref
     )
     at_end = lax.axis_index("gz") == groups_z - 1
     p_ref[8 * YC + 8 :, :] = jnp.zeros((8, XC), jnp.float32)
     p_ref[wide_rows(0), :] = numbers[0]
     p_ref[wide_rows(1), :] = numbers[1]
-    p_ref[wide_rows(2), :] = numbers[2] + jnp.where(at_end, h_ref[2, 32:34, :], 0.0)
+    p_ref[wide_rows(2), :] = numbers[2] + jnp.where(at_end, h_ref[3, 32:34, :], 0.0)
     p_ref[wide_rows(3), :] = sides[0]
     p_ref[wide_rows(4), :] = sides[1]
 
@@ -761,18 +768,15 @@
     co_z, side_z, num_z = f32(3, ZC - 1, YC, XC), f32(ZC - 1, YC, XC), f32(3, YC, XC)
     x_shape = f32(2 * ROUNDS + 2, ROWS, XC)
     line = (groups_y + 1, ZC, XC)
-    message = f32(3 * ZC + 1, XC)
 
     (x1,) = call(x_kernel, [x_shape])(c, m)
-    pay, co_y1, side, co_y2, fluxz, c1, y_entry, toward_south, toward_north = call(
+    pay, co_y1, side, co_y2, fluxz, c1, y_entry = call(
         front_kernel,
-        [f32(groups_y, 8 * ZC, XC), co_y, side_y, co_y, block, block, f32(ZC, XC), message, message],
-        [cells] * 4 + [(8 * ZC, XC)],
+        [f32(groups_y, 8 * ZC + 8, XC), co_y, side_y, co_y, block, block, f32(ZC, XC)],
+        [cells] * 4 + [(8 * ZC + 8, XC)],
         spread_to=groups_y,
         groups=groups_y,
     )(t, c, m, x1, *z_halo, *y_halo)
-    of_south = lax.ppermute(toward_north, "gy", up["gy"])
-    of_north = lax.ppermute(toward_south, "gy", down["gy"])
     x2, co_z1, num_z1, co_z2, num_z2, z_entry = call(
         ahead_kernel,
         [x_shape, co_z, num_z, co_z, num_z, f32(YC, XC)],
@@ -782,9 +786,9 @@
     numbers, side, co_wide, side_wide = call(
         middle_kernel,
         [f32(SHARED, XC), side_z, f32(3, ZC - 1, 2, XC), f32(ZC - 1, 2, XC)],
-        [line, cells, (3, 2 * ZC + 2, XC)],
+        [line, cells, (7, 40, XC)],
         **sizes,
-    )(everyone, co_y1, side, fluxz, m, co_z1, num_z1, num_z2, y_entry, of_south, of_north)
+    )(everyone, co_y1, side, fluxz, m, co_z1, num_z1, num_z2, y_entry, *y_halo)
     pair = share(numbers)
     (pay,) = call(
         merge_kernel, [f32(chips, 40, XC)], [(40, XC)], spread_to=chips, copies=chips

time: 125 us -> 125 us (level)
  waiting for transfers between devices: 11.7 us -> 17.1 us
  starting transfers between devices: 25.1 us -> 20.6 us
    all_to_all x1, waiting for transfers between devices: 3.08 us -> 16.3 us  [gather_y(): return lax.all_to_all(pay, 'gy', 0, 0, tiled=True)]
    ppermute x2 -> x0, waiting for transfers between devices: 7.84 us -> none  [the longest x1 5.32 us: body(): of_south = lax.ppermute(toward_north, 'gy', up['gy'])]
    ppermute x2 -> x0, starting transfers between devices: 4.55 us -> none  [the longest x1 3.26 us: body(): of_south = lax.ppermute(toward_north, 'gy', up['gy'])]
  transfers between devices with their start and end apart: 7 -> 5, of which waited for: 4 -> 2; matrix products, arithmetic and copies ran while one was open for 0% -> 0% of each run, Pallas kernels for 2% -> 2%
where the time goes in v4:
time: 125 us
  blocking collectives  76.7 us (61%)
  starting transfers between devices  20.6 us (16%)
  waiting for transfers between devices  17.1 us (14%)
  Pallas kernels  9.45 us (8%)
    all_to_all x2, blocking collectives, gather_z(): lax.all_to_all(pay, 'gz', 0, 0, tiled=True, axis_index_groups=same_core)  49.4 us
    all_gather x4, blocking collectives, share(): return lax.all_gather(numbers, 'gz', axis_index_groups=pairs)  16.5 us
    all_to_all x1, waiting for transfers between devices, gather_y(): return lax.all_to_all(pay, 'gy', 0, 0, tiled=True)  16.3 us
    all_to_all x1, blocking collectives, gather_y(): return lax.all_to_all(pay, 'gy', 0, 0, tiled=True)  10.8 us
    all_to_all x1, starting transfers between devices, gather_y(): return lax.all_to_all(pay, 'gy', 0, 0, tiled=True)  7.92 us
    ppermute x1, starting transfers between devices, body(): lax.ppermute(zhi, 'gz', up['gz'])  4.39 us
    ppermute x1, starting transfers between devices, body(): lax.ppermute(yhi, 'gy', up['gy'])  3.95 us
    ppermute x1, starting transfers between devices, body(): lax.ppermute(zlo, 'gz', down['gz'])  3.04 us
  transfers between devices with their start and end apart: 5, of which 2 were waited for; matrix products, arithmetic and copies ran while one was open for 0% of the time, Pallas kernels for 2%

profile of v4, /device:TPU:1, one launch (start us, length us, event | category | flops | bytes accessed | tf_op | source)
XLA Modules:
  0.0 124.6 jit_solution(4168372924342408244)
XLA Ops:
  0.6 1.0 edges_kernel.1
  1.6 3.9 %collective-permute-start.2 = (f32[3,16,128]{2,1,0:T(8,128)S(1)}, f32[3,16,128]{2,1,0:T(8,128)S(1)}, u32[]{:S(2)}, u32[]{:S(2)}) collective-permute-start(f32[3,16,128]{2,1,0:T(8,128)S(1)} %get-tuple-element.37), channel_id=1, source_target_pairs={{0,1},{1,2},{2,3},{3,4},{4,5},{5,6},{6,7},{7,8},{8,9},{9,10},{10,1... | collective-permute-start | bytes 73736 | tf_op jit(solution)/shard_map/ppermute | solution.py:755
  5.6 1.3 %collective-permute-start.3 = (f32[3,16,128]{2,1,0:T(8,128)S(1)}, f32[3,16,128]{2,1,0:T(8,128)S(1)}, u32[]{:S(2)}, u32[]{:S(2)}) collective-permute-start(f32[3,16,128]{2,1,0:T(8,128)S(1)} %get-tuple-element.38), channel_id=1, source_target_pairs={{1,0},{2,1},{3,2},{4,3},{5,4},{6,5},{7,6},{8,7},{9,8},{10,9},{11,1... | collective-permute-start | bytes 73736 | tf_op jit(solution)/shard_map/ppermute | solution.py:755
  6.9 4.4 %collective-permute-start = (f32[3,8,128]{2,1,0:T(8,128)S(1)}, f32[3,8,128]{2,1,0:T(8,128)S(1)}, u32[]{:S(2)}, u32[]{:S(2)}) collective-permute-start(f32[3,8,128]{2,1,0:T(8,128)S(1)} %get-tuple-element.35), channel_id=1, source_target_pairs={{0,16},{16,32},{32,48},{48,64},{64,80},{80,96},{96,112},{112,128},... | collective-permute-start | bytes 36872 | tf_op jit(solution)/shard_map/ppermute | solution.py:754
  11.3 3.0 %collective-permute-start.1 = (f32[3,8,128]{2,1,0:T(8,128)S(1)}, f32[3,8,128]{2,1,0:T(8,128)S(1)}, u32[]{:S(2)}, u32[]{:S(2)}) collective-permute-start(f32[3,8,128]{2,1,0:T(8,128)S(1)} %get-tuple-element.36), channel_id=1, source_target_pairs={{16,0},{32,16},{48,32},{64,48},{80,64},{96,80},{112,96},{128,112},... | collective-permute-start | bytes 36872 | tf_op jit(solution)/shard_map/ppermute | solution.py:754
  14.3 1.1 x_kernel.1.x_ref
  15.4 0.0 collective-permute-done.below_ref
  15.4 0.8 collective-permute-done.1.above_ref
  16.3 0.0 collective-permute-done.2.south_ref
  16.3 0.0 collective-permute-done.3.north_ref
  16.3 2.0 %front_kernel.1 = (f32[16,136,128]{2,1,0:T(8,128)}, f32[3,7,16,128]{3,2,1,0:T(8,128)S(1)}, f32[7,16,128]{2,1,0:T(8,128)S(1)}, f32[3,7,16,128]{3,2,1,0:T(8,128)S(...) custom-call(f32[128,128]{1,0:T(8,128)S(1)} %get-tuple-element.32.t_ref, ...), custom_call_target="tpu_custom_call" | custom-call | tf_op jit(solution)/shard_map/front_kernel/pallas_call | solution.py:773
  18.3 7.9 %all-to-all-start = ((f32[16,136,128]{2,1,0:T(8,128)}), f32[16,136,128]{2,1,0:T(8,128)S(1)}, u32[]{:S(2)}, u32[]{:S(2)}) async-start(f32[16,136,128]{2,1,0:T(8,128)} %get-tuple-element.39), calls=%async_computation | async-start | bytes 2228224 | tf_op jit(solution)/shard_map/all_to_all | solution.py:758
  26.2 1.2 ahead_kernel.1
  27.3 16.3 %all-to-all-done.all_ref = f32[16,136,128]{2,1,0:T(8,128)S(1)} async-done(((f32[16,136,128]{2,1,0:T(8,128)}), f32[16,136,128]{2,1,0:T(8,128)S(1)}, u32[]{:S(2)}, u32[]{:S(2)}) %all-to-all-start) | async-done | bytes 1114144 | tf_op jit(solution)/shard_map/all_to_all | solution.py:758
  43.6 0.2 middle_kernel.1
  43.9 1.9 %all-gather = f32[160,128]{1,0:T(8,128)S(1)} all-gather(f32[80,128]{1,0:T(8,128)S(1)} %get-tuple-element.48), channel_id=2, replica_groups={{0,16},{32,48},{64,80},{96,112},{128,144},{160,176},{192,208},{224,240}..., dimensions={0}, use_global_device_ids=true | all-gather | bytes 122880 | tf_op jit(solution)/shard_map/all_gather | solution.py:764
  45.7 0.6 merge_kernel.1
  46.4 32.4 %all_to_all.20.all_ref = f32[16,40,128]{2,1,0:T(8,128)S(1)} all-to-all(f32[16,40,128]{2,1,0:T(8,128)S(1)} %merge_kernel.1), channel_id=1, replica_groups={{0,32,64,96,128,160,192,224,256,288,320,352,384,416,448,480},{16,48,80,..., dimensions={0} | all-to-all | bytes 655360 | tf_op jit(solution)/shard_map/all_to_all | solution.py:761
  78.8 0.1 chain_kernel.1
  78.9 8.1 %all-gather.1 = f32[32,128]{1,0:T(8,128)S(1)} all-gather(f32[16,128]{1,0:T(8,128)S(1)} %chain_kernel.1), channel_id=3, replica_groups={{0,16},{32,48},{64,80},{96,112},{128,144},{160,176},{192,208},{224,240}..., dimensions={0}, use_global_device_ids=true | all-gather | bytes 24576 | tf_op jit(solution)/shard_map/all_gather | solution.py:764
  87.0 2.1 %turn_kernel.1 = (f32[16,32,128]{2,1,0:T(8,128)S(1)}, f32[7,16,128]{2,1,0:T(8,128)S(1)}, f32[128,128]{1,0:T(8,128)S(1)}, f32[128,128]{1,0:T(8,128)}) custom-call(f32[2,80,128]{2,1,0:T(8,128)S(1)} %bitcast.10, f32[2,16,128]{2,1,0:T(8,128)S(1)} %bitcast.15, f32[3,15,8,128]{3,2,1,0:T(8,128)S(1)} %get-tuple-element.44.co_z_ref, ...), custom_call_target="tpu_custom_call" | custom-call | tf_op jit(solution)/shard_map/turn_kernel/pallas_call | solution.py:798
  89.0 10.8 %all_to_all.21.more_ref = f32[16,32,128]{2,1,0:T(8,128)S(1)} all-to-all(f32[16,32,128]{2,1,0:T(8,128)S(1)} %get-tuple-element.55), channel_id=1, replica_groups=mesh['gz'=32,'gy'=16] {'gy'}, dimensions={0} | all-to-all | bytes 524288 | tf_op jit(solution)/shard_map/all_to_all | solution.py:758
  99.8 0.2 later_middle_kernel.1
  100.0 3.0 %all-gather.2 = f32[32,128]{1,0:T(8,128)S(1)} all-gather(f32[16,128]{1,0:T(8,128)S(1)} %get-tuple-element.59), channel_id=4, replica_groups={{0,16},{32,48},{64,80},{96,112},{128,144},{160,176},{192,208},{224,240}..., dimensions={0}, use_global_device_ids=true | all-gather | bytes 24576 | tf_op jit(solution)/shard_map/all_gather | solution.py:764
  102.9 0.3 later_merge_kernel.1
  103.2 17.0 %all_to_all.22.more_ref = f32[16,8,128]{2,1,0:T(8,128)S(1)} all-to-all(f32[16,8,128]{2,1,0:T(8,128)S(1)} %later_merge_kernel.1), channel_id=1, replica_groups={{0,32,64,96,128,160,192,224,256,288,320,352,384,416,448,480},{16,48,80,..., dimensions={0} | all-to-all | bytes 131072 | tf_op jit(solution)/shard_map/all_to_all | solution.py:761
  120.2 0.1 later_chain_kernel.1
  120.3 3.6 %all-gather.3 = f32[16,128]{1,0:T(8,128)S(1)} all-gather(f32[8,128]{1,0:T(8,128)S(1)} %later_chain_kernel.1), channel_id=5, replica_groups={{0,16},{32,48},{64,80},{96,112},{128,144},{160,176},{192,208},{224,240}..., dimensions={0}, use_global_device_ids=true | all-gather | bytes 12288 | tf_op jit(solution)/shard_map/all_gather | solution.py:764
  123.9 0.7 back_kernel.1
Async XLA Ops:
  1.6 14.7 %collective-permute-start.2 = (f32[3,16,128]{2,1,0:T(8,128)S(1)}, f32[3,16,128]{2,1,0:T(8,128)S(1)}, u32[]{:S(2)}, u32[]{:S(2)}) collective-permute-start(f32[3,16,128]{2,1,0:T(8,128)S(1)} %get-tuple-element.37), channel_id=1, source_target_pairs={{0,1},{1,2},{2,3},{3,4},{4,5},{5,6},{6,7},{7,8},{8,9},{9,10},{10,1... | collective-permute-start | bytes 73736 | tf_op jit(solution)/shard_map/ppermute | solution.py:755
  5.6 10.7 %collective-permute-start.3 = (f32[3,16,128]{2,1,0:T(8,128)S(1)}, f32[3,16,128]{2,1,0:T(8,128)S(1)}, u32[]{:S(2)}, u32[]{:S(2)}) collective-permute-start(f32[3,16,128]{2,1,0:T(8,128)S(1)} %get-tuple-element.38), channel_id=1, source_target_pairs={{1,0},{2,1},{3,2},{4,3},{5,4},{6,5},{7,6},{8,7},{9,8},{10,9},{11,1... | collective-permute-start | bytes 73736 | tf_op jit(solution)/shard_map/ppermute | solution.py:755
  6.9 8.6 %collective-permute-start = (f32[3,8,128]{2,1,0:T(8,128)S(1)}, f32[3,8,128]{2,1,0:T(8,128)S(1)}, u32[]{:S(2)}, u32[]{:S(2)}) collective-permute-start(f32[3,8,128]{2,1,0:T(8,128)S(1)} %get-tuple-element.35), channel_id=1, source_target_pairs={{0,16},{16,32},{32,48},{48,64},{64,80},{80,96},{96,112},{112,128},... | collective-permute-start | bytes 36872 | tf_op jit(solution)/shard_map/ppermute | solution.py:754
  11.3 5.0 %collective-permute-start.1 = (f32[3,8,128]{2,1,0:T(8,128)S(1)}, f32[3,8,128]{2,1,0:T(8,128)S(1)}, u32[]{:S(2)}, u32[]{:S(2)}) collective-permute-start(f32[3,8,128]{2,1,0:T(8,128)S(1)} %get-tuple-element.36), channel_id=1, source_target_pairs={{16,0},{32,16},{48,32},{64,48},{80,64},{96,80},{112,96},{128,112},... | collective-permute-start | bytes 36872 | tf_op jit(solution)/shard_map/ppermute | solution.py:754
  18.3 25.4 %all-to-all-start = ((f32[16,136,128]{2,1,0:T(8,128)}), f32[16,136,128]{2,1,0:T(8,128)S(1)}, u32[]{:S(2)}, u32[]{:S(2)}) async-start(f32[16,136,128]{2,1,0:T(8,128)} %get-tuple-element.39), calls=%async_computation | async-start | bytes 2228224 | tf_op jit(solution)/shard_map/all_to_all | solution.py:758

commit v5 on v4

--- a/solution.py
+++ b/solution.py
@@ -164,7 +164,7 @@
     x_coefficients(c_ref, m_ref, x_ref)
 
 
-def z_coefficients(groups_z, c_ref, m_ref, below, above, co_ref, num_ref):
+def z_coefficients(groups_z, c_ref, m_ref, below, above, co_ref, num_ref, row):
     ks = [below]
     for z in range(ZC):
         ks.append(conduct_of(m_ref[z_rows(z), :], c_ref[z_rows(z), :]))
@@ -177,10 +177,10 @@
         faces[0],
         co_ref,
     )
-    num_ref[0] = numbers[0]
-    num_ref[1] = numbers[1]
     at_end = lax.axis_index("gz") == groups_z - 1
-    num_ref[2] = numbers[2] + jnp.where(at_end, faces[ZC], 0.0)
+    num_ref[row : row + YC] = numbers[0]
+    num_ref[row + YC : row + 2 * YC] = numbers[1]
+    num_ref[row + 2 * YC : row + 3 * YC] = numbers[2] + jnp.where(at_end, faces[ZC], 0.0)
     return faces[ZC]
 
 
@@ -192,18 +192,19 @@
     above_ref,
     x_ref,
     co1_ref,
-    num1_ref,
     co2_ref,
-    num2_ref,
+    num_ref,
     entry_ref,
     *,
     groups_z,
 ):
     x_coefficients(next_c_ref, m_ref, x_ref)
     entry_ref[...] = z_coefficients(
-        groups_z, c_ref, m_ref, below_ref[1], above_ref[1], co1_ref, num1_ref
-    )
-    z_coefficients(groups_z, next_c_ref, m_ref, below_ref[2], above_ref[2], co2_ref, num2_ref)
+        groups_z, c_ref, m_ref, below_ref[1], above_ref[1], co1_ref, num_ref, 0
+    )
+    z_coefficients(
+        groups_z, next_c_ref, m_ref, below_ref[2], above_ref[2], co2_ref, num_ref, 3 * YC
+    )
 
 
 def flow_rhs(t_ref, c_ref, m_ref, x_ref, zt, yt, zk, yk, outs, scratch):
@@ -379,19 +380,12 @@
     return before, own
 
 
-def main_rows(q):
+def block_rows(q):
     return pl.ds(YC * q, YC)
 
 
-def later_rows(q):
-    return pl.ds(YC * (5 + q), YC)
-
-
 def wide_rows(q):
-    return pl.ds(8 * YC + 2 * q, 2)
-
-
-SHARED = 8 * YC + 16
+    return pl.ds(2 * YC + 2 * q, 2)
 
 
 def middle_kernel(
@@ -401,8 +395,6 @@
     fluxz_ref,
     m_ref,
     co_z_ref,
-    num1_ref,
-    num2_ref,
     y_entry_ref,
     south_ref,
     north_ref,
@@ -425,12 +417,10 @@
     def right(i):
         return store_of(m_ref[z_rows(i), :]) * v_ref[z_rows(i), :] - fluxz_ref[z_rows(i), :]
 
-    for q in range(3):
-        p_ref[main_rows(q), :] = num1_ref[q]
-        p_ref[later_rows(q), :] = num2_ref[q]
     sides = reduce_sides(ZC, right, co_z_ref, side_z_ref)
-    p_ref[main_rows(3), :] = sides[0]
-    p_ref[main_rows(4), :] = sides[1]
+    p_ref[24:32, :] = jnp.zeros((8, XC), jnp.float32)
+    p_ref[block_rows(0), :] = sides[0]
+    p_ref[block_rows(1), :] = sides[1]
 
     me = lax.axis_index("gy")
     then = jnp.minimum(me + 1, groups_y - 1)
@@ -471,7 +461,6 @@
         ZC, lambda i: h_ref[6, 2 * i : 2 * i + 2, :], co_wide_ref, side_wide_ref
     )
     at_end = lax.axis_index("gz") == groups_z - 1
-    p_ref[8 * YC + 8 :, :] = jnp.zeros((8, XC), jnp.float32)
     p_ref[wide_rows(0), :] = numbers[0]
     p_ref[wide_rows(1), :] = numbers[1]
     p_ref[wide_rows(2), :] = numbers[2] + jnp.where(at_end, h_ref[3, 32:34, :], 0.0)
@@ -510,7 +499,6 @@
 
 
 HALF = YC // 2
-WIDTH = HALF + 1
 
 
 def node_between(low, high):
@@ -530,16 +518,16 @@
     return high[3] + high[1] * inv * side, low[4] + low[1] * inv * side
 
 
-def first_numbers(pair_ref, rows):
-    return [[pair_ref[core, rows(q), :] for q in range(5)] for core in range(2)]
-
-
-def later_numbers(pair_ref, more_ref):
+def block_numbers(coef_ref, side_ref, step):
     return [
-        [pair_ref[core, later_rows(q), :] for q in range(3)]
-        + [more_ref[core, main_rows(q), :] for q in range(2)]
+        [coef_ref[core, block_rows(3 * step + q), :] for q in range(3)]
+        + [side_ref[core, block_rows(q), :] for q in range(2)]
         for core in range(2)
     ]
+
+
+def wide_numbers(side_ref):
+    return [[side_ref[core, wide_rows(q), :] for q in range(5)] for core in range(2)]
 
 
 def my_half(number):
@@ -548,60 +536,142 @@
     return jnp.where(core == 0, number[:half], number[half:])
 
 
-def merge_kernel(pair_ref, pay_ref, p_ref, sem, *, copies):
-    p_ref[32:40] = jnp.zeros((8, XC), jnp.float32)
-    low, high = first_numbers(pair_ref, main_rows)
+def halves(q):
+    return pl.ds(HALF * q, HALF)
+
+
+def links_kernel(coef_ref, link_ref, low_ref, high_ref):
+    for step in range(2):
+        low, high = (
+            [coef_ref[core, block_rows(3 * step + q), :] for q in range(3)] for core in range(2)
+        )
+        back_ground, edge, ground = merged_coefficients(low, high)
+        link_ref[halves(step), :] = my_half(edge)
+        low_ref[halves(step), :] = my_half(back_ground + edge)
+        high_ref[halves(step), :] = my_half(ground + edge)
+
+
+def merge_kernel(
+    coef_ref,
+    pair_ref,
+    link_ref,
+    low_ref,
+    high_ref,
+    from_low_ref,
+    from_high_ref,
+    pay_ref,
+    scale_ref,
+    p_ref,
+    sem,
+    *,
+    copies,
+):
+    p_ref[16:24] = jnp.zeros((8, XC), jnp.float32)
+    for step in range(2):
+        rows = halves(step)
+        own = high_ref[rows, :] + from_high_ref[rows, :]
+        root = jnp.sqrt(own)
+        own_inv = 1.0 / root
+        last_inv = 1.0 / jnp.sqrt(from_low_ref[rows, :] + low_ref[rows, :])
+        scale_ref[halves(2 * step), :] = own_inv
+        scale_ref[halves(2 * step + 1), :] = last_inv
+        p_ref[halves(3 * step), :] = link_ref[rows, :] * (own_inv * last_inv)
+        if step == 0:
+            scale_ref[halves(4), :] = root
+            scale_ref[halves(5), :] = from_high_ref[rows, :]
+    low, high = block_numbers(coef_ref, pair_ref, 0)
+    side, back_side = merged_sides(low, high)
+    p_ref[halves(1), :] = my_half(side) * scale_ref[halves(0), :]
+    p_ref[halves(2), :] = my_half(back_side) * scale_ref[halves(1), :]
+    low, high = wide_numbers(pair_ref)
     for q, number in enumerate(merged_coefficients(low, high) + merged_sides(low, high)):
-        p_ref[WIDTH * q : WIDTH * q + HALF] = my_half(number)
-    low, high = first_numbers(pair_ref, wide_rows)
-    for q, number in enumerate(merged_coefficients(low, high) + merged_sides(low, high)):
-        p_ref[WIDTH * q + HALF : WIDTH * q + WIDTH] = my_half(number)
-    low, high = ([pair_ref[core, later_rows(q), :] for q in range(3)] for core in range(2))
-    for q, number in enumerate(merged_coefficients(low, high)):
-        row = 5 * WIDTH + HALF * q
-        p_ref[row : row + HALF] = my_half(number)
+        p_ref[16 + q : 17 + q] = my_half(number)
     spread(p_ref, pay_ref, sem, copies)
 
 
-def later_merge_kernel(pair_ref, more_ref, pay_ref, p_ref, sem, *, copies):
-    low, high = later_numbers(pair_ref, more_ref)
-    for q, number in enumerate(merged_sides(low, high)):
-        p_ref[HALF * q : HALF * q + HALF] = my_half(number)
+def later_merge_kernel(coef_ref, more_ref, scale_ref, pay_ref, p_ref, sem, *, copies):
+    side, back_side = merged_sides(*block_numbers(coef_ref, more_ref, 1))
+    p_ref[halves(0), :] = my_half(side) * scale_ref[halves(2), :]
+    p_ref[halves(1), :] = my_half(back_side) * scale_ref[halves(3), :]
     spread(p_ref, pay_ref, sem, copies)
 
 
-def chain_kernel(all_ref, out_ref, s_ref, *, chips):
-    s_ref[0] = jnp.zeros((WIDTH, XC), jnp.float32)
+def unit_chain(count, link, side_of, put):
+    half = count // 2
+    gain, part = [None] * count, [None] * count
+    diag_l = diag_r = None
+    side_l, side_r = side_of(0), side_of(count - 1)
+    for i in range(half - 1):
+        j = count - 1 - i
+        edge_l, edge_r = link(i + 1), link(j)
+        if i == 0:
+            gain[i], part[i], gain[j], part[j] = edge_l, side_l, edge_r, side_r
+        else:
+            inv_l, inv_r = 1.0 / diag_l, 1.0 / diag_r
+            gain[i], part[i] = edge_l * inv_l, side_l * inv_l
+            gain[j], part[j] = edge_r * inv_r, side_r * inv_r
+        diag_l = 1.0 - edge_l * gain[i]
+        side_l = side_of(i + 1) + edge_l * part[i]
+        diag_r = 1.0 - edge_r * gain[j]
+        side_r = side_of(j - 1) + edge_r * part[j]
+    edge = link(half)
+    if half == 1:
+        diag_l = diag_r = jnp.ones_like(edge)
+    inv = 1.0 / (diag_l * diag_r - edge * edge)
+    low = (side_l * diag_r + edge * side_r) * inv
+    high = (side_r * diag_l + edge * side_l) * inv
+    put(half - 1, low)
+    put(half, high)
+    for i in range(half - 2, -1, -1):
+        low = part[i] + gain[i] * low
+        put(i, low)
+        j = count - 1 - i
+        high = part[j] + gain[j] * high
+        put(j, high)
+
+
+def chain_kernel(all_ref, scale_ref, out_ref, s_ref, w_ref, *, chips):
+    s_ref[0] = jnp.zeros((HALF, XC), jnp.float32)
+    w_ref[0] = jnp.zeros((1, XC), jnp.float32)
+
+    def side_of(j):
+        side = all_ref[j, halves(1), :]
+        return side + all_ref[j + 1, halves(2), :] if j + 1 < chips else side
 
     def put(j, value):
         s_ref[j + 1] = value
 
-    chain(chips, lambda j, q: all_ref[j, WIDTH * q : WIDTH * q + WIDTH, :], put)
+    def put_wide(j, value):
+        w_ref[j + 1] = value
+
+    unit_chain(chips, lambda j: all_ref[j, halves(0), :], side_of, put)
+    chain(chips, lambda j, q: all_ref[j, 16 + q : 17 + q, :], put_wide)
     me = lax.div(lax.axis_index("gz"), 2)
     then = jnp.minimum(me + 1, chips - 1)
-    own, after = s_ref[me + 1], s_ref[then + 1]
-    numbers = [all_ref[then, WIDTH * q : WIDTH * q + WIDTH, :] for q in (0, 1, 4)]
+    own = s_ref[me + 1] * scale_ref[halves(0), :]
+    inflow = all_ref[then, halves(0), :] * s_ref[then + 1] + all_ref[then, halves(2), :]
     out_ref[8:16] = jnp.zeros((8, XC), jnp.float32)
-    out_ref[0:WIDTH] = s_ref[me]
-    out_ref[WIDTH : 2 * WIDTH] = own
-    out_ref[2 * WIDTH : 3 * WIDTH] = numbers[0] * own + numbers[1] * (own - after) - numbers[2]
-
-
-def later_chain_kernel(all_ref, more_ref, out_ref, s_ref, *, chips):
+    out_ref[halves(0), :] = s_ref[me] * scale_ref[halves(1), :]
+    out_ref[halves(1), :] = own
+    out_ref[halves(2), :] = scale_ref[halves(5), :] * own - scale_ref[halves(4), :] * inflow
+    out_ref[12:13] = w_ref[me]
+    out_ref[13:14] = w_ref[me + 1]
+
+
+def later_chain_kernel(all_ref, more_ref, scale_ref, out_ref, s_ref, *, chips):
     s_ref[0] = jnp.zeros((HALF, XC), jnp.float32)
+
+    def side_of(j):
+        side = more_ref[j, halves(0), :]
+        return side + more_ref[j + 1, halves(1), :] if j + 1 < chips else side
 
     def put(j, value):
         s_ref[j + 1] = value
 
-    def read(j, q):
-        if q < 3:
-            return all_ref[j, 5 * WIDTH + HALF * q : 5 * WIDTH + HALF * (q + 1), :]
-        return more_ref[j, HALF * (q - 3) : HALF * (q - 2), :]
-
-    chain(chips, read, put)
+    unit_chain(chips, lambda j: all_ref[j, halves(3), :], side_of, put)
     me = lax.div(lax.axis_index("gz"), 2)
-    out_ref[0:HALF] = s_ref[me]
-    out_ref[HALF : 2 * HALF] = s_ref[me + 1]
+    out_ref[halves(0), :] = s_ref[me] * scale_ref[halves(3), :]
+    out_ref[halves(1), :] = s_ref[me + 1] * scale_ref[halves(2), :]
 
 
 def ends_of(low, high, before, last):
@@ -611,16 +681,15 @@
     return jnp.where(upper, node, before), jnp.where(upper, last, node), node
 
 
-def joined(res_ref, u_ref, width, count):
+def joined(res_ref, u_ref, count):
     for q in range(count):
         for core in range(2):
-            rows = pl.ds(HALF * core, HALF)
-            u_ref[q, rows, :] = res_ref[core, width * q : width * q + HALF, :]
-
-
-def back_kernel(pair_ref, more_ref, res_ref, co_z_ref, side_z_ref, t_ref, u_ref):
-    joined(res_ref, u_ref, HALF, 2)
-    low, high = later_numbers(pair_ref, more_ref)
+            u_ref[q, halves(core), :] = res_ref[core, halves(q), :]
+
+
+def back_kernel(coef_ref, more_ref, res_ref, co_z_ref, side_z_ref, t_ref, u_ref):
+    joined(res_ref, u_ref, 2)
+    low, high = block_numbers(coef_ref, more_ref, 1)
     before, own, _ = ends_of(low, high, u_ref[0], u_ref[1])
 
     def place(i, value):
@@ -630,6 +699,7 @@
 
 
 def turn_kernel(
+    coef_ref,
     pair_ref,
     res_ref,
     co_z_ref,
@@ -663,8 +733,8 @@
     groups_y,
     groups_z,
 ):
-    joined(res_ref, u_ref, WIDTH, 3)
-    low, high = first_numbers(pair_ref, main_rows)
+    joined(res_ref, u_ref, 3)
+    low, high = block_numbers(coef_ref, pair_ref, 0)
     last = u_ref[1]
     before, own, node = ends_of(low, high, u_ref[0], last)
 
@@ -679,9 +749,8 @@
 
     for q in range(2):
         for core in range(2):
-            row = WIDTH * q + HALF
-            w_ref[q, core : core + 1] = res_ref[core, row : row + 1, :]
-    low, high = first_numbers(pair_ref, wide_rows)
+            w_ref[q, core : core + 1] = res_ref[core, 12 + q : 13 + q, :]
+    low, high = wide_numbers(pair_ref)
     before_wide, own_wide, _ = ends_of(low, high, w_ref[0], w_ref[1])
 
     def place_wide(i, value):
@@ -765,7 +834,9 @@
 
     sizes = dict(groups_y=groups_y, groups_z=groups_z)
     co_y, side_y = f32(3, YC - 1, ZC, XC), f32(YC - 1, ZC, XC)
-    co_z, side_z, num_z = f32(3, ZC - 1, YC, XC), f32(ZC - 1, YC, XC), f32(3, YC, XC)
+    co_z, side_z = f32(3, ZC - 1, YC, XC), f32(ZC - 1, YC, XC)
+    next_chip = [(i, i + 2) for i in range(groups_z - 2)]
+    last_chip = [(j, i) for i, j in next_chip]
     x_shape = f32(2 * ROUNDS + 2, ROWS, XC)
     line = (groups_y + 1, ZC, XC)
 
@@ -777,24 +848,35 @@
         spread_to=groups_y,
         groups=groups_y,
     )(t, c, m, x1, *z_halo, *y_halo)
-    x2, co_z1, num_z1, co_z2, num_z2, z_entry = call(
+    x2, co_z1, co_z2, numbers, z_entry = call(
         ahead_kernel,
-        [x_shape, co_z, num_z, co_z, num_z, f32(YC, XC)],
+        [x_shape, co_z, co_z, f32(6 * YC, XC), f32(YC, XC)],
         groups_z=groups_z,
     )(c, c1, m, *z_halo)
+    coef = share(numbers)
+    link, low, high = call(links_kernel, [f32(YC, XC)] * 3)(coef)
+    from_low = lax.ppermute(high, "gz", next_chip)
+    from_high = lax.ppermute(low, "gz", last_chip)
     everyone = gather_y(pay)
     numbers, side, co_wide, side_wide = call(
         middle_kernel,
-        [f32(SHARED, XC), side_z, f32(3, ZC - 1, 2, XC), f32(ZC - 1, 2, XC)],
+        [f32(4 * YC, XC), side_z, f32(3, ZC - 1, 2, XC), f32(ZC - 1, 2, XC)],
         [line, cells, (7, 40, XC)],
         **sizes,
-    )(everyone, co_y1, side, fluxz, m, co_z1, num_z1, num_z2, y_entry, *y_halo)
+    )(everyone, co_y1, side, fluxz, m, co_z1, y_entry, *y_halo)
     pair = share(numbers)
-    (pay,) = call(
-        merge_kernel, [f32(chips, 40, XC)], [(40, XC)], spread_to=chips, copies=chips
-    )(pair)
+    pay, scale = call(
+        merge_kernel,
+        [f32(chips, 24, XC), f32(24, XC)],
+        [(24, XC)],
+        spread_to=chips,
+        copies=chips,
+    )(coef, pair, link, low, high, from_low, from_high)
     column = gather_z(pay)
-    (found,) = call(chain_kernel, [f32(16, XC)], [(chips + 1, WIDTH, XC)], chips=chips)(column)
+    half_line = (chips + 1, HALF, XC)
+    (found,) = call(
+        chain_kernel, [f32(16, XC)], [half_line, (chips + 1, 1, XC)], chips=chips
+    )(column, scale)
     pay, side, fluxz, c2 = call(
         turn_kernel,
         [f32(groups_y, 2 * ZC, XC), side_y, block, block],
@@ -802,6 +884,7 @@
         spread_to=groups_y,
         **sizes,
     )(
+        coef,
         pair,
         share(found),
         co_z1,
@@ -822,11 +905,11 @@
     more = share(numbers)
     (pay,) = call(
         later_merge_kernel, [f32(chips, YC, XC)], [(YC, XC)], spread_to=chips, copies=chips
-    )(pair, more)
-    (found,) = call(
-        later_chain_kernel, [f32(YC, XC)], [(chips + 1, HALF, XC)], chips=chips
-    )(column, gather_z(pay))
-    (t2,) = call(back_kernel, [block], [(2, YC, XC)])(pair, more, share(found), co_z2, side)
+    )(coef, more, scale)
+    (found,) = call(later_chain_kernel, [f32(YC, XC)], [half_line], chips=chips)(
+        column, gather_z(pay), scale
+    )
+    (t2,) = call(back_kernel, [block], [(2, YC, XC)])(coef, more, share(found), co_z2, side)
     return t2.reshape(warmth.shape), c2.reshape(cure.shape)
 
 

time: 125 us -> 119 us (0.952)
  waiting for transfers between devices: 17.1 us -> 9.79 us
  starting transfers between devices: 20.6 us -> 26 us
  blocking collectives: 76.7 us -> 72.9 us
    all_to_all x1, waiting for transfers between devices: 16.3 us -> 8.95 us  [gather_y(): return lax.all_to_all(pay, 'gy', 0, 0, tiled=True)]
    ppermute x0 -> x2, starting transfers between devices: none -> 5.46 us  [the longest x1 4.17 us: body(): from_low = lax.ppermute(high, 'gz', next_chip)]
    all_to_all x2, blocking collectives: 49.4 us -> 47.1 us  [gather_z(): lax.all_to_all(pay, 'gz', 0, 0, tiled=True, axis_index_groups=same_core)]
    all_gather x4 -> x5, blocking collectives: 16.5 us -> 15 us  [share(): return lax.all_gather(numbers, 'gz', axis_index_groups=pairs)]
  transfers between devices with their start and end apart: 5 -> 7, of which waited for: 2 -> 2; matrix products, arithmetic and copies ran while one was open for 0% -> 0% of each run, Pallas kernels for 2% -> 2%
where the time goes in v5:
time: 119 us
  blocking collectives  72.9 us (61%)
  starting transfers between devices  26 us (22%)
  waiting for transfers between devices  9.79 us (8%)
  Pallas kernels  9.29 us (8%)
    all_to_all x2, blocking collectives, gather_z(): lax.all_to_all(pay, 'gz', 0, 0, tiled=True, axis_index_groups=same_core)  47.1 us
    all_gather x5, blocking collectives, share(): return lax.all_gather(numbers, 'gz', axis_index_groups=pairs)  15 us
    all_to_all x1, blocking collectives, gather_y(): return lax.all_to_all(pay, 'gy', 0, 0, tiled=True)  10.8 us
    all_to_all x1, waiting for transfers between devices, gather_y(): return lax.all_to_all(pay, 'gy', 0, 0, tiled=True)  8.95 us
    all_to_all x1, starting transfers between devices, gather_y(): return lax.all_to_all(pay, 'gy', 0, 0, tiled=True)  7.92 us
    ppermute x1, starting transfers between devices, body(): lax.ppermute(zhi, 'gz', up['gz'])  4.39 us
    ppermute x1, starting transfers between devices, body(): from_low = lax.ppermute(high, 'gz', next_chip)  4.17 us
    ppermute x1, starting transfers between devices, body(): lax.ppermute(yhi, 'gy', up['gy'])  3.95 us
  transfers between devices with their start and end apart: 7, of which 2 were waited for; matrix products, arithmetic and copies ran while one was open for 0% of the time, Pallas kernels for 2%

profile of v5, /device:TPU:1, one launch (start us, length us, event | category | flops | bytes accessed | tf_op | source)
XLA Modules:
  0.0 118.8 jit_solution(10126968647546873312)
XLA Ops:
  0.6 1.0 edges_kernel.1
  1.6 3.9 %collective-permute-start.2 = (f32[3,16,128]{2,1,0:T(8,128)S(1)}, f32[3,16,128]{2,1,0:T(8,128)S(1)}, u32[]{:S(2)}, u32[]{:S(2)}) collective-permute-start(f32[3,16,128]{2,1,0:T(8,128)S(1)} %get-tuple-element.41), channel_id=1, source_target_pairs={{0,1},{1,2},{2,3},{3,4},{4,5},{5,6},{6,7},{7,8},{8,9},{9,10},{10,1... | collective-permute-start | bytes 73736 | tf_op jit(solution)/shard_map/ppermute | solution.py:824
  5.6 1.3 %collective-permute-start.3 = (f32[3,16,128]{2,1,0:T(8,128)S(1)}, f32[3,16,128]{2,1,0:T(8,128)S(1)}, u32[]{:S(2)}, u32[]{:S(2)}) collective-permute-start(f32[3,16,128]{2,1,0:T(8,128)S(1)} %get-tuple-element.42), channel_id=1, source_target_pairs={{1,0},{2,1},{3,2},{4,3},{5,4},{6,5},{7,6},{8,7},{9,8},{10,9},{11,1... | collective-permute-start | bytes 73736 | tf_op jit(solution)/shard_map/ppermute | solution.py:824
  6.9 4.4 %collective-permute-start = (f32[3,8,128]{2,1,0:T(8,128)S(1)}, f32[3,8,128]{2,1,0:T(8,128)S(1)}, u32[]{:S(2)}, u32[]{:S(2)}) collective-permute-start(f32[3,8,128]{2,1,0:T(8,128)S(1)} %get-tuple-element.39), channel_id=1, source_target_pairs={{0,16},{16,32},{32,48},{48,64},{64,80},{80,96},{96,112},{112,128},... | collective-permute-start | bytes 36872 | tf_op jit(solution)/shard_map/ppermute | solution.py:823
  11.3 3.0 %collective-permute-start.1 = (f32[3,8,128]{2,1,0:T(8,128)S(1)}, f32[3,8,128]{2,1,0:T(8,128)S(1)}, u32[]{:S(2)}, u32[]{:S(2)}) collective-permute-start(f32[3,8,128]{2,1,0:T(8,128)S(1)} %get-tuple-element.40), channel_id=1, source_target_pairs={{16,0},{32,16},{48,32},{64,48},{80,64},{96,80},{112,96},{128,112},... | collective-permute-start | bytes 36872 | tf_op jit(solution)/shard_map/ppermute | solution.py:823
  14.3 1.1 x_kernel.1.x_ref
  15.4 0.0 collective-permute-done.below_ref
  15.4 0.8 collective-permute-done.1.above_ref
  16.3 0.0 collective-permute-done.2.south_ref
  16.3 0.0 collective-permute-done.3.north_ref
  16.3 2.0 %front_kernel.1 = (f32[16,136,128]{2,1,0:T(8,128)}, f32[3,7,16,128]{3,2,1,0:T(8,128)S(1)}, f32[7,16,128]{2,1,0:T(8,128)S(1)}, f32[3,7,16,128]{3,2,1,0:T(8,128)S(...) custom-call(f32[128,128]{1,0:T(8,128)S(1)} %get-tuple-element.37.t_ref, ...), custom_call_target="tpu_custom_call" | custom-call | tf_op jit(solution)/shard_map/front_kernel/pallas_call | solution.py:844
  18.3 7.9 %all-to-all-start = ((f32[16,136,128]{2,1,0:T(8,128)}), f32[16,136,128]{2,1,0:T(8,128)S(1)}, u32[]{:S(2)}, u32[]{:S(2)}) async-start(f32[16,136,128]{2,1,0:T(8,128)} %get-tuple-element.45), calls=%async_computation | async-start | bytes 2228224 | tf_op jit(solution)/shard_map/all_to_all | solution.py:827
  26.2 1.2 ahead_kernel.1
  27.3 1.8 %all-gather = f32[96,128]{1,0:T(8,128)S(1)} all-gather(f32[48,128]{1,0:T(8,128)S(1)} %get-tuple-element.44), channel_id=2, replica_groups={{0,16},{32,48},{64,80},{96,112},{128,144},{160,176},{192,208},{224,240}..., dimensions={0}, use_global_device_ids=true | all-gather | bytes 73728 | tf_op jit(solution)/shard_map/all_gather | solution.py:833
  29.2 1.3 %collective-permute-start.5 = (f32[8,128]{1,0:T(8,128)S(1)}, f32[8,128]{1,0:T(8,128)S(1)}, u32[]{:S(2)}, u32[]{:S(2)}) collective-permute-start(f32[8,128]{1,0:T(8,128)S(1)} %get-tuple-element.53.low_ref), channel_id=1, source_target_pairs={{32,0},{48,16},{64,32},{80,48},{96,64},{112,80},{128,96},{144,112}... | collective-permute-start | bytes 12296 | tf_op jit(solution)/shard_map/ppermute | solution.py:859
  30.5 4.2 %collective-permute-start.4 = (f32[8,128]{1,0:T(8,128)S(1)}, f32[8,128]{1,0:T(8,128)S(1)}, u32[]{:S(2)}, u32[]{:S(2)}) collective-permute-start(f32[8,128]{1,0:T(8,128)S(1)} %get-tuple-element.54.high_ref), channel_id=1, source_target_pairs={{0,32},{16,48},{32,64},{48,80},{64,96},{80,112},{96,128},{112,144}... | collective-permute-start | bytes 12296 | tf_op jit(solution)/shard_map/ppermute | solution.py:858
  34.7 9.0 %all-to-all-done.all_ref = f32[16,136,128]{2,1,0:T(8,128)S(1)} async-done(((f32[16,136,128]{2,1,0:T(8,128)}), f32[16,136,128]{2,1,0:T(8,128)S(1)}, u32[]{:S(2)}, u32[]{:S(2)}) %all-to-all-start) | async-done | bytes 1114144 | tf_op jit(solution)/shard_map/all_to_all | solution.py:827
  43.6 0.2 middle_kernel.1
  43.9 1.8 %all-gather.1 = f32[64,128]{1,0:T(8,128)S(1)} all-gather(f32[32,128]{1,0:T(8,128)S(1)} %get-tuple-element.51), channel_id=3, replica_groups={{0,16},{32,48},{64,80},{96,112},{128,144},{160,176},{192,208},{224,240}..., dimensions={0}, use_global_device_ids=true | all-gather | bytes 49152 | tf_op jit(solution)/shard_map/all_gather | solution.py:833
  45.7 0.0 collective-permute-done.5.from_high_ref
  45.7 0.0 collective-permute-done.4.from_low_ref
  45.7 0.5 merge_kernel.1
  46.2 29.9 %all_to_all.20.all_ref = f32[16,24,128]{2,1,0:T(8,128)S(1)} all-to-all(f32[16,24,128]{2,1,0:T(8,128)S(1)} %get-tuple-element.55), channel_id=1, replica_groups={{0,32,64,96,128,160,192,224,256,288,320,352,384,416,448,480},{16,48,80,..., dimensions={0} | all-to-all | bytes 393216 | tf_op jit(solution)/shard_map/all_to_all | solution.py:830
  76.1 0.1 chain_kernel.1
  76.2 4.8 %all-gather.2 = f32[32,128]{1,0:T(8,128)S(1)} all-gather(f32[16,128]{1,0:T(8,128)S(1)} %chain_kernel.1), channel_id=4, replica_groups={{0,16},{32,48},{64,80},{96,112},{128,144},{160,176},{192,208},{224,240}..., dimensions={0}, use_global_device_ids=true | all-gather | bytes 24576 | tf_op jit(solution)/shard_map/all_gather | solution.py:833
  81.0 2.1 %turn_kernel.1 = (f32[16,32,128]{2,1,0:T(8,128)S(1)}, f32[7,16,128]{2,1,0:T(8,128)S(1)}, f32[128,128]{1,0:T(8,128)S(1)}, f32[128,128]{1,0:T(8,128)}) custom-call(f32[2,48,128]{2,1,0:T(8,128)S(1)} %bitcast.12, f32[2,32,128]{2,1,0:T(8,128)S(1)} %bitcast.16, f32[2,16,128]{2,1,0:T(8,128)S(1)} %bitcast.19, f32[3,15,8,128]{3,2,1,0:T(8,128)S(1)} %get-tuple-element.49.co_z_ref, ...), custom_call_target="tpu_custom_call" | custom-call | tf_op jit(solution)/shard_map/turn_kernel/pallas_call | solution.py:880
  83.0 10.8 %all_to_all.21.more_ref = f32[16,32,128]{2,1,0:T(8,128)S(1)} all-to-all(f32[16,32,128]{2,1,0:T(8,128)S(1)} %get-tuple-element.63), channel_id=1, replica_groups=mesh['gz'=32,'gy'=16] {'gy'}, dimensions={0} | all-to-all | bytes 524288 | tf_op jit(solution)/shard_map/all_to_all | solution.py:827
  93.8 0.2 later_middle_kernel.1
  94.0 3.0 %all-gather.3 = f32[32,128]{1,0:T(8,128)S(1)} all-gather(f32[16,128]{1,0:T(8,128)S(1)} %get-tuple-element.67), channel_id=5, replica_groups={{0,16},{32,48},{64,80},{96,112},{128,144},{160,176},{192,208},{224,240}..., dimensions={0}, use_global_device_ids=true | all-gather | bytes 24576 | tf_op jit(solution)/shard_map/all_gather | solution.py:833
  96.9 0.3 later_merge_kernel.1
  97.2 17.2 %all_to_all.22.more_ref = f32[16,8,128]{2,1,0:T(8,128)S(1)} all-to-all(f32[16,8,128]{2,1,0:T(8,128)S(1)} %later_merge_kernel.1), channel_id=1, replica_groups={{0,32,64,96,128,160,192,224,256,288,320,352,384,416,448,480},{16,48,80,..., dimensions={0} | all-to-all | bytes 131072 | tf_op jit(solution)/shard_map/all_to_all | solution.py:830
  114.4 0.1 later_chain_kernel.1
  114.5 3.6 %all-gather.4 = f32[16,128]{1,0:T(8,128)S(1)} all-gather(f32[8,128]{1,0:T(8,128)S(1)} %later_chain_kernel.1), channel_id=6, replica_groups={{0,16},{32,48},{64,80},{96,112},{128,144},{160,176},{192,208},{224,240}..., dimensions={0}, use_global_device_ids=true | all-gather | bytes 12288 | tf_op jit(solution)/shard_map/all_gather | solution.py:833
  118.1 0.7 back_kernel.1
  (1 shorter events, 0.0 us)
Async XLA Ops:
  1.6 14.7 %collective-permute-start.2 = (f32[3,16,128]{2,1,0:T(8,128)S(1)}, f32[3,16,128]{2,1,0:T(8,128)S(1)}, u32[]{:S(2)}, u32[]{:S(2)}) collective-permute-start(f32[3,16,128]{2,1,0:T(8,128)S(1)} %get-tuple-element.41), channel_id=1, source_target_pairs={{0,1},{1,2},{2,3},{3,4},{4,5},{5,6},{6,7},{7,8},{8,9},{9,10},{10,1... | collective-permute-start | bytes 73736 | tf_op jit(solution)/shard_map/ppermute | solution.py:824
  5.6 10.7 %collective-permute-start.3 = (f32[3,16,128]{2,1,0:T(8,128)S(1)}, f32[3,16,128]{2,1,0:T(8,128)S(1)}, u32[]{:S(2)}, u32[]{:S(2)}) collective-permute-start(f32[3,16,128]{2,1,0:T(8,128)S(1)} %get-tuple-element.42), channel_id=1, source_target_pairs={{1,0},{2,1},{3,2},{4,3},{5,4},{6,5},{7,6},{8,7},{9,8},{10,9},{11,1... | collective-permute-start | bytes 73736 | tf_op jit(solution)/shard_map/ppermute | solution.py:824
  6.9 8.6 %collective-permute-start = (f32[3,8,128]{2,1,0:T(8,128)S(1)}, f32[3,8,128]{2,1,0:T(8,128)S(1)}, u32[]{:S(2)}, u32[]{:S(2)}) collective-permute-start(f32[3,8,128]{2,1,0:T(8,128)S(1)} %get-tuple-element.39), channel_id=1, source_target_pairs={{0,16},{16,32},{32,48},{48,64},{64,80},{80,96},{96,112},{112,128},... | collective-permute-start | bytes 36872 | tf_op jit(solution)/shard_map/ppermute | solution.py:823
  11.3 5.0 %collective-permute-start.1 = (f32[3,8,128]{2,1,0:T(8,128)S(1)}, f32[3,8,128]{2,1,0:T(8,128)S(1)}, u32[]{:S(2)}, u32[]{:S(2)}) collective-permute-start(f32[3,8,128]{2,1,0:T(8,128)S(1)} %get-tuple-element.40), channel_id=1, source_target_pairs={{16,0},{32,16},{48,32},{64,48},{80,64},{96,80},{112,96},{128,112},... | collective-permute-start | bytes 36872 | tf_op jit(solution)/shard_map/ppermute | solution.py:823
  18.3 25.4 %all-to-all-start = ((f32[16,136,128]{2,1,0:T(8,128)}), f32[16,136,128]{2,1,0:T(8,128)S(1)}, u32[]{:S(2)}, u32[]{:S(2)}) async-start(f32[16,136,128]{2,1,0:T(8,128)} %get-tuple-element.45), calls=%async_computation | async-start | bytes 2228224 | tf_op jit(solution)/shard_map/all_to_all | solution.py:827
  29.2 16.5 %collective-permute-start.5 = (f32[8,128]{1,0:T(8,128)S(1)}, f32[8,128]{1,0:T(8,128)S(1)}, u32[]{:S(2)}, u32[]{:S(2)}) collective-permute-start(f32[8,128]{1,0:T(8,128)S(1)} %get-tuple-element.53.low_ref), channel_id=1, source_target_pairs={{32,0},{48,16},{64,32},{80,48},{96,64},{112,80},{128,96},{144,112}... | collective-permute-start | bytes 12296 | tf_op jit(solution)/shard_map/ppermute | solution.py:859
  30.5 15.2 %collective-permute-start.4 = (f32[8,128]{1,0:T(8,128)S(1)}, f32[8,128]{1,0:T(8,128)S(1)}, u32[]{:S(2)}, u32[]{:S(2)}) collective-permute-start(f32[8,128]{1,0:T(8,128)S(1)} %get-tuple-element.54.high_ref), channel_id=1, source_target_pairs={{0,32},{16,48},{32,64},{48,80},{64,96},{80,112},{96,128},{112,144}... | collective-permute-start | bytes 12296 | tf_op jit(solution)/shard_map/ppermute | solution.py:858

commit v6 on v5

--- a/solution.py
+++ b/solution.py
@@ -190,14 +190,35 @@
     m_ref,
     below_ref,
     above_ref,
+    south_ref,
+    north_ref,
     x_ref,
     co1_ref,
     co2_ref,
     num_ref,
     entry_ref,
+    co_y_ref,
+    link_ref,
+    low_ref,
+    high_ref,
+    k_ref,
+    g_ref,
     *,
+    groups_y,
     groups_z,
 ):
+    m = m_ref[...]
+    k_ref[...] = conduct_of(m, next_c_ref[...])
+    g_ref[...] = store_of(m)
+    ks = [south_ref[2]] + [k_ref[y_rows(y), :] for y in range(YC)] + [north_ref[2]]
+    faces = [0.5 * (ks[i] + ks[i + 1]) for i in range(YC + 1)]
+    back_ground, edge, ground = reduce_coefficients(
+        YC, lambda i: g_ref[y_rows(i), :], lambda i: faces[i + 1], faces[0], co_y_ref
+    )
+    at_end = lax.axis_index("gy") == groups_y - 1
+    link_ref[...] = edge
+    low_ref[...] = back_ground + edge
+    high_ref[...] = ground + edge + jnp.where(at_end, faces[YC], 0.0)
     x_coefficients(next_c_ref, m_ref, x_ref)
     entry_ref[...] = z_coefficients(
         groups_z, c_ref, m_ref, below_ref[1], above_ref[1], co1_ref, num_ref, 0
@@ -274,7 +295,6 @@
     pay_ref,
     co1_ref,
     side_ref,
-    co2_ref,
     fluxz_ref,
     cure_ref,
     entry_ref,
@@ -306,17 +326,10 @@
     )
     ground = ground + jnp.where(at_end, face_y[YC], 0.0)
     side, back_side = reduce_sides(YC, lambda i: r_ref[y_rows(i), :], co1_ref, side_ref)
-    for y, row in ((0, 8 * ZC), (YC - 1, 8 * ZC + 4)):
+    for y, row in ((0, 5 * ZC), (YC - 1, 5 * ZC + 4)):
         for i, corner in enumerate((below_ref[0], above_ref[0], below_ref[1], above_ref[1])):
             p_ref[row + i : row + i + 1] = corner[y : y + 1]
-    k_ref[...] = conduct_of(m_ref[...], cure_ref[...])
-    ks = [south_ref[2]] + [k_ref[y_rows(y), :] for y in range(YC)] + [north_ref[2]]
-    faces = [0.5 * (ks[i] + ks[i + 1]) for i in range(YC + 1)]
-    back_ground2, edge2, ground2 = reduce_coefficients(
-        YC, lambda i: g_ref[y_rows(i), :], lambda i: faces[i + 1], faces[0], co2_ref
-    )
-    ground2 = ground2 + jnp.where(at_end, faces[YC], 0.0)
-    numbers = (back_ground, edge, ground, side, back_side, back_ground2, edge2, ground2)
+    numbers = (back_ground, edge, ground, side, back_side)
     for q, number in enumerate(numbers):
         p_ref[ZC * q : ZC * q + ZC] = number
     spread(p_ref, pay_ref, sem, groups)
@@ -363,21 +376,11 @@
     return own - (back_ground * own + edge * (own - after) - back_side) / entry
 
 
-def y_solution(groups_y, read, co_ref, side_ref, s_ref, v_ref):
-    s_ref[0] = jnp.zeros((ZC, XC), jnp.float32)
-
-    def put(j, value):
-        s_ref[j + 1] = value
-
-    chain(groups_y, read, put)
-    me = lax.axis_index("gy")
-
+def substitute_y(before, own, co_ref, side_ref, v_ref):
     def place(i, value):
         v_ref[y_rows(i), :] = value
 
-    before, own = s_ref[me], s_ref[me + 1]
     substitute(YC, before, own, co_ref, side_ref, place)
-    return before, own
 
 
 def block_rows(q):
@@ -412,7 +415,15 @@
     def read(j, q):
         return all_ref[j, ZC * q : ZC * q + ZC, :]
 
-    before, own = y_solution(groups_y, read, co_y_ref, side_y_ref, s_ref, v_ref)
+    s_ref[0] = jnp.zeros((ZC, XC), jnp.float32)
+
+    def put(j, value):
+        s_ref[j + 1] = value
+
+    chain(groups_y, read, put)
+    me = lax.axis_index("gy")
+    before, own = s_ref[me], s_ref[me + 1]
+    substitute_y(before, own, co_y_ref, side_y_ref, v_ref)
 
     def right(i):
         return store_of(m_ref[z_rows(i), :]) * v_ref[z_rows(i), :] - fluxz_ref[z_rows(i), :]
@@ -422,7 +433,6 @@
     p_ref[block_rows(0), :] = sides[0]
     p_ref[block_rows(1), :] = sides[1]
 
-    me = lax.axis_index("gy")
     then = jnp.minimum(me + 1, groups_y - 1)
     north = first_of_next(
         own,
@@ -434,8 +444,8 @@
     )
     last = jnp.maximum(me - 1, 0)
     beside = (
-        (0, before, south_ref, all_ref[last, 8 * ZC + 4 : 8 * ZC + 8, :]),
-        (1, north, north_ref, all_ref[then, 8 * ZC : 8 * ZC + 4, :]),
+        (0, before, south_ref, all_ref[last, 5 * ZC + 4 : 5 * ZC + 8, :]),
+        (1, north, north_ref, all_ref[then, 5 * ZC : 5 * ZC + 4, :]),
     )
     for side, value, halo_ref, corners in beside:
         rows = pl.ds(2 + side, ZC, stride=2)
@@ -470,7 +480,7 @@
 
 def later_middle_kernel(
     all_ref,
-    more_ref,
+    scale_ref,
     co_y_ref,
     side_y_ref,
     fluxz_ref,
@@ -483,12 +493,19 @@
     *,
     groups_y,
 ):
-    def read(j, q):
-        if q < 3:
-            return all_ref[j, ZC * (5 + q) : ZC * (6 + q), :]
-        return more_ref[j, ZC * (q - 3) : ZC * (q - 2), :]
-
-    y_solution(groups_y, read, co_y_ref, side_y_ref, s_ref, v_ref)
+    s_ref[0] = jnp.zeros((ZC, XC), jnp.float32)
+
+    def side_of(j):
+        side = all_ref[j, ZC : 2 * ZC, :]
+        return side + all_ref[j + 1, 2 * ZC : 3 * ZC, :] if j + 1 < groups_y else side
+
+    def put(j, value):
+        s_ref[j + 1] = value
+
+    unit_chain(groups_y, lambda j: all_ref[j, 0:ZC, :], side_of, put)
+    me = lax.axis_index("gy")
+    before, own = s_ref[me] * scale_ref[1], s_ref[me + 1] * scale_ref[0]
+    substitute_y(before, own, co_y_ref, side_y_ref, v_ref)
 
     def right(i):
         return store_of(m_ref[z_rows(i), :]) * v_ref[z_rows(i), :] - fluxz_ref[z_rows(i), :]
@@ -711,6 +728,11 @@
     m_ref,
     x_ref,
     co_y_ref,
+    link_ref,
+    low_ref,
+    high_ref,
+    from_low_ref,
+    from_high_ref,
     below_ref,
     above_ref,
     south_ref,
@@ -719,6 +741,7 @@
     side_y_ref,
     fluxz_ref,
     cure_ref,
+    scale_ref,
     u_ref,
     w_ref,
     t_ref,
@@ -773,8 +796,13 @@
         (k_ref, g_ref, fy_ref, r_ref),
     )
     side, back_side = reduce_sides(YC, lambda i: r_ref[y_rows(i), :], co_y_ref, side_y_ref)
-    p_ref[0:ZC] = side
-    p_ref[ZC : 2 * ZC] = back_side
+    own_inv = 1.0 / jnp.sqrt(high_ref[...] + from_high_ref[...])
+    last_inv = 1.0 / jnp.sqrt(from_low_ref[...] + low_ref[...])
+    scale_ref[0] = own_inv
+    scale_ref[1] = last_inv
+    p_ref[0:ZC] = link_ref[...] * (own_inv * last_inv)
+    p_ref[ZC : 2 * ZC] = side * own_inv
+    p_ref[2 * ZC : 3 * ZC] = back_side * last_inv
     spread(p_ref, pay_ref, sem, groups_y)
 
 
@@ -841,18 +869,20 @@
     line = (groups_y + 1, ZC, XC)
 
     (x1,) = call(x_kernel, [x_shape])(c, m)
-    pay, co_y1, side, co_y2, fluxz, c1, y_entry = call(
+    pay, co_y1, side, fluxz, c1, y_entry = call(
         front_kernel,
-        [f32(groups_y, 8 * ZC + 8, XC), co_y, side_y, co_y, block, block, f32(ZC, XC)],
-        [cells] * 4 + [(8 * ZC + 8, XC)],
+        [f32(groups_y, 5 * ZC + 8, XC), co_y, side_y, block, block, f32(ZC, XC)],
+        [cells] * 4 + [(5 * ZC + 8, XC)],
         spread_to=groups_y,
         groups=groups_y,
     )(t, c, m, x1, *z_halo, *y_halo)
-    x2, co_z1, co_z2, numbers, z_entry = call(
+    y_row = f32(ZC, XC)
+    x2, co_z1, co_z2, numbers, z_entry, co_y2, link_y, low_y, high_y = call(
         ahead_kernel,
-        [x_shape, co_z, co_z, f32(6 * YC, XC), f32(YC, XC)],
-        groups_z=groups_z,
-    )(c, c1, m, *z_halo)
+        [x_shape, co_z, co_z, f32(6 * YC, XC), f32(YC, XC), co_y, y_row, y_row, y_row],
+        [cells] * 2,
+        **sizes,
+    )(c, c1, m, *z_halo, *y_halo)
     coef = share(numbers)
     link, low, high = call(links_kernel, [f32(YC, XC)] * 3)(coef)
     from_low = lax.ppermute(high, "gz", next_chip)
@@ -872,15 +902,18 @@
         spread_to=chips,
         copies=chips,
     )(coef, pair, link, low, high, from_low, from_high)
+    pay, send_low, send_high = lax.optimization_barrier((pay, low_y, high_y))
     column = gather_z(pay)
+    from_south = lax.ppermute(send_high, "gy", up["gy"])
+    from_north = lax.ppermute(send_low, "gy", down["gy"])
     half_line = (chips + 1, HALF, XC)
     (found,) = call(
         chain_kernel, [f32(16, XC)], [half_line, (chips + 1, 1, XC)], chips=chips
     )(column, scale)
-    pay, side, fluxz, c2 = call(
+    pay, side, fluxz, c2, scale_y = call(
         turn_kernel,
-        [f32(groups_y, 2 * ZC, XC), side_y, block, block],
-        [(3, YC, XC), (2, 2, XC), cells, (2 * ZC, XC)] + [cells] * 4 + [(2 * ZC, XC)],
+        [f32(groups_y, 3 * ZC, XC), side_y, block, block, f32(2, ZC, XC)],
+        [(3, YC, XC), (2, 2, XC), cells, (2 * ZC, XC)] + [cells] * 4 + [(3 * ZC, XC)],
         spread_to=groups_y,
         **sizes,
     )(
@@ -896,12 +929,17 @@
         m,
         x2,
         co_y2,
+        link_y,
+        low_y,
+        high_y,
+        from_south,
+        from_north,
         *z_halo,
         *y_halo,
     )
     numbers, side = call(
         later_middle_kernel, [f32(2 * YC, XC), side_z], [line, cells], groups_y=groups_y
-    )(everyone, gather_y(pay), co_y2, side, fluxz, m, co_z2)
+    )(gather_y(pay), scale_y, co_y2, side, fluxz, m, co_z2)
     more = share(numbers)
     (pay,) = call(
         later_merge_kernel, [f32(chips, YC, XC)], [(YC, XC)], spread_to=chips, copies=chips

time: 119 us -> 116 us (0.975)
  blocking collectives: 72.9 us -> 45.1 us
  starting transfers between devices: 26 us -> 45.1 us
  waiting for transfers between devices: 9.79 us -> 14.9 us
    all_to_all x2 -> x1, blocking collectives: 47.1 us -> 15.7 us  [gather_z(): lax.all_to_all(pay, 'gz', 0, 0, tiled=True, axis_index_groups=same_core)]
    all_to_all x0 -> x1, starting transfers between devices: none -> 16 us  [gather_z(): lax.all_to_all(pay, 'gz', 0, 0, tiled=True, axis_index_groups=same_core)]
    all_to_all x0 -> x1, waiting for transfers between devices: none -> 9.87 us  [gather_z(): lax.all_to_all(pay, 'gz', 0, 0, tiled=True, axis_index_groups=same_core)]
    all_to_all x1, waiting for transfers between devices: 8.95 us -> 4.2 us  [gather_y(): return lax.all_to_all(pay, 'gy', 0, 0, tiled=True)]
    all_to_all x1, blocking collectives: 10.8 us -> 14.4 us  [gather_y(): return lax.all_to_all(pay, 'gy', 0, 0, tiled=True)]
    ppermute x0 -> x2, starting transfers between devices: none -> 3.04 us  [the longest x1 1.74 us: body(): from_south = lax.ppermute(send_high, 'gy', up['gy'])]
  transfers between devices with their start and end apart: 7 -> 10, of which waited for: 2 -> 3; matrix products, arithmetic and copies ran while one was open for 0% -> 0% of each run, Pallas kernels for 2% -> 2%
where the time goes in v6:
time: 116 us
  starting transfers between devices  45.1 us (39%)
  blocking collectives  45.1 us (39%)
  waiting for transfers between devices  14.9 us (13%)
  Pallas kernels  9.87 us (9%)
    all_to_all x1, starting transfers between devices, gather_z(): lax.all_to_all(pay, 'gz', 0, 0, tiled=True, axis_index_groups=same_core)  16 us
    all_to_all x1, blocking collectives, gather_z(): lax.all_to_all(pay, 'gz', 0, 0, tiled=True, axis_index_groups=same_core)  15.7 us
    all_gather x5, blocking collectives, share(): return lax.all_gather(numbers, 'gz', axis_index_groups=pairs)  15 us
    all_to_all x1, blocking collectives, gather_y(): return lax.all_to_all(pay, 'gy', 0, 0, tiled=True)  14.4 us
    all_to_all x1, waiting for transfers between devices, gather_z(): lax.all_to_all(pay, 'gz', 0, 0, tiled=True, axis_index_groups=same_core)  9.87 us
    all_to_all x1, starting transfers between devices, gather_y(): return lax.all_to_all(pay, 'gy', 0, 0, tiled=True)  7.92 us
    ppermute x1, starting transfers between devices, body(): lax.ppermute(zhi, 'gz', up['gz'])  4.39 us
    all_to_all x1, waiting for transfers between devices, gather_y(): return lax.all_to_all(pay, 'gy', 0, 0, tiled=True)  4.2 us
  transfers between devices with their start and end apart: 10, of which 3 were waited for; matrix products, arithmetic and copies ran while one was open for 0% of the time, Pallas kernels for 2%

profile of v6, /device:TPU:1, one launch (start us, length us, event | category | flops | bytes accessed | tf_op | source)
XLA Modules:
  0.0 115.8 jit_solution(13815563244838001671)
XLA Ops:
  0.6 1.0 edges_kernel.1
  1.6 3.9 %collective-permute-start.2 = (f32[3,16,128]{2,1,0:T(8,128)S(1)}, f32[3,16,128]{2,1,0:T(8,128)S(1)}, u32[]{:S(2)}, u32[]{:S(2)}) collective-permute-start(f32[3,16,128]{2,1,0:T(8,128)S(1)} %get-tuple-element.48), channel_id=1, source_target_pairs={{0,1},{1,2},{2,3},{3,4},{4,5},{5,6},{6,7},{7,8},{8,9},{9,10},{10,1... | collective-permute-start | bytes 73736 | tf_op jit(solution)/shard_map/ppermute | solution.py:852
  5.6 1.3 %collective-permute-start.3 = (f32[3,16,128]{2,1,0:T(8,128)S(1)}, f32[3,16,128]{2,1,0:T(8,128)S(1)}, u32[]{:S(2)}, u32[]{:S(2)}) collective-permute-start(f32[3,16,128]{2,1,0:T(8,128)S(1)} %get-tuple-element.49), channel_id=1, source_target_pairs={{1,0},{2,1},{3,2},{4,3},{5,4},{6,5},{7,6},{8,7},{9,8},{10,9},{11,1... | collective-permute-start | bytes 73736 | tf_op jit(solution)/shard_map/ppermute | solution.py:852
  6.9 4.4 %collective-permute-start = (f32[3,8,128]{2,1,0:T(8,128)S(1)}, f32[3,8,128]{2,1,0:T(8,128)S(1)}, u32[]{:S(2)}, u32[]{:S(2)}) collective-permute-start(f32[3,8,128]{2,1,0:T(8,128)S(1)} %get-tuple-element.46), channel_id=1, source_target_pairs={{0,16},{16,32},{32,48},{48,64},{64,80},{80,96},{96,112},{112,128},... | collective-permute-start | bytes 36872 | tf_op jit(solution)/shard_map/ppermute | solution.py:851
  11.3 3.0 %collective-permute-start.1 = (f32[3,8,128]{2,1,0:T(8,128)S(1)}, f32[3,8,128]{2,1,0:T(8,128)S(1)}, u32[]{:S(2)}, u32[]{:S(2)}) collective-permute-start(f32[3,8,128]{2,1,0:T(8,128)S(1)} %get-tuple-element.47), channel_id=1, source_target_pairs={{16,0},{32,16},{48,32},{64,48},{80,64},{96,80},{112,96},{128,112},... | collective-permute-start | bytes 36872 | tf_op jit(solution)/shard_map/ppermute | solution.py:851
  14.3 1.1 x_kernel.1.x_ref
  15.4 0.0 collective-permute-done.below_ref
  15.4 0.8 collective-permute-done.1.above_ref
  16.3 0.0 collective-permute-done.2.south_ref
  16.3 0.0 collective-permute-done.3.north_ref
  16.3 1.9 %front_kernel.1 = (f32[16,88,128]{2,1,0:T(8,128)}, f32[3,7,16,128]{3,2,1,0:T(8,128)S(1)}, f32[7,16,128]{2,1,0:T(8,128)S(1)}, f32[128,128]{1,0:T(8,128)S(1)}, f32...) custom-call(f32[128,128]{1,0:T(8,128)S(1)} %get-tuple-element.44.t_ref, f32[128,128]{1,0:T(8,128)S(1)} %get-tuple-element.43.c_ref, ...), custom_call_target="tpu_custom_call" | custom-call | tf_op jit(solution)/shard_map/front_kernel/pallas_call | solution.py:872
  18.1 7.9 %all-to-all-start = ((f32[16,88,128]{2,1,0:T(8,128)}), f32[16,88,128]{2,1,0:T(8,128)S(1)}, u32[]{:S(2)}, u32[]{:S(2)}) async-start(f32[16,88,128]{2,1,0:T(8,128)} %get-tuple-element.52), calls=%async_computation | async-start | bytes 1441792 | tf_op jit(solution)/shard_map/all_to_all | solution.py:855
  26.1 1.2 %ahead_kernel.1 = (f32[16,128,128]{2,1,0:T(8,128)S(1)}, f32[3,15,8,128]{3,2,1,0:T(8,128)S(1)}, f32[3,15,8,128]{3,2,1,0:T(8,128)S(1)}, f32[48,128]{1,0:T(8,128)S(...) custom-call(f32[128,128]{1,0:T(8,128)S(1)} %get-tuple-element.43.c_r, ...), custom_call_target="tpu_custom_call" | custom-call | tf_op jit(solution)/shard_map/ahead_kernel/pallas_call | solution.py:880
  27.2 1.8 %all-gather = f32[96,128]{1,0:T(8,128)S(1)} all-gather(f32[48,128]{1,0:T(8,128)S(1)} %get-tuple-element.51), channel_id=2, replica_groups={{0,16},{32,48},{64,80},{96,112},{128,144},{160,176},{192,208},{224,240}..., dimensions={0}, use_global_device_ids=true | all-gather | bytes 73728 | tf_op jit(solution)/shard_map/all_gather | solution.py:861
  29.1 1.3 %collective-permute-start.5 = (f32[8,128]{1,0:T(8,128)S(1)}, f32[8,128]{1,0:T(8,128)S(1)}, u32[]{:S(2)}, u32[]{:S(2)}) collective-permute-start(f32[8,128]{1,0:T(8,128)S(1)} %get-tuple-element.60.low_ref), channel_id=1, source_target_pairs={{32,0},{48,16},{64,32},{80,48},{96,64},{112,80},{128,96},{144,112}... | collective-permute-start | bytes 12296 | tf_op jit(solution)/shard_map/ppermute | solution.py:889
  30.4 4.2 %collective-permute-start.4 = (f32[8,128]{1,0:T(8,128)S(1)}, f32[8,128]{1,0:T(8,128)S(1)}, u32[]{:S(2)}, u32[]{:S(2)}) collective-permute-start(f32[8,128]{1,0:T(8,128)S(1)} %get-tuple-element.61.high_ref), channel_id=1, source_target_pairs={{0,32},{16,48},{32,64},{48,80},{64,96},{80,112},{96,128},{112,144}... | collective-permute-start | bytes 12296 | tf_op jit(solution)/shard_map/ppermute | solution.py:888
  34.6 4.2 %all-to-all-done.all_ref = f32[16,88,128]{2,1,0:T(8,128)S(1)} async-done(((f32[16,88,128]{2,1,0:T(8,128)}), f32[16,88,128]{2,1,0:T(8,128)S(1)}, u32[]{:S(2)}, u32[]{:S(2)}) %all-to-all-start) | async-done | bytes 720928 | tf_op jit(solution)/shard_map/all_to_all | solution.py:855
  38.8 0.2 middle_kernel.1
  39.0 1.8 %all-gather.1 = f32[64,128]{1,0:T(8,128)S(1)} all-gather(f32[32,128]{1,0:T(8,128)S(1)} %get-tuple-element.58), channel_id=3, replica_groups={{0,16},{32,48},{64,80},{96,112},{128,144},{160,176},{192,208},{224,240}..., dimensions={0}, use_global_device_ids=true | all-gather | bytes 49152 | tf_op jit(solution)/shard_map/all_gather | solution.py:861
  40.9 0.0 collective-permute-done.5.from_high_ref
  40.9 0.0 collective-permute-done.4.from_low_ref
  40.9 0.8 merge_kernel.1
  41.7 16.0 %all-to-all-start.1 = ((f32[16,24,128]{2,1,0:T(8,128)}), f32[16,24,128]{2,1,0:T(8,128)S(1)}, u32[]{:S(2)}, u32[]{:S(2)}) async-start(f32[16,24,128]{2,1,0:T(8,128)} %get-tuple-element.65), calls=%async_computation.1 | async-start | bytes 393216 | tf_op jit(solution)/shard_map/all_to_all | solution.py:858
  57.7 1.7 %collective-permute-start.6 = (f32[16,128]{1,0:T(8,128)S(1)}, f32[16,128]{1,0:T(8,128)S(1)}, u32[]{:S(2)}, u32[]{:S(2)}) collective-permute-start(f32[16,128]{1,0:T(8,128)S(1)} %get-tuple-element.74.high_ref), channel_id=1, source_target_pairs={{0,1},{1,2},{2,3},{3,4},{4,5},{5,6},{6,7},{7,8},{8,9},{9,10},{10,1... | collective-permute-start | bytes 24584 | tf_op jit(solution)/shard_map/ppermute | solution.py:907
  59.5 1.3 %collective-permute-start.7 = (f32[16,128]{1,0:T(8,128)S(1)}, f32[16,128]{1,0:T(8,128)S(1)}, u32[]{:S(2)}, u32[]{:S(2)}) collective-permute-start(f32[16,128]{1,0:T(8,128)S(1)} %get-tuple-element.75.low_ref), channel_id=1, source_target_pairs={{1,0},{2,1},{3,2},{4,3},{5,4},{6,5},{7,6},{8,7},{9,8},{10,9},{11,1... | collective-permute-start | bytes 24584 | tf_op jit(solution)/shard_map/ppermute | solution.py:908
  60.8 9.9 %all-to-all-done.1.all_ref = f32[16,24,128]{2,1,0:T(8,128)S(1)} async-done(((f32[16,24,128]{2,1,0:T(8,128)}), f32[16,24,128]{2,1,0:T(8,128)S(1)}, u32[]{:S(2)}, u32[]{:S(2)}) %all-to-all-start.1) | async-done | bytes 196640 | tf_op jit(solution)/shard_map/all_to_all | solution.py:858
  70.7 0.1 chain_kernel.1
  70.8 4.8 %all-gather.2 = f32[32,128]{1,0:T(8,128)S(1)} all-gather(f32[16,128]{1,0:T(8,128)S(1)} %chain_kernel.1), channel_id=4, replica_groups={{0,16},{32,48},{64,80},{96,112},{128,144},{160,176},{192,208},{224,240}..., dimensions={0}, use_global_device_ids=true | all-gather | bytes 24576 | tf_op jit(solution)/shard_map/all_gather | solution.py:861
  75.6 0.0 collective-permute-done.6.from_low_ref
  75.6 0.0 collective-permute-done.7.from_high_ref
  75.6 2.4 %turn_kernel.1 = (f32[16,48,128]{2,1,0:T(8,128)S(1)}, f32[7,16,128]{2,1,0:T(8,128)S(1)}, f32[128,128]{1,0:T(8,128)S(1)}, f32[128,128]{1,0:T(8,128)}, f32[2,16,128]{2,1,0:T(8,128)S(1)}) custom-call(f32[2,48,128]{2,1,0:T(8,128)S(1)} %bitcast.12, f32[2,32,128]{2,1,0:T(8,128)S(1)} %bitcast.16, f32[2,16,128]{2,1,0:T(8,128)S(1)} %bitcast.19, ...), custom_call_target="tpu_custom_call" | custom-call | tf_op jit(solution)/shard_map/turn_kernel/pallas_call | solution.py:913
  77.9 14.4 %all_to_all.20.all_ref = f32[16,48,128]{2,1,0:T(8,128)S(1)} all-to-all(f32[16,48,128]{2,1,0:T(8,128)S(1)} %get-tuple-element.76), channel_id=1, replica_groups=mesh['gz'=32,'gy'=16] {'gy'}, dimensions={0} | all-to-all | bytes 786432 | tf_op jit(solution)/shard_map/all_to_all | solution.py:855
  92.3 0.1 later_middle_kernel.1
  92.5 3.0 %all-gather.3 = f32[32,128]{1,0:T(8,128)S(1)} all-gather(f32[16,128]{1,0:T(8,128)S(1)} %get-tuple-element.81), channel_id=5, replica_groups={{0,16},{32,48},{64,80},{96,112},{128,144},{160,176},{192,208},{224,240}..., dimensions={0}, use_global_device_ids=true | all-gather | bytes 24576 | tf_op jit(solution)/shard_map/all_gather | solution.py:861
  95.4 0.3 later_merge_kernel.1
  95.7 15.7 %all_to_all.21.more_ref = f32[16,8,128]{2,1,0:T(8,128)S(1)} all-to-all(f32[16,8,128]{2,1,0:T(8,128)S(1)} %later_merge_kernel.1), channel_id=1, replica_groups={{0,32,64,96,128,160,192,224,256,288,320,352,384,416,448,480},{16,48,80,..., dimensions={0} | all-to-all | bytes 131072 | tf_op jit(solution)/shard_map/all_to_all | solution.py:858
  111.4 0.1 later_chain_kernel.1
  111.5 3.6 %all-gather.4 = f32[16,128]{1,0:T(8,128)S(1)} all-gather(f32[8,128]{1,0:T(8,128)S(1)} %later_chain_kernel.1), channel_id=6, replica_groups={{0,16},{32,48},{64,80},{96,112},{128,144},{160,176},{192,208},{224,240}..., dimensions={0}, use_global_device_ids=true | all-gather | bytes 12288 | tf_op jit(solution)/shard_map/all_gather | solution.py:861
  115.1 0.7 back_kernel.1
  (1 shorter events, 0.0 us)
Async XLA Ops:
  1.6 14.7 %collective-permute-start.2 = (f32[3,16,128]{2,1,0:T(8,128)S(1)}, f32[3,16,128]{2,1,0:T(8,128)S(1)}, u32[]{:S(2)}, u32[]{:S(2)}) collective-permute-start(f32[3,16,128]{2,1,0:T(8,128)S(1)} %get-tuple-element.48), channel_id=1, source_target_pairs={{0,1},{1,2},{2,3},{3,4},{4,5},{5,6},{6,7},{7,8},{8,9},{9,10},{10,1... | collective-permute-start | bytes 73736 | tf_op jit(solution)/shard_map/ppermute | solution.py:852
  5.6 10.7 %collective-permute-start.3 = (f32[3,16,128]{2,1,0:T(8,128)S(1)}, f32[3,16,128]{2,1,0:T(8,128)S(1)}, u32[]{:S(2)}, u32[]{:S(2)}) collective-permute-start(f32[3,16,128]{2,1,0:T(8,128)S(1)} %get-tuple-element.49), channel_id=1, source_target_pairs={{1,0},{2,1},{3,2},{4,3},{5,4},{6,5},{7,6},{8,7},{9,8},{10,9},{11,1... | collective-permute-start | bytes 73736 | tf_op jit(solution)/shard_map/ppermute | solution.py:852
  6.9 8.6 %collective-permute-start = (f32[3,8,128]{2,1,0:T(8,128)S(1)}, f32[3,8,128]{2,1,0:T(8,128)S(1)}, u32[]{:S(2)}, u32[]{:S(2)}) collective-permute-start(f32[3,8,128]{2,1,0:T(8,128)S(1)} %get-tuple-element.46), channel_id=1, source_target_pairs={{0,16},{16,32},{32,48},{48,64},{64,80},{80,96},{96,112},{112,128},... | collective-permute-start | bytes 36872 | tf_op jit(solution)/shard_map/ppermute | solution.py:851
  11.3 5.0 %collective-permute-start.1 = (f32[3,8,128]{2,1,0:T(8,128)S(1)}, f32[3,8,128]{2,1,0:T(8,128)S(1)}, u32[]{:S(2)}, u32[]{:S(2)}) collective-permute-start(f32[3,8,128]{2,1,0:T(8,128)S(1)} %get-tuple-element.47), channel_id=1, source_target_pairs={{16,0},{32,16},{48,32},{64,48},{80,64},{96,80},{112,96},{128,112},... | collective-permute-start | bytes 36872 | tf_op jit(solution)/shard_map/ppermute | solution.py:851
  18.1 20.6 %all-to-all-start = ((f32[16,88,128]{2,1,0:T(8,128)}), f32[16,88,128]{2,1,0:T(8,128)S(1)}, u32[]{:S(2)}, u32[]{:S(2)}) async-start(f32[16,88,128]{2,1,0:T(8,128)} %get-tuple-element.52), calls=%async_computation | async-start | bytes 1441792 | tf_op jit(solution)/shard_map/all_to_all | solution.py:855
  29.1 11.8 %collective-permute-start.5 = (f32[8,128]{1,0:T(8,128)S(1)}, f32[8,128]{1,0:T(8,128)S(1)}, u32[]{:S(2)}, u32[]{:S(2)}) collective-permute-start(f32[8,128]{1,0:T(8,128)S(1)} %get-tuple-element.60.low_ref), channel_id=1, source_target_pairs={{32,0},{48,16},{64,32},{80,48},{96,64},{112,80},{128,96},{144,112}... | collective-permute-start | bytes 12296 | tf_op jit(solution)/shard_map/ppermute | solution.py:889
  30.4 10.5 %collective-permute-start.4 = (f32[8,128]{1,0:T(8,128)S(1)}, f32[8,128]{1,0:T(8,128)S(1)}, u32[]{:S(2)}, u32[]{:S(2)}) collective-permute-start(f32[8,128]{1,0:T(8,128)S(1)} %get-tuple-element.61.high_ref), channel_id=1, source_target_pairs={{0,32},{16,48},{32,64},{48,80},{64,96},{80,112},{96,128},{112,144}... | collective-permute-start | bytes 12296 | tf_op jit(solution)/shard_map/ppermute | solution.py:888
  41.7 28.9 %all-to-all-start.1 = ((f32[16,24,128]{2,1,0:T(8,128)}), f32[16,24,128]{2,1,0:T(8,128)S(1)}, u32[]{:S(2)}, u32[]{:S(2)}) async-start(f32[16,24,128]{2,1,0:T(8,128)} %get-tuple-element.65), calls=%async_computation.1 | async-start | bytes 393216 | tf_op jit(solution)/shard_map/all_to_all | solution.py:858
  57.7 17.8 %collective-permute-start.6 = (f32[16,128]{1,0:T(8,128)S(1)}, f32[16,128]{1,0:T(8,128)S(1)}, u32[]{:S(2)}, u32[]{:S(2)}) collective-permute-start(f32[16,128]{1,0:T(8,128)S(1)} %get-tuple-element.74.high_ref), channel_id=1, source_target_pairs={{0,1},{1,2},{2,3},{3,4},{4,5},{5,6},{6,7},{7,8},{8,9},{9,10},{10,1... | collective-permute-start | bytes 24584 | tf_op jit(solution)/shard_map/ppermute | solution.py:907
  59.5 16.1 %collective-permute-start.7 = (f32[16,128]{1,0:T(8,128)S(1)}, f32[16,128]{1,0:T(8,128)S(1)}, u32[]{:S(2)}, u32[]{:S(2)}) collective-permute-start(f32[16,128]{1,0:T(8,128)S(1)} %get-tuple-element.75.low_ref), channel_id=1, source_target_pairs={{1,0},{2,1},{3,2},{4,3},{5,4},{6,5},{7,6},{8,7},{9,8},{10,9},{11,1... | collective-permute-start | bytes 24584 | tf_op jit(solution)/shard_map/ppermute | solution.py:908

commit v7 on v6

--- a/solution.py
+++ b/solution.py
@@ -184,19 +184,33 @@
     return faces[ZC]
 
 
-def ahead_kernel(
+def columns_kernel(
     c_ref,
     next_c_ref,
     m_ref,
     below_ref,
     above_ref,
-    south_ref,
-    north_ref,
-    x_ref,
     co1_ref,
     co2_ref,
     num_ref,
     entry_ref,
+    *,
+    groups_z,
+):
+    entry_ref[...] = z_coefficients(
+        groups_z, c_ref, m_ref, below_ref[1], above_ref[1], co1_ref, num_ref, 0
+    )
+    z_coefficients(
+        groups_z, next_c_ref, m_ref, below_ref[2], above_ref[2], co2_ref, num_ref, 3 * YC
+    )
+
+
+def ahead_kernel(
+    next_c_ref,
+    m_ref,
+    south_ref,
+    north_ref,
+    x_ref,
     co_y_ref,
     link_ref,
     low_ref,
@@ -205,7 +219,6 @@
     g_ref,
     *,
     groups_y,
-    groups_z,
 ):
     m = m_ref[...]
     k_ref[...] = conduct_of(m, next_c_ref[...])
@@ -220,12 +233,6 @@
     low_ref[...] = back_ground + edge
     high_ref[...] = ground + edge + jnp.where(at_end, faces[YC], 0.0)
     x_coefficients(next_c_ref, m_ref, x_ref)
-    entry_ref[...] = z_coefficients(
-        groups_z, c_ref, m_ref, below_ref[1], above_ref[1], co1_ref, num_ref, 0
-    )
-    z_coefficients(
-        groups_z, next_c_ref, m_ref, below_ref[2], above_ref[2], co2_ref, num_ref, 3 * YC
-    )
 
 
 def flow_rhs(t_ref, c_ref, m_ref, x_ref, zt, yt, zk, yk, outs, scratch):
@@ -876,17 +883,22 @@
         spread_to=groups_y,
         groups=groups_y,
     )(t, c, m, x1, *z_halo, *y_halo)
-    y_row = f32(ZC, XC)
-    x2, co_z1, co_z2, numbers, z_entry, co_y2, link_y, low_y, high_y = call(
-        ahead_kernel,
-        [x_shape, co_z, co_z, f32(6 * YC, XC), f32(YC, XC), co_y, y_row, y_row, y_row],
-        [cells] * 2,
-        **sizes,
-    )(c, c1, m, *z_halo, *y_halo)
+    co_z1, co_z2, numbers, z_entry = call(
+        columns_kernel,
+        [co_z, co_z, f32(6 * YC, XC), f32(YC, XC)],
+        groups_z=groups_z,
+    )(c, c1, m, *z_halo)
     coef = share(numbers)
     link, low, high = call(links_kernel, [f32(YC, XC)] * 3)(coef)
     from_low = lax.ppermute(high, "gz", next_chip)
     from_high = lax.ppermute(low, "gz", last_chip)
+    y_row = f32(ZC, XC)
+    x2, co_y2, link_y, low_y, high_y = call(
+        ahead_kernel,
+        [x_shape, co_y, y_row, y_row, y_row],
+        [cells] * 2,
+        groups_y=groups_y,
+    )(c1, m, *y_halo)
     everyone = gather_y(pay)
     numbers, side, co_wide, side_wide = call(
         middle_kernel,

time: 116 us -> 116 us (level)
  no operation moved by 1% of the time
where the time goes in v7:
time: 116 us; the launch traced here: 115 us
  starting transfers between devices  45.1 us (39%)
  blocking collectives  44.8 us (39%)
  waiting for transfers between devices  14.7 us (13%)
  Pallas kernels  10 us (9%)
    all_to_all x1, blocking collectives, gather_z(): lax.all_to_all(pay, 'gz', 0, 0, tiled=True, axis_index_groups=same_core)  16.3 us
    all_to_all x1, starting transfers between devices, gather_z(): lax.all_to_all(pay, 'gz', 0, 0, tiled=True, axis_index_groups=same_core)  16 us
    all_gather x5, blocking collectives, share(): return lax.all_gather(numbers, 'gz', axis_index_groups=pairs)  15 us
    all_to_all x1, blocking collectives, gather_y(): return lax.all_to_all(pay, 'gy', 0, 0, tiled=True)  13.5 us
    all_to_all x1, waiting for transfers between devices, gather_z(): lax.all_to_all(pay, 'gz', 0, 0, tiled=True, axis_index_groups=same_core)  9.87 us
    all_to_all x1, starting transfers between devices, gather_y(): return lax.all_to_all(pay, 'gy', 0, 0, tiled=True)  7.92 us
    ppermute x1, starting transfers between devices, body(): lax.ppermute(zhi, 'gz', up['gz'])  4.39 us
    ppermute x1, starting transfers between devices, body(): from_low = lax.ppermute(high, 'gz', next_chip)  4.17 us
  transfers between devices with their start and end apart: 10, of which 3 were waited for; matrix products, arithmetic and copies ran while one was open for 0% of the time, Pallas kernels for 2%

profile of v7, /device:TPU:1, one launch (start us, length us, event | category | flops | bytes accessed | tf_op | source)
XLA Modules:
  0.0 115.5 jit_solution(4631030715932900219)
XLA Ops:
  0.6 1.0 edges_kernel.1
  1.6 3.9 %collective-permute-start.2 = (f32[3,16,128]{2,1,0:T(8,128)S(1)}, f32[3,16,128]{2,1,0:T(8,128)S(1)}, u32[]{:S(2)}, u32[]{:S(2)}) collective-permute-start(f32[3,16,128]{2,1,0:T(8,128)S(1)} %get-tuple-element.48), channel_id=1, source_target_pairs={{0,1},{1,2},{2,3},{3,4},{4,5},{5,6},{6,7},{7,8},{8,9},{9,10},{10,1... | collective-permute-start | bytes 73736 | tf_op jit(solution)/shard_map/ppermute | solution.py:859
  5.6 1.3 %collective-permute-start.3 = (f32[3,16,128]{2,1,0:T(8,128)S(1)}, f32[3,16,128]{2,1,0:T(8,128)S(1)}, u32[]{:S(2)}, u32[]{:S(2)}) collective-permute-start(f32[3,16,128]{2,1,0:T(8,128)S(1)} %get-tuple-element.49), channel_id=1, source_target_pairs={{1,0},{2,1},{3,2},{4,3},{5,4},{6,5},{7,6},{8,7},{9,8},{10,9},{11,1... | collective-permute-start | bytes 73736 | tf_op jit(solution)/shard_map/ppermute | solution.py:859
  6.9 4.4 %collective-permute-start = (f32[3,8,128]{2,1,0:T(8,128)S(1)}, f32[3,8,128]{2,1,0:T(8,128)S(1)}, u32[]{:S(2)}, u32[]{:S(2)}) collective-permute-start(f32[3,8,128]{2,1,0:T(8,128)S(1)} %get-tuple-element.46), channel_id=1, source_target_pairs={{0,16},{16,32},{32,48},{48,64},{64,80},{80,96},{96,112},{112,128},... | collective-permute-start | bytes 36872 | tf_op jit(solution)/shard_map/ppermute | solution.py:858
  11.3 3.0 %collective-permute-start.1 = (f32[3,8,128]{2,1,0:T(8,128)S(1)}, f32[3,8,128]{2,1,0:T(8,128)S(1)}, u32[]{:S(2)}, u32[]{:S(2)}) collective-permute-start(f32[3,8,128]{2,1,0:T(8,128)S(1)} %get-tuple-element.47), channel_id=1, source_target_pairs={{16,0},{32,16},{48,32},{64,48},{80,64},{96,80},{112,96},{128,112},... | collective-permute-start | bytes 36872 | tf_op jit(solution)/shard_map/ppermute | solution.py:858
  14.3 1.1 x_kernel.1.x_ref
  15.4 0.0 collective-permute-done.below_ref
  15.4 0.8 collective-permute-done.1.above_ref
  16.3 0.0 collective-permute-done.2.south_ref
  16.3 0.0 collective-permute-done.3.north_ref
  16.3 1.9 %front_kernel.1 = (f32[16,88,128]{2,1,0:T(8,128)}, f32[3,7,16,128]{3,2,1,0:T(8,128)S(1)}, f32[7,16,128]{2,1,0:T(8,128)S(1)}, f32[128,128]{1,0:T(8,128)S(1)}, f32...) custom-call(f32[128,128]{1,0:T(8,128)S(1)} %get-tuple-element.44.t_ref, f32[128,128]{1,0:T(8,128)S(1)} %get-tuple-element.43.c_ref, ...), custom_call_target="tpu_custom_call" | custom-call | tf_op jit(solution)/shard_map/front_kernel/pallas_call | solution.py:879
  18.1 7.9 %all-to-all-start = ((f32[16,88,128]{2,1,0:T(8,128)}), f32[16,88,128]{2,1,0:T(8,128)S(1)}, u32[]{:S(2)}, u32[]{:S(2)}) async-start(f32[16,88,128]{2,1,0:T(8,128)} %get-tuple-element.52), calls=%async_computation | async-start | bytes 1441792 | tf_op jit(solution)/shard_map/all_to_all | solution.py:862
  26.1 0.2 columns_kernel.1
  26.2 1.8 %all-gather = f32[96,128]{1,0:T(8,128)S(1)} all-gather(f32[48,128]{1,0:T(8,128)S(1)} %get-tuple-element.51), channel_id=2, replica_groups={{0,16},{32,48},{64,80},{96,112},{128,144},{160,176},{192,208},{224,240}..., dimensions={0}, use_global_device_ids=true | all-gather | bytes 73728 | tf_op jit(solution)/shard_map/all_gather | solution.py:868
  28.1 1.3 %collective-permute-start.5 = (f32[8,128]{1,0:T(8,128)S(1)}, f32[8,128]{1,0:T(8,128)S(1)}, u32[]{:S(2)}, u32[]{:S(2)}) collective-permute-start(f32[8,128]{1,0:T(8,128)S(1)} %get-tuple-element.60.low_ref), channel_id=1, source_target_pairs={{32,0},{48,16},{64,32},{80,48},{96,64},{112,80},{128,96},{144,112}... | collective-permute-start | bytes 12296 | tf_op jit(solution)/shard_map/ppermute | solution.py:894
  29.4 4.2 %collective-permute-start.4 = (f32[8,128]{1,0:T(8,128)S(1)}, f32[8,128]{1,0:T(8,128)S(1)}, u32[]{:S(2)}, u32[]{:S(2)}) collective-permute-start(f32[8,128]{1,0:T(8,128)S(1)} %get-tuple-element.61.high_ref), channel_id=1, source_target_pairs={{0,32},{16,48},{32,64},{48,80},{64,96},{80,112},{96,128},{112,144}... | collective-permute-start | bytes 12296 | tf_op jit(solution)/shard_map/ppermute | solution.py:893
  33.6 1.2 %ahead_kernel.1 = (f32[16,128,128]{2,1,0:T(8,128)S(1)}, f32[3,7,16,128]{3,2,1,0:T(8,128)S(1)}, f32[16,128]{1,0:T(8,128)S(1)}, f32[16,128]{1,0:T(8,128)S(1)}, f32[16,128]{1,0:T(8,128)S(1)}) custom-call(f32[128,128]{1,0:T(8,128)S(1)} %get-tuple-element.50.next_c_ref.c_ref, s32[128,128]{1,0:T(8,128)S(1)} %get-tuple-element.45.m_ref, ...), custom_call_target="tpu_custom_call" | custom-call | tf_op jit(solution)/shard_map/ahead_kernel/pallas_call | solution.py:896
  34.7 4.0 %all-to-all-done.all_ref = f32[16,88,128]{2,1,0:T(8,128)S(1)} async-done(((f32[16,88,128]{2,1,0:T(8,128)}), f32[16,88,128]{2,1,0:T(8,128)S(1)}, u32[]{:S(2)}, u32[]{:S(2)}) %all-to-all-start) | async-done | bytes 720928 | tf_op jit(solution)/shard_map/all_to_all | solution.py:862
  38.8 0.2 middle_kernel.1
  39.0 1.8 %all-gather.1 = f32[64,128]{1,0:T(8,128)S(1)} all-gather(f32[32,128]{1,0:T(8,128)S(1)} %get-tuple-element.58), channel_id=3, replica_groups={{0,16},{32,48},{64,80},{96,112},{128,144},{160,176},{192,208},{224,240}..., dimensions={0}, use_global_device_ids=true | all-gather | bytes 49152 | tf_op jit(solution)/shard_map/all_gather | solution.py:868
  40.9 0.0 collective-permute-done.5.from_high_ref
  40.9 0.0 collective-permute-done.4.from_low_ref
  40.9 0.8 merge_kernel.1
  41.7 16.0 %all-to-all-start.1 = ((f32[16,24,128]{2,1,0:T(8,128)}), f32[16,24,128]{2,1,0:T(8,128)S(1)}, u32[]{:S(2)}, u32[]{:S(2)}) async-start(f32[16,24,128]{2,1,0:T(8,128)} %get-tuple-element.65), calls=%async_computation.1 | async-start | bytes 393216 | tf_op jit(solution)/shard_map/all_to_all | solution.py:865
  57.7 1.7 %collective-permute-start.6 = (f32[16,128]{1,0:T(8,128)S(1)}, f32[16,128]{1,0:T(8,128)S(1)}, u32[]{:S(2)}, u32[]{:S(2)}) collective-permute-start(f32[16,128]{1,0:T(8,128)S(1)} %get-tuple-element.74.high_ref), channel_id=1, source_target_pairs={{0,1},{1,2},{2,3},{3,4},{4,5},{5,6},{6,7},{7,8},{8,9},{9,10},{10,1... | collective-permute-start | bytes 24584 | tf_op jit(solution)/shard_map/ppermute | solution.py:919
  59.5 1.3 %collective-permute-start.7 = (f32[16,128]{1,0:T(8,128)S(1)}, f32[16,128]{1,0:T(8,128)S(1)}, u32[]{:S(2)}, u32[]{:S(2)}) collective-permute-start(f32[16,128]{1,0:T(8,128)S(1)} %get-tuple-element.75.low_ref), channel_id=1, source_target_pairs={{1,0},{2,1},{3,2},{4,3},{5,4},{6,5},{7,6},{8,7},{9,8},{10,9},{11,1... | collective-permute-start | bytes 24584 | tf_op jit(solution)/shard_map/ppermute | solution.py:920
  60.8 9.9 %all-to-all-done.1.all_ref = f32[16,24,128]{2,1,0:T(8,128)S(1)} async-done(((f32[16,24,128]{2,1,0:T(8,128)}), f32[16,24,128]{2,1,0:T(8,128)S(1)}, u32[]{:S(2)}, u32[]{:S(2)}) %all-to-all-start.1) | async-done | bytes 196640 | tf_op jit(solution)/shard_map/all_to_all | solution.py:865
  70.7 0.1 chain_kernel.1
  70.8 4.8 %all-gather.2 = f32[32,128]{1,0:T(8,128)S(1)} all-gather(f32[16,128]{1,0:T(8,128)S(1)} %chain_kernel.1), channel_id=4, replica_groups={{0,16},{32,48},{64,80},{96,112},{128,144},{160,176},{192,208},{224,240}..., dimensions={0}, use_global_device_ids=true | all-gather | bytes 24576 | tf_op jit(solution)/shard_map/all_gather | solution.py:868
  75.5 0.0 collective-permute-done.6.from_low_ref
  75.5 0.0 collective-permute-done.7.from_high_ref
  75.5 2.4 %turn_kernel.1 = (f32[16,48,128]{2,1,0:T(8,128)S(1)}, f32[7,16,128]{2,1,0:T(8,128)S(1)}, f32[128,128]{1,0:T(8,128)S(1)}, f32[128,128]{1,0:T(8,128)}, f32[2,16,128]{2,1,0:T(8,128)S(1)}) custom-call(f32[2,48,128]{2,1,0:T(8,128)S(1)} %bitcast.12, f32[2,32,128]{2,1,0:T(8,128)S(1)} %bitcast.16, f32[2,16,128]{2,1,0:T(8,128)S(1)} %bitcast.19, ...), custom_call_target="tpu_custom_call" | custom-call | tf_op jit(solution)/shard_map/turn_kernel/pallas_call | solution.py:925
  77.9 13.5 %all_to_all.20.all_ref = f32[16,48,128]{2,1,0:T(8,128)S(1)} all-to-all(f32[16,48,128]{2,1,0:T(8,128)S(1)} %get-tuple-element.76), channel_id=1, replica_groups=mesh['gz'=32,'gy'=16] {'gy'}, dimensions={0} | all-to-all | bytes 786432 | tf_op jit(solution)/shard_map/all_to_all | solution.py:862
  91.4 0.1 later_middle_kernel.1
  91.6 3.0 %all-gather.3 = f32[32,128]{1,0:T(8,128)S(1)} all-gather(f32[16,128]{1,0:T(8,128)S(1)} %get-tuple-element.81), channel_id=5, replica_groups={{0,16},{32,48},{64,80},{96,112},{128,144},{160,176},{192,208},{224,240}..., dimensions={0}, use_global_device_ids=true | all-gather | bytes 24576 | tf_op jit(solution)/shard_map/all_gather | solution.py:868
  94.5 0.3 later_merge_kernel.1
  94.8 16.3 %all_to_all.21.more_ref = f32[16,8,128]{2,1,0:T(8,128)S(1)} all-to-all(f32[16,8,128]{2,1,0:T(8,128)S(1)} %later_merge_kernel.1), channel_id=1, replica_groups={{0,32,64,96,128,160,192,224,256,288,320,352,384,416,448,480},{16,48,80,..., dimensions={0} | all-to-all | bytes 131072 | tf_op jit(solution)/shard_map/all_to_all | solution.py:865
  111.1 0.1 later_chain_kernel.1
  111.2 3.6 %all-gather.4 = f32[16,128]{1,0:T(8,128)S(1)} all-gather(f32[8,128]{1,0:T(8,128)S(1)} %later_chain_kernel.1), channel_id=6, replica_groups={{0,16},{32,48},{64,80},{96,112},{128,144},{160,176},{192,208},{224,240}..., dimensions={0}, use_global_device_ids=true | all-gather | bytes 12288 | tf_op jit(solution)/shard_map/all_gather | solution.py:868
  114.8 0.7 back_kernel.1
  (1 shorter events, 0.0 us)
Async XLA Ops:
  1.6 14.7 %collective-permute-start.2 = (f32[3,16,128]{2,1,0:T(8,128)S(1)}, f32[3,16,128]{2,1,0:T(8,128)S(1)}, u32[]{:S(2)}, u32[]{:S(2)}) collective-permute-start(f32[3,16,128]{2,1,0:T(8,128)S(1)} %get-tuple-element.48), channel_id=1, source_target_pairs={{0,1},{1,2},{2,3},{3,4},{4,5},{5,6},{6,7},{7,8},{8,9},{9,10},{10,1... | collective-permute-start | bytes 73736 | tf_op jit(solution)/shard_map/ppermute | solution.py:859
  5.6 10.7 %collective-permute-start.3 = (f32[3,16,128]{2,1,0:T(8,128)S(1)}, f32[3,16,128]{2,1,0:T(8,128)S(1)}, u32[]{:S(2)}, u32[]{:S(2)}) collective-permute-start(f32[3,16,128]{2,1,0:T(8,128)S(1)} %get-tuple-element.49), channel_id=1, source_target_pairs={{1,0},{2,1},{3,2},{4,3},{5,4},{6,5},{7,6},{8,7},{9,8},{10,9},{11,1... | collective-permute-start | bytes 73736 | tf_op jit(solution)/shard_map/ppermute | solution.py:859
  6.9 8.6 %collective-permute-start = (f32[3,8,128]{2,1,0:T(8,128)S(1)}, f32[3,8,128]{2,1,0:T(8,128)S(1)}, u32[]{:S(2)}, u32[]{:S(2)}) collective-permute-start(f32[3,8,128]{2,1,0:T(8,128)S(1)} %get-tuple-element.46), channel_id=1, source_target_pairs={{0,16},{16,32},{32,48},{48,64},{64,80},{80,96},{96,112},{112,128},... | collective-permute-start | bytes 36872 | tf_op jit(solution)/shard_map/ppermute | solution.py:858
  11.3 5.0 %collective-permute-start.1 = (f32[3,8,128]{2,1,0:T(8,128)S(1)}, f32[3,8,128]{2,1,0:T(8,128)S(1)}, u32[]{:S(2)}, u32[]{:S(2)}) collective-permute-start(f32[3,8,128]{2,1,0:T(8,128)S(1)} %get-tuple-element.47), channel_id=1, source_target_pairs={{16,0},{32,16},{48,32},{64,48},{80,64},{96,80},{112,96},{128,112},... | collective-permute-start | bytes 36872 | tf_op jit(solution)/shard_map/ppermute | solution.py:858
  18.1 20.6 %all-to-all-start = ((f32[16,88,128]{2,1,0:T(8,128)}), f32[16,88,128]{2,1,0:T(8,128)S(1)}, u32[]{:S(2)}, u32[]{:S(2)}) async-start(f32[16,88,128]{2,1,0:T(8,128)} %get-tuple-element.52), calls=%async_computation | async-start | bytes 1441792 | tf_op jit(solution)/shard_map/all_to_all | solution.py:862
  28.1 12.8 %collective-permute-start.5 = (f32[8,128]{1,0:T(8,128)S(1)}, f32[8,128]{1,0:T(8,128)S(1)}, u32[]{:S(2)}, u32[]{:S(2)}) collective-permute-start(f32[8,128]{1,0:T(8,128)S(1)} %get-tuple-element.60.low_ref), channel_id=1, source_target_pairs={{32,0},{48,16},{64,32},{80,48},{96,64},{112,80},{128,96},{144,112}... | collective-permute-start | bytes 12296 | tf_op jit(solution)/shard_map/ppermute | solution.py:894
  29.4 11.5 %collective-permute-start.4 = (f32[8,128]{1,0:T(8,128)S(1)}, f32[8,128]{1,0:T(8,128)S(1)}, u32[]{:S(2)}, u32[]{:S(2)}) collective-permute-start(f32[8,128]{1,0:T(8,128)S(1)} %get-tuple-element.61.high_ref), channel_id=1, source_target_pairs={{0,32},{16,48},{32,64},{48,80},{64,96},{80,112},{96,128},{112,144}... | collective-permute-start | bytes 12296 | tf_op jit(solution)/shard_map/ppermute | solution.py:893
  41.7 28.9 %all-to-all-start.1 = ((f32[16,24,128]{2,1,0:T(8,128)}), f32[16,24,128]{2,1,0:T(8,128)S(1)}, u32[]{:S(2)}, u32[]{:S(2)}) async-start(f32[16,24,128]{2,1,0:T(8,128)} %get-tuple-element.65), calls=%async_computation.1 | async-start | bytes 393216 | tf_op jit(solution)/shard_map/all_to_all | solution.py:865
  57.7 17.8 %collective-permute-start.6 = (f32[16,128]{1,0:T(8,128)S(1)}, f32[16,128]{1,0:T(8,128)S(1)}, u32[]{:S(2)}, u32[]{:S(2)}) collective-permute-start(f32[16,128]{1,0:T(8,128)S(1)} %get-tuple-element.74.high_ref), channel_id=1, source_target_pairs={{0,1},{1,2},{2,3},{3,4},{4,5},{5,6},{6,7},{7,8},{8,9},{9,10},{10,1... | collective-permute-start | bytes 24584 | tf_op jit(solution)/shard_map/ppermute | solution.py:919
  59.5 16.1 %collective-permute-start.7 = (f32[16,128]{1,0:T(8,128)S(1)}, f32[16,128]{1,0:T(8,128)S(1)}, u32[]{:S(2)}, u32[]{:S(2)}) collective-permute-start(f32[16,128]{1,0:T(8,128)S(1)} %get-tuple-element.75.low_ref), channel_id=1, source_target_pairs={{1,0},{2,1},{3,2},{4,3},{5,4},{6,5},{7,6},{8,7},{9,8},{10,9},{11,1... | collective-permute-start | bytes 24584 | tf_op jit(solution)/shard_map/ppermute | solution.py:920

commit v8 on v6

--- a/solution.py
+++ b/solution.py
@@ -144,18 +144,16 @@
                 rows = z_rows(z0 + b)
                 ground, left, right = gs[b], ls[b], rs[b]
                 inv = 1.0 / (ground + left + right)
-                to_left = left * pltpu.roll(inv, low, 1)
-                to_right = right * pltpu.roll(inv, high, 1)
-                x_ref[2 * level, rows, :] = to_left
-                x_ref[2 * level + 1, rows, :] = to_right
+                up, down = right * inv, left * inv
+                x_ref[2 * level, rows, :] = up
+                x_ref[2 * level + 1, rows, :] = down
                 gs[b] = (
-                    ground
-                    + to_left * pltpu.roll(ground, low, 1)
-                    + to_right * pltpu.roll(ground, high, 1)
+                    ground + pltpu.roll(up * ground, low, 1) + pltpu.roll(down * ground, high, 1)
                 )
                 if level + 1 < ROUNDS:
-                    ls[b] = to_left * pltpu.roll(left, low, 1)
-                    rs[b] = to_right * pltpu.roll(right, high, 1)
+                    link = up * left
+                    ls[b] = pltpu.roll(link, low, 1)
+                    rs[b] = pltpu.roll(link, high, 1)
         for b in range(batch):
             x_ref[2 * ROUNDS, z_rows(z0 + b), :] = stores[b] / gs[b]
 
@@ -274,8 +272,8 @@
                 side = sides[b]
                 sides[b] = (
                     side
-                    + x_ref[2 * level, rows, :] * pltpu.roll(side, low, 1)
-                    + x_ref[2 * level + 1, rows, :] * pltpu.roll(side, high, 1)
+                    + pltpu.roll(x_ref[2 * level, rows, :] * side, low, 1)
+                    + pltpu.roll(x_ref[2 * level + 1, rows, :] * side, high, 1)
                 )
         for b in range(batch):
             rows = z_rows(z0 + b)

time: 116 us -> 116 us (level)
  no operation moved by 1% of the time
where the time goes in v8:
time: 116 us; the launch traced here: 115 us
  starting transfers between devices  45.1 us (39%)
  blocking collectives  44.9 us (39%)
  waiting for transfers between devices  15.3 us (13%)
  Pallas kernels  9.4 us (8%)
    all_to_all x1, starting transfers between devices, gather_z(): lax.all_to_all(pay, 'gz', 0, 0, tiled=True, axis_index_groups=same_core)  16 us
    all_to_all x1, blocking collectives, gather_z(): lax.all_to_all(pay, 'gz', 0, 0, tiled=True, axis_index_groups=same_core)  15.7 us
    all_gather x5, blocking collectives, share(): return lax.all_gather(numbers, 'gz', axis_index_groups=pairs)  15 us
    all_to_all x1, blocking collectives, gather_y(): return lax.all_to_all(pay, 'gy', 0, 0, tiled=True)  14.2 us
    all_to_all x1, waiting for transfers between devices, gather_z(): lax.all_to_all(pay, 'gz', 0, 0, tiled=True, axis_index_groups=same_core)  9.87 us
    all_to_all x1, starting transfers between devices, gather_y(): return lax.all_to_all(pay, 'gy', 0, 0, tiled=True)  7.92 us
    ppermute x1, starting transfers between devices, body(): lax.ppermute(zhi, 'gz', up['gz'])  4.39 us
    all_to_all x1, waiting for transfers between devices, gather_y(): return lax.all_to_all(pay, 'gy', 0, 0, tiled=True)  4.37 us
  transfers between devices with their start and end apart: 10, of which 3 were waited for; matrix products, arithmetic and copies ran while one was open for 0% of the time, Pallas kernels for 2%

profile of v8, /device:TPU:1, one launch (start us, length us, event | category | flops | bytes accessed | tf_op | source)
XLA Modules:
  0.0 115.5 jit_solution(3296849349091327784)
XLA Ops:
  0.6 1.0 edges_kernel.1
  1.6 3.9 %collective-permute-start.2 = (f32[3,16,128]{2,1,0:T(8,128)S(1)}, f32[3,16,128]{2,1,0:T(8,128)S(1)}, u32[]{:S(2)}, u32[]{:S(2)}) collective-permute-start(f32[3,16,128]{2,1,0:T(8,128)S(1)} %get-tuple-element.48), channel_id=1, source_target_pairs={{0,1},{1,2},{2,3},{3,4},{4,5},{5,6},{6,7},{7,8},{8,9},{9,10},{10,1... | collective-permute-start | bytes 73736 | tf_op jit(solution)/shard_map/ppermute | solution.py:850
  5.6 1.3 %collective-permute-start.3 = (f32[3,16,128]{2,1,0:T(8,128)S(1)}, f32[3,16,128]{2,1,0:T(8,128)S(1)}, u32[]{:S(2)}, u32[]{:S(2)}) collective-permute-start(f32[3,16,128]{2,1,0:T(8,128)S(1)} %get-tuple-element.49), channel_id=1, source_target_pairs={{1,0},{2,1},{3,2},{4,3},{5,4},{6,5},{7,6},{8,7},{9,8},{10,9},{11,1... | collective-permute-start | bytes 73736 | tf_op jit(solution)/shard_map/ppermute | solution.py:850
  6.9 4.4 %collective-permute-start = (f32[3,8,128]{2,1,0:T(8,128)S(1)}, f32[3,8,128]{2,1,0:T(8,128)S(1)}, u32[]{:S(2)}, u32[]{:S(2)}) collective-permute-start(f32[3,8,128]{2,1,0:T(8,128)S(1)} %get-tuple-element.46), channel_id=1, source_target_pairs={{0,16},{16,32},{32,48},{48,64},{64,80},{80,96},{96,112},{112,128},... | collective-permute-start | bytes 36872 | tf_op jit(solution)/shard_map/ppermute | solution.py:849
  11.3 3.0 %collective-permute-start.1 = (f32[3,8,128]{2,1,0:T(8,128)S(1)}, f32[3,8,128]{2,1,0:T(8,128)S(1)}, u32[]{:S(2)}, u32[]{:S(2)}) collective-permute-start(f32[3,8,128]{2,1,0:T(8,128)S(1)} %get-tuple-element.47), channel_id=1, source_target_pairs={{16,0},{32,16},{48,32},{64,48},{80,64},{96,80},{112,96},{128,112},... | collective-permute-start | bytes 36872 | tf_op jit(solution)/shard_map/ppermute | solution.py:849
  14.3 0.9 x_kernel.1.x_ref
  15.3 0.0 collective-permute-done.below_ref
  15.3 1.0 collective-permute-done.1.above_ref
  16.3 0.0 collective-permute-done.2.south_ref
  16.3 0.0 collective-permute-done.3.north_ref
  16.3 1.9 %front_kernel.1 = (f32[16,88,128]{2,1,0:T(8,128)}, f32[3,7,16,128]{3,2,1,0:T(8,128)S(1)}, f32[7,16,128]{2,1,0:T(8,128)S(1)}, f32[128,128]{1,0:T(8,128)S(1)}, f32...) custom-call(f32[128,128]{1,0:T(8,128)S(1)} %get-tuple-element.44.t_ref, f32[128,128]{1,0:T(8,128)S(1)} %get-tuple-element.43.c_ref, ...), custom_call_target="tpu_custom_call" | custom-call | tf_op jit(solution)/shard_map/front_kernel/pallas_call | solution.py:870
  18.1 7.9 %all-to-all-start = ((f32[16,88,128]{2,1,0:T(8,128)}), f32[16,88,128]{2,1,0:T(8,128)S(1)}, u32[]{:S(2)}, u32[]{:S(2)}) async-start(f32[16,88,128]{2,1,0:T(8,128)} %get-tuple-element.52), calls=%async_computation | async-start | bytes 1441792 | tf_op jit(solution)/shard_map/all_to_all | solution.py:853
  26.1 1.0 ahead_kernel.1
  27.1 1.8 %all-gather = f32[96,128]{1,0:T(8,128)S(1)} all-gather(f32[48,128]{1,0:T(8,128)S(1)} %get-tuple-element.51), channel_id=2, replica_groups={{0,16},{32,48},{64,80},{96,112},{128,144},{160,176},{192,208},{224,240}..., dimensions={0}, use_global_device_ids=true | all-gather | bytes 73728 | tf_op jit(solution)/shard_map/all_gather | solution.py:859
  28.9 1.3 %collective-permute-start.5 = (f32[8,128]{1,0:T(8,128)S(1)}, f32[8,128]{1,0:T(8,128)S(1)}, u32[]{:S(2)}, u32[]{:S(2)}) collective-permute-start(f32[8,128]{1,0:T(8,128)S(1)} %get-tuple-element.60.low_ref), channel_id=1, source_target_pairs={{32,0},{48,16},{64,32},{80,48},{96,64},{112,80},{128,96},{144,112}... | collective-permute-start | bytes 12296 | tf_op jit(solution)/shard_map/ppermute | solution.py:887
  30.2 4.2 %collective-permute-start.4 = (f32[8,128]{1,0:T(8,128)S(1)}, f32[8,128]{1,0:T(8,128)S(1)}, u32[]{:S(2)}, u32[]{:S(2)}) collective-permute-start(f32[8,128]{1,0:T(8,128)S(1)} %get-tuple-element.61.high_ref), channel_id=1, source_target_pairs={{0,32},{16,48},{32,64},{48,80},{64,96},{80,112},{96,128},{112,144}... | collective-permute-start | bytes 12296 | tf_op jit(solution)/shard_map/ppermute | solution.py:886
  34.4 4.4 %all-to-all-done.all_ref = f32[16,88,128]{2,1,0:T(8,128)S(1)} async-done(((f32[16,88,128]{2,1,0:T(8,128)}), f32[16,88,128]{2,1,0:T(8,128)S(1)}, u32[]{:S(2)}, u32[]{:S(2)}) %all-to-all-start) | async-done | bytes 720928 | tf_op jit(solution)/shard_map/all_to_all | solution.py:853
  38.8 0.2 middle_kernel.1
  39.0 1.8 %all-gather.1 = f32[64,128]{1,0:T(8,128)S(1)} all-gather(f32[32,128]{1,0:T(8,128)S(1)} %get-tuple-element.58), channel_id=3, replica_groups={{0,16},{32,48},{64,80},{96,112},{128,144},{160,176},{192,208},{224,240}..., dimensions={0}, use_global_device_ids=true | all-gather | bytes 49152 | tf_op jit(solution)/shard_map/all_gather | solution.py:859
  40.9 0.0 collective-permute-done.5.from_high_ref
  40.9 0.0 collective-permute-done.4.from_low_ref
  40.9 0.8 merge_kernel.1
  41.7 16.0 %all-to-all-start.1 = ((f32[16,24,128]{2,1,0:T(8,128)}), f32[16,24,128]{2,1,0:T(8,128)S(1)}, u32[]{:S(2)}, u32[]{:S(2)}) async-start(f32[16,24,128]{2,1,0:T(8,128)} %get-tuple-element.65), calls=%async_computation.1 | async-start | bytes 393216 | tf_op jit(solution)/shard_map/all_to_all | solution.py:856
  57.7 1.7 %collective-permute-start.6 = (f32[16,128]{1,0:T(8,128)S(1)}, f32[16,128]{1,0:T(8,128)S(1)}, u32[]{:S(2)}, u32[]{:S(2)}) collective-permute-start(f32[16,128]{1,0:T(8,128)S(1)} %get-tuple-element.74.high_ref), channel_id=1, source_target_pairs={{0,1},{1,2},{2,3},{3,4},{4,5},{5,6},{6,7},{7,8},{8,9},{9,10},{10,1... | collective-permute-start | bytes 24584 | tf_op jit(solution)/shard_map/ppermute | solution.py:905
  59.5 1.3 %collective-permute-start.7 = (f32[16,128]{1,0:T(8,128)S(1)}, f32[16,128]{1,0:T(8,128)S(1)}, u32[]{:S(2)}, u32[]{:S(2)}) collective-permute-start(f32[16,128]{1,0:T(8,128)S(1)} %get-tuple-element.75.low_ref), channel_id=1, source_target_pairs={{1,0},{2,1},{3,2},{4,3},{5,4},{6,5},{7,6},{8,7},{9,8},{10,9},{11,1... | collective-permute-start | bytes 24584 | tf_op jit(solution)/shard_map/ppermute | solution.py:906
  60.8 9.9 %all-to-all-done.1.all_ref = f32[16,24,128]{2,1,0:T(8,128)S(1)} async-done(((f32[16,24,128]{2,1,0:T(8,128)}), f32[16,24,128]{2,1,0:T(8,128)S(1)}, u32[]{:S(2)}, u32[]{:S(2)}) %all-to-all-start.1) | async-done | bytes 196640 | tf_op jit(solution)/shard_map/all_to_all | solution.py:856
  70.7 0.1 chain_kernel.1
  70.8 4.8 %all-gather.2 = f32[32,128]{1,0:T(8,128)S(1)} all-gather(f32[16,128]{1,0:T(8,128)S(1)} %chain_kernel.1), channel_id=4, replica_groups={{0,16},{32,48},{64,80},{96,112},{128,144},{160,176},{192,208},{224,240}..., dimensions={0}, use_global_device_ids=true | all-gather | bytes 24576 | tf_op jit(solution)/shard_map/all_gather | solution.py:859
  75.6 0.0 collective-permute-done.6.from_low_ref
  75.6 0.0 collective-permute-done.7.from_high_ref
  75.6 2.2 %turn_kernel.1 = (f32[16,48,128]{2,1,0:T(8,128)S(1)}, f32[7,16,128]{2,1,0:T(8,128)S(1)}, f32[128,128]{1,0:T(8,128)S(1)}, f32[128,128]{1,0:T(8,128)}, f32[2,16,128]{2,1,0:T(8,128)S(1)}) custom-call(f32[2,48,128]{2,1,0:T(8,128)S(1)} %bitcast.12, f32[2,32,128]{2,1,0:T(8,128)S(1)} %bitcast.16, f32[2,16,128]{2,1,0:T(8,128)S(1)} %bitcast.19, ...), custom_call_target="tpu_custom_call" | custom-call | tf_op jit(solution)/shard_map/turn_kernel/pallas_call | solution.py:911
  77.8 14.2 %all_to_all.20.all_ref = f32[16,48,128]{2,1,0:T(8,128)S(1)} all-to-all(f32[16,48,128]{2,1,0:T(8,128)S(1)} %get-tuple-element.76), channel_id=1, replica_groups=mesh['gz'=32,'gy'=16] {'gy'}, dimensions={0} | all-to-all | bytes 786432 | tf_op jit(solution)/shard_map/all_to_all | solution.py:853
  92.0 0.1 later_middle_kernel.1
  92.2 3.0 %all-gather.3 = f32[32,128]{1,0:T(8,128)S(1)} all-gather(f32[16,128]{1,0:T(8,128)S(1)} %get-tuple-element.81), channel_id=5, replica_groups={{0,16},{32,48},{64,80},{96,112},{128,144},{160,176},{192,208},{224,240}..., dimensions={0}, use_global_device_ids=true | all-gather | bytes 24576 | tf_op jit(solution)/shard_map/all_gather | solution.py:859
  95.1 0.3 later_merge_kernel.1
  95.4 15.7 %all_to_all.21.more_ref = f32[16,8,128]{2,1,0:T(8,128)S(1)} all-to-all(f32[16,8,128]{2,1,0:T(8,128)S(1)} %later_merge_kernel.1), channel_id=1, replica_groups={{0,32,64,96,128,160,192,224,256,288,320,352,384,416,448,480},{16,48,80,..., dimensions={0} | all-to-all | bytes 131072 | tf_op jit(solution)/shard_map/all_to_all | solution.py:856
  111.1 0.1 later_chain_kernel.1
  111.2 3.6 %all-gather.4 = f32[16,128]{1,0:T(8,128)S(1)} all-gather(f32[8,128]{1,0:T(8,128)S(1)} %later_chain_kernel.1), channel_id=6, replica_groups={{0,16},{32,48},{64,80},{96,112},{128,144},{160,176},{192,208},{224,240}..., dimensions={0}, use_global_device_ids=true | all-gather | bytes 12288 | tf_op jit(solution)/shard_map/all_gather | solution.py:859
  114.8 0.7 back_kernel.1
  (1 shorter events, 0.0 us)
Async XLA Ops:
  1.6 14.7 %collective-permute-start.2 = (f32[3,16,128]{2,1,0:T(8,128)S(1)}, f32[3,16,128]{2,1,0:T(8,128)S(1)}, u32[]{:S(2)}, u32[]{:S(2)}) collective-permute-start(f32[3,16,128]{2,1,0:T(8,128)S(1)} %get-tuple-element.48), channel_id=1, source_target_pairs={{0,1},{1,2},{2,3},{3,4},{4,5},{5,6},{6,7},{7,8},{8,9},{9,10},{10,1... | collective-permute-start | bytes 73736 | tf_op jit(solution)/shard_map/ppermute | solution.py:850
  5.6 10.7 %collective-permute-start.3 = (f32[3,16,128]{2,1,0:T(8,128)S(1)}, f32[3,16,128]{2,1,0:T(8,128)S(1)}, u32[]{:S(2)}, u32[]{:S(2)}) collective-permute-start(f32[3,16,128]{2,1,0:T(8,128)S(1)} %get-tuple-element.49), channel_id=1, source_target_pairs={{1,0},{2,1},{3,2},{4,3},{5,4},{6,5},{7,6},{8,7},{9,8},{10,9},{11,1... | collective-permute-start | bytes 73736 | tf_op jit(solution)/shard_map/ppermute | solution.py:850
  6.9 8.4 %collective-permute-start = (f32[3,8,128]{2,1,0:T(8,128)S(1)}, f32[3,8,128]{2,1,0:T(8,128)S(1)}, u32[]{:S(2)}, u32[]{:S(2)}) collective-permute-start(f32[3,8,128]{2,1,0:T(8,128)S(1)} %get-tuple-element.46), channel_id=1, source_target_pairs={{0,16},{16,32},{32,48},{48,64},{64,80},{80,96},{96,112},{112,128},... | collective-permute-start | bytes 36872 | tf_op jit(solution)/shard_map/ppermute | solution.py:849
  11.3 5.0 %collective-permute-start.1 = (f32[3,8,128]{2,1,0:T(8,128)S(1)}, f32[3,8,128]{2,1,0:T(8,128)S(1)}, u32[]{:S(2)}, u32[]{:S(2)}) collective-permute-start(f32[3,8,128]{2,1,0:T(8,128)S(1)} %get-tuple-element.47), channel_id=1, source_target_pairs={{16,0},{32,16},{48,32},{64,48},{80,64},{96,80},{112,96},{128,112},... | collective-permute-start | bytes 36872 | tf_op jit(solution)/shard_map/ppermute | solution.py:849
  18.1 20.6 %all-to-all-start = ((f32[16,88,128]{2,1,0:T(8,128)}), f32[16,88,128]{2,1,0:T(8,128)S(1)}, u32[]{:S(2)}, u32[]{:S(2)}) async-start(f32[16,88,128]{2,1,0:T(8,128)} %get-tuple-element.52), calls=%async_computation | async-start | bytes 1441792 | tf_op jit(solution)/shard_map/all_to_all | solution.py:853
  28.9 11.9 %collective-permute-start.5 = (f32[8,128]{1,0:T(8,128)S(1)}, f32[8,128]{1,0:T(8,128)S(1)}, u32[]{:S(2)}, u32[]{:S(2)}) collective-permute-start(f32[8,128]{1,0:T(8,128)S(1)} %get-tuple-element.60.low_ref), channel_id=1, source_target_pairs={{32,0},{48,16},{64,32},{80,48},{96,64},{112,80},{128,96},{144,112}... | collective-permute-start | bytes 12296 | tf_op jit(solution)/shard_map/ppermute | solution.py:887
  30.2 10.6 %collective-permute-start.4 = (f32[8,128]{1,0:T(8,128)S(1)}, f32[8,128]{1,0:T(8,128)S(1)}, u32[]{:S(2)}, u32[]{:S(2)}) collective-permute-start(f32[8,128]{1,0:T(8,128)S(1)} %get-tuple-element.61.high_ref), channel_id=1, source_target_pairs={{0,32},{16,48},{32,64},{48,80},{64,96},{80,112},{96,128},{112,144}... | collective-permute-start | bytes 12296 | tf_op jit(solution)/shard_map/ppermute | solution.py:886
  41.7 28.9 %all-to-all-start.1 = ((f32[16,24,128]{2,1,0:T(8,128)}), f32[16,24,128]{2,1,0:T(8,128)S(1)}, u32[]{:S(2)}, u32[]{:S(2)}) async-start(f32[16,24,128]{2,1,0:T(8,128)} %get-tuple-element.65), calls=%async_computation.1 | async-start | bytes 393216 | tf_op jit(solution)/shard_map/all_to_all | solution.py:856
  57.7 17.8 %collective-permute-start.6 = (f32[16,128]{1,0:T(8,128)S(1)}, f32[16,128]{1,0:T(8,128)S(1)}, u32[]{:S(2)}, u32[]{:S(2)}) collective-permute-start(f32[16,128]{1,0:T(8,128)S(1)} %get-tuple-element.74.high_ref), channel_id=1, source_target_pairs={{0,1},{1,2},{2,3},{3,4},{4,5},{5,6},{6,7},{7,8},{8,9},{9,10},{10,1... | collective-permute-start | bytes 24584 | tf_op jit(solution)/shard_map/ppermute | solution.py:905
  59.5 16.1 %collective-permute-start.7 = (f32[16,128]{1,0:T(8,128)S(1)}, f32[16,128]{1,0:T(8,128)S(1)}, u32[]{:S(2)}, u32[]{:S(2)}) collective-permute-start(f32[16,128]{1,0:T(8,128)S(1)} %get-tuple-element.75.low_ref), channel_id=1, source_target_pairs={{1,0},{2,1},{3,2},{4,3},{5,4},{6,5},{7,6},{8,7},{9,8},{10,9},{11,1... | collective-permute-start | bytes 24584 | tf_op jit(solution)/shard_map/ppermute | solution.py:906

commit v9 on v8

--- a/solution.py
+++ b/solution.py
@@ -68,8 +68,8 @@
 
 def spread(one_ref, out_ref, sem, count):
     copies = [pltpu.make_async_copy(one_ref, out_ref.at[d], sem.at[d]) for d in range(count)]
-    for copy in copies:
-        copy.start()
+    for d, copy in enumerate(copies):
+        copy.start(priority=d % 2)
     for copy in copies:
         copy.wait()
 

time: 116 us -> 116 us (level)
  no operation moved by 1% of the time
where the time goes in v9:
time: 116 us
  starting transfers between devices  45.1 us (39%)
  blocking collectives  45 us (39%)
  waiting for transfers between devices  15.3 us (13%)
  Pallas kernels  9.41 us (8%)
    all_to_all x1, starting transfers between devices, gather_z(): lax.all_to_all(pay, 'gz', 0, 0, tiled=True, axis_index_groups=same_core)  16 us
    all_to_all x1, blocking collectives, gather_z(): lax.all_to_all(pay, 'gz', 0, 0, tiled=True, axis_index_groups=same_core)  15.7 us
    all_gather x5, blocking collectives, share(): return lax.all_gather(numbers, 'gz', axis_index_groups=pairs)  15 us
    all_to_all x1, blocking collectives, gather_y(): return lax.all_to_all(pay, 'gy', 0, 0, tiled=True)  14.2 us
    all_to_all x1, waiting for transfers between devices, gather_z(): lax.all_to_all(pay, 'gz', 0, 0, tiled=True, axis_index_groups=same_core)  9.87 us
    all_to_all x1, starting transfers between devices, gather_y(): return lax.all_to_all(pay, 'gy', 0, 0, tiled=True)  7.92 us
    ppermute x1, starting transfers between devices, body(): lax.ppermute(zhi, 'gz', up['gz'])  4.39 us
    all_to_all x1, waiting for transfers between devices, gather_y(): return lax.all_to_all(pay, 'gy', 0, 0, tiled=True)  4.37 us
  transfers between devices with their start and end apart: 10, of which 3 were waited for; matrix products, arithmetic and copies ran while one was open for 0% of the time, Pallas kernels for 2%

profile of v9, /device:TPU:1, one launch (start us, length us, event | category | flops | bytes accessed | tf_op | source)
XLA Modules:
  0.0 115.5 jit_solution(3962068132576375803)
XLA Ops:
  0.6 1.0 edges_kernel.1
  1.6 3.9 %collective-permute-start.2 = (f32[3,16,128]{2,1,0:T(8,128)S(1)}, f32[3,16,128]{2,1,0:T(8,128)S(1)}, u32[]{:S(2)}, u32[]{:S(2)}) collective-permute-start(f32[3,16,128]{2,1,0:T(8,128)S(1)} %get-tuple-element.48), channel_id=1, source_target_pairs={{0,1},{1,2},{2,3},{3,4},{4,5},{5,6},{6,7},{7,8},{8,9},{9,10},{10,1... | collective-permute-start | bytes 73736 | tf_op jit(solution)/shard_map/ppermute | solution.py:850
  5.6 1.3 %collective-permute-start.3 = (f32[3,16,128]{2,1,0:T(8,128)S(1)}, f32[3,16,128]{2,1,0:T(8,128)S(1)}, u32[]{:S(2)}, u32[]{:S(2)}) collective-permute-start(f32[3,16,128]{2,1,0:T(8,128)S(1)} %get-tuple-element.49), channel_id=1, source_target_pairs={{1,0},{2,1},{3,2},{4,3},{5,4},{6,5},{7,6},{8,7},{9,8},{10,9},{11,1... | collective-permute-start | bytes 73736 | tf_op jit(solution)/shard_map/ppermute | solution.py:850
  6.9 4.4 %collective-permute-start = (f32[3,8,128]{2,1,0:T(8,128)S(1)}, f32[3,8,128]{2,1,0:T(8,128)S(1)}, u32[]{:S(2)}, u32[]{:S(2)}) collective-permute-start(f32[3,8,128]{2,1,0:T(8,128)S(1)} %get-tuple-element.46), channel_id=1, source_target_pairs={{0,16},{16,32},{32,48},{48,64},{64,80},{80,96},{96,112},{112,128},... | collective-permute-start | bytes 36872 | tf_op jit(solution)/shard_map/ppermute | solution.py:849
  11.3 3.0 %collective-permute-start.1 = (f32[3,8,128]{2,1,0:T(8,128)S(1)}, f32[3,8,128]{2,1,0:T(8,128)S(1)}, u32[]{:S(2)}, u32[]{:S(2)}) collective-permute-start(f32[3,8,128]{2,1,0:T(8,128)S(1)} %get-tuple-element.47), channel_id=1, source_target_pairs={{16,0},{32,16},{48,32},{64,48},{80,64},{96,80},{112,96},{128,112},... | collective-permute-start | bytes 36872 | tf_op jit(solution)/shard_map/ppermute | solution.py:849
  14.3 0.9 x_kernel.1.x_ref
  15.3 0.0 collective-permute-done.below_ref
  15.3 1.0 collective-permute-done.1.above_ref
  16.3 0.0 collective-permute-done.2.south_ref
  16.3 0.0 collective-permute-done.3.north_ref
  16.3 1.9 %front_kernel.1 = (f32[16,88,128]{2,1,0:T(8,128)}, f32[3,7,16,128]{3,2,1,0:T(8,128)S(1)}, f32[7,16,128]{2,1,0:T(8,128)S(1)}, f32[128,128]{1,0:T(8,128)S(1)}, f32...) custom-call(f32[128,128]{1,0:T(8,128)S(1)} %get-tuple-element.44.t_ref, f32[128,128]{1,0:T(8,128)S(1)} %get-tuple-element.43.c_ref, ...), custom_call_target="tpu_custom_call" | custom-call | tf_op jit(solution)/shard_map/front_kernel/pallas_call | solution.py:870
  18.2 7.9 %all-to-all-start = ((f32[16,88,128]{2,1,0:T(8,128)}), f32[16,88,128]{2,1,0:T(8,128)S(1)}, u32[]{:S(2)}, u32[]{:S(2)}) async-start(f32[16,88,128]{2,1,0:T(8,128)} %get-tuple-element.52), calls=%async_computation | async-start | bytes 1441792 | tf_op jit(solution)/shard_map/all_to_all | solution.py:853
  26.1 1.0 ahead_kernel.1
  27.1 1.8 %all-gather = f32[96,128]{1,0:T(8,128)S(1)} all-gather(f32[48,128]{1,0:T(8,128)S(1)} %get-tuple-element.51), channel_id=2, replica_groups={{0,16},{32,48},{64,80},{96,112},{128,144},{160,176},{192,208},{224,240}..., dimensions={0}, use_global_device_ids=true | all-gather | bytes 73728 | tf_op jit(solution)/shard_map/all_gather | solution.py:859
  28.9 1.3 %collective-permute-start.5 = (f32[8,128]{1,0:T(8,128)S(1)}, f32[8,128]{1,0:T(8,128)S(1)}, u32[]{:S(2)}, u32[]{:S(2)}) collective-permute-start(f32[8,128]{1,0:T(8,128)S(1)} %get-tuple-element.60.low_ref), channel_id=1, source_target_pairs={{32,0},{48,16},{64,32},{80,48},{96,64},{112,80},{128,96},{144,112}... | collective-permute-start | bytes 12296 | tf_op jit(solution)/shard_map/ppermute | solution.py:887
  30.2 4.2 %collective-permute-start.4 = (f32[8,128]{1,0:T(8,128)S(1)}, f32[8,128]{1,0:T(8,128)S(1)}, u32[]{:S(2)}, u32[]{:S(2)}) collective-permute-start(f32[8,128]{1,0:T(8,128)S(1)} %get-tuple-element.61.high_ref), channel_id=1, source_target_pairs={{0,32},{16,48},{32,64},{48,80},{64,96},{80,112},{96,128},{112,144}... | collective-permute-start | bytes 12296 | tf_op jit(solution)/shard_map/ppermute | solution.py:886
  34.4 4.4 %all-to-all-done.all_ref = f32[16,88,128]{2,1,0:T(8,128)S(1)} async-done(((f32[16,88,128]{2,1,0:T(8,128)}), f32[16,88,128]{2,1,0:T(8,128)S(1)}, u32[]{:S(2)}, u32[]{:S(2)}) %all-to-all-start) | async-done | bytes 720928 | tf_op jit(solution)/shard_map/all_to_all | solution.py:853
  38.8 0.2 middle_kernel.1
  39.0 1.8 %all-gather.1 = f32[64,128]{1,0:T(8,128)S(1)} all-gather(f32[32,128]{1,0:T(8,128)S(1)} %get-tuple-element.58), channel_id=3, replica_groups={{0,16},{32,48},{64,80},{96,112},{128,144},{160,176},{192,208},{224,240}..., dimensions={0}, use_global_device_ids=true | all-gather | bytes 49152 | tf_op jit(solution)/shard_map/all_gather | solution.py:859
  40.9 0.0 collective-permute-done.5.from_high_ref
  40.9 0.0 collective-permute-done.4.from_low_ref
  40.9 0.8 merge_kernel.1
  41.7 16.0 %all-to-all-start.1 = ((f32[16,24,128]{2,1,0:T(8,128)}), f32[16,24,128]{2,1,0:T(8,128)S(1)}, u32[]{:S(2)}, u32[]{:S(2)}) async-start(f32[16,24,128]{2,1,0:T(8,128)} %get-tuple-element.65), calls=%async_computation.1 | async-start | bytes 393216 | tf_op jit(solution)/shard_map/all_to_all | solution.py:856
  57.8 1.7 %collective-permute-start.6 = (f32[16,128]{1,0:T(8,128)S(1)}, f32[16,128]{1,0:T(8,128)S(1)}, u32[]{:S(2)}, u32[]{:S(2)}) collective-permute-start(f32[16,128]{1,0:T(8,128)S(1)} %get-tuple-element.74.high_ref), channel_id=1, source_target_pairs={{0,1},{1,2},{2,3},{3,4},{4,5},{5,6},{6,7},{7,8},{8,9},{9,10},{10,1... | collective-permute-start | bytes 24584 | tf_op jit(solution)/shard_map/ppermute | solution.py:905
  59.5 1.3 %collective-permute-start.7 = (f32[16,128]{1,0:T(8,128)S(1)}, f32[16,128]{1,0:T(8,128)S(1)}, u32[]{:S(2)}, u32[]{:S(2)}) collective-permute-start(f32[16,128]{1,0:T(8,128)S(1)} %get-tuple-element.75.low_ref), channel_id=1, source_target_pairs={{1,0},{2,1},{3,2},{4,3},{5,4},{6,5},{7,6},{8,7},{9,8},{10,9},{11,1... | collective-permute-start | bytes 24584 | tf_op jit(solution)/shard_map/ppermute | solution.py:906
  60.8 9.9 %all-to-all-done.1.all_ref = f32[16,24,128]{2,1,0:T(8,128)S(1)} async-done(((f32[16,24,128]{2,1,0:T(8,128)}), f32[16,24,128]{2,1,0:T(8,128)S(1)}, u32[]{:S(2)}, u32[]{:S(2)}) %all-to-all-start.1) | async-done | bytes 196640 | tf_op jit(solution)/shard_map/all_to_all | solution.py:856
  70.7 0.1 chain_kernel.1
  70.8 4.8 %all-gather.2 = f32[32,128]{1,0:T(8,128)S(1)} all-gather(f32[16,128]{1,0:T(8,128)S(1)} %chain_kernel.1), channel_id=4, replica_groups={{0,16},{32,48},{64,80},{96,112},{128,144},{160,176},{192,208},{224,240}..., dimensions={0}, use_global_device_ids=true | all-gather | bytes 24576 | tf_op jit(solution)/shard_map/all_gather | solution.py:859
  75.6 0.0 collective-permute-done.6.from_low_ref
  75.6 0.0 collective-permute-done.7.from_high_ref
  75.6 2.2 %turn_kernel.1 = (f32[16,48,128]{2,1,0:T(8,128)S(1)}, f32[7,16,128]{2,1,0:T(8,128)S(1)}, f32[128,128]{1,0:T(8,128)S(1)}, f32[128,128]{1,0:T(8,128)}, f32[2,16,128]{2,1,0:T(8,128)S(1)}) custom-call(f32[2,48,128]{2,1,0:T(8,128)S(1)} %bitcast.12, f32[2,32,128]{2,1,0:T(8,128)S(1)} %bitcast.16, f32[2,16,128]{2,1,0:T(8,128)S(1)} %bitcast.19, ...), custom_call_target="tpu_custom_call" | custom-call | tf_op jit(solution)/shard_map/turn_kernel/pallas_call | solution.py:911
  77.8 14.2 %all_to_all.20.all_ref = f32[16,48,128]{2,1,0:T(8,128)S(1)} all-to-all(f32[16,48,128]{2,1,0:T(8,128)S(1)} %get-tuple-element.76), channel_id=1, replica_groups=mesh['gz'=32,'gy'=16] {'gy'}, dimensions={0} | all-to-all | bytes 786432 | tf_op jit(solution)/shard_map/all_to_all | solution.py:853
  92.0 0.1 later_middle_kernel.1
  92.2 3.0 %all-gather.3 = f32[32,128]{1,0:T(8,128)S(1)} all-gather(f32[16,128]{1,0:T(8,128)S(1)} %get-tuple-element.81), channel_id=5, replica_groups={{0,16},{32,48},{64,80},{96,112},{128,144},{160,176},{192,208},{224,240}..., dimensions={0}, use_global_device_ids=true | all-gather | bytes 24576 | tf_op jit(solution)/shard_map/all_gather | solution.py:859
  95.1 0.3 later_merge_kernel.1
  95.4 15.7 %all_to_all.21.more_ref = f32[16,8,128]{2,1,0:T(8,128)S(1)} all-to-all(f32[16,8,128]{2,1,0:T(8,128)S(1)} %later_merge_kernel.1), channel_id=1, replica_groups={{0,32,64,96,128,160,192,224,256,288,320,352,384,416,448,480},{16,48,80,..., dimensions={0} | all-to-all | bytes 131072 | tf_op jit(solution)/shard_map/all_to_all | solution.py:856
  111.1 0.1 later_chain_kernel.1
  111.2 3.6 %all-gather.4 = f32[16,128]{1,0:T(8,128)S(1)} all-gather(f32[8,128]{1,0:T(8,128)S(1)} %later_chain_kernel.1), channel_id=6, replica_groups={{0,16},{32,48},{64,80},{96,112},{128,144},{160,176},{192,208},{224,240}..., dimensions={0}, use_global_device_ids=true | all-gather | bytes 12288 | tf_op jit(solution)/shard_map/all_gather | solution.py:859
  114.8 0.7 back_kernel.1
  (1 shorter events, 0.0 us)
Async XLA Ops:
  1.6 14.7 %collective-permute-start.2 = (f32[3,16,128]{2,1,0:T(8,128)S(1)}, f32[3,16,128]{2,1,0:T(8,128)S(1)}, u32[]{:S(2)}, u32[]{:S(2)}) collective-permute-start(f32[3,16,128]{2,1,0:T(8,128)S(1)} %get-tuple-element.48), channel_id=1, source_target_pairs={{0,1},{1,2},{2,3},{3,4},{4,5},{5,6},{6,7},{7,8},{8,9},{9,10},{10,1... | collective-permute-start | bytes 73736 | tf_op jit(solution)/shard_map/ppermute | solution.py:850
  5.6 10.7 %collective-permute-start.3 = (f32[3,16,128]{2,1,0:T(8,128)S(1)}, f32[3,16,128]{2,1,0:T(8,128)S(1)}, u32[]{:S(2)}, u32[]{:S(2)}) collective-permute-start(f32[3,16,128]{2,1,0:T(8,128)S(1)} %get-tuple-element.49), channel_id=1, source_target_pairs={{1,0},{2,1},{3,2},{4,3},{5,4},{6,5},{7,6},{8,7},{9,8},{10,9},{11,1... | collective-permute-start | bytes 73736 | tf_op jit(solution)/shard_map/ppermute | solution.py:850
  6.9 8.4 %collective-permute-start = (f32[3,8,128]{2,1,0:T(8,128)S(1)}, f32[3,8,128]{2,1,0:T(8,128)S(1)}, u32[]{:S(2)}, u32[]{:S(2)}) collective-permute-start(f32[3,8,128]{2,1,0:T(8,128)S(1)} %get-tuple-element.46), channel_id=1, source_target_pairs={{0,16},{16,32},{32,48},{48,64},{64,80},{80,96},{96,112},{112,128},... | collective-permute-start | bytes 36872 | tf_op jit(solution)/shard_map/ppermute | solution.py:849
  11.3 5.0 %collective-permute-start.1 = (f32[3,8,128]{2,1,0:T(8,128)S(1)}, f32[3,8,128]{2,1,0:T(8,128)S(1)}, u32[]{:S(2)}, u32[]{:S(2)}) collective-permute-start(f32[3,8,128]{2,1,0:T(8,128)S(1)} %get-tuple-element.47), channel_id=1, source_target_pairs={{16,0},{32,16},{48,32},{64,48},{80,64},{96,80},{112,96},{128,112},... | collective-permute-start | bytes 36872 | tf_op jit(solution)/shard_map/ppermute | solution.py:849
  18.2 20.6 %all-to-all-start = ((f32[16,88,128]{2,1,0:T(8,128)}), f32[16,88,128]{2,1,0:T(8,128)S(1)}, u32[]{:S(2)}, u32[]{:S(2)}) async-start(f32[16,88,128]{2,1,0:T(8,128)} %get-tuple-element.52), calls=%async_computation | async-start | bytes 1441792 | tf_op jit(solution)/shard_map/all_to_all | solution.py:853
  28.9 11.9 %collective-permute-start.5 = (f32[8,128]{1,0:T(8,128)S(1)}, f32[8,128]{1,0:T(8,128)S(1)}, u32[]{:S(2)}, u32[]{:S(2)}) collective-permute-start(f32[8,128]{1,0:T(8,128)S(1)} %get-tuple-element.60.low_ref), channel_id=1, source_target_pairs={{32,0},{48,16},{64,32},{80,48},{96,64},{112,80},{128,96},{144,112}... | collective-permute-start | bytes 12296 | tf_op jit(solution)/shard_map/ppermute | solution.py:887
  30.2 10.6 %collective-permute-start.4 = (f32[8,128]{1,0:T(8,128)S(1)}, f32[8,128]{1,0:T(8,128)S(1)}, u32[]{:S(2)}, u32[]{:S(2)}) collective-permute-start(f32[8,128]{1,0:T(8,128)S(1)} %get-tuple-element.61.high_ref), channel_id=1, source_target_pairs={{0,32},{16,48},{32,64},{48,80},{64,96},{80,112},{96,128},{112,144}... | collective-permute-start | bytes 12296 | tf_op jit(solution)/shard_map/ppermute | solution.py:886
  41.7 28.9 %all-to-all-start.1 = ((f32[16,24,128]{2,1,0:T(8,128)}), f32[16,24,128]{2,1,0:T(8,128)S(1)}, u32[]{:S(2)}, u32[]{:S(2)}) async-start(f32[16,24,128]{2,1,0:T(8,128)} %get-tuple-element.65), calls=%async_computation.1 | async-start | bytes 393216 | tf_op jit(solution)/shard_map/all_to_all | solution.py:856
  57.8 17.8 %collective-permute-start.6 = (f32[16,128]{1,0:T(8,128)S(1)}, f32[16,128]{1,0:T(8,128)S(1)}, u32[]{:S(2)}, u32[]{:S(2)}) collective-permute-start(f32[16,128]{1,0:T(8,128)S(1)} %get-tuple-element.74.high_ref), channel_id=1, source_target_pairs={{0,1},{1,2},{2,3},{3,4},{4,5},{5,6},{6,7},{7,8},{8,9},{9,10},{10,1... | collective-permute-start | bytes 24584 | tf_op jit(solution)/shard_map/ppermute | solution.py:905
  59.5 16.1 %collective-permute-start.7 = (f32[16,128]{1,0:T(8,128)S(1)}, f32[16,128]{1,0:T(8,128)S(1)}, u32[]{:S(2)}, u32[]{:S(2)}) collective-permute-start(f32[16,128]{1,0:T(8,128)S(1)} %get-tuple-element.75.low_ref), channel_id=1, source_target_pairs={{1,0},{2,1},{3,2},{4,3},{5,4},{6,5},{7,6},{8,7},{9,8},{10,9},{11,1... | collective-permute-start | bytes 24584 | tf_op jit(solution)/shard_map/ppermute | solution.py:906
